TPU v7x, 32 devices: a whole 2x2x4 slice. The times are simulated.
32 devices in a mesh: dp: 8 (over z, y), sp: 4 (over x, core).
Axes of the slice: x: 2, y: 2, z: 4, core: 2. Of those that a mesh axis runs over, the one named last changes fastest.
Arguments:
- tokens: bfloat16 [4, 4096, 768], P(None, ('dp', 'sp')), may hold values from -6 to 6
- cotangent: bfloat16 [4, 4096, 768], P(None, ('dp', 'sp')), may hold values from -6 to 6
- seq_cut: int32 [4, 8], P(None, 'dp'), may hold values from 128 to 512, as said below
- ln1_gain: bfloat16 [768], P(('dp', 'sp')), may hold values from 0.5 to 1.5
- ln1_bias: bfloat16 [768], P(('dp', 'sp')), may hold values from -3 to 3
- w_qkv: bfloat16 [768, 2304], P(('dp', 'sp')), may hold values from -0.21875 to 0.21875
- b_query: bfloat16 [768], P(('dp', 'sp')), may hold values from -4 to 4
- b_value: bfloat16 [768], P(('dp', 'sp')), may hold values from -0.75 to 0.75
- w_out: bfloat16 [768, 768], P(('dp', 'sp')), may hold values from -6 to 6
- b_out: bfloat16 [768], P(('dp', 'sp')), may hold values from -6 to 6
- ln2_gain: bfloat16 [768], P(('dp', 'sp')), may hold values from 0.5 to 1.5
- ln2_bias: bfloat16 [768], P(('dp', 'sp')), may hold values from -3 to 3
- w_fc: bfloat16 [768, 3072], P(('dp', 'sp')), may hold values from -0.21875 to 0.21875
- b_fc: bfloat16 [3072], P(('dp', 'sp')), may hold values from -4 to 4
- w_proj: bfloat16 [3072, 768], P(('dp', 'sp')), may hold values from -0.75 to 0.75
- b_proj: bfloat16 [768], P(('dp', 'sp')), may hold values from -6 to 6
Outputs:
- layer_out: bfloat16 [4, 4096, 768], P(None, ('dp', 'sp'))
- input_grad: float32 [4, 4096, 768], P(None, ('dp', 'sp'))
- grad_ln1_gain: float32 [768], P(('dp', 'sp'))
- grad_ln1_bias: float32 [768], P(('dp', 'sp'))
- grad_w_qkv: float32 [768, 2304], P(('dp', 'sp'))
- grad_b_query: float32 [768], P(('dp', 'sp'))
- grad_b_value: float32 [768], P(('dp', 'sp'))
- grad_w_out: float32 [768, 768], P(('dp', 'sp'))
- grad_b_out: float32 [768], P(('dp', 'sp'))
- grad_ln2_gain: float32 [768], P(('dp', 'sp'))
- grad_ln2_bias: float32 [768], P(('dp', 'sp'))
- grad_w_fc: float32 [768, 3072], P(('dp', 'sp'))
- grad_b_fc: float32 [3072], P(('dp', 'sp'))
- grad_w_proj: float32 [3072, 768], P(('dp', 'sp'))
- grad_b_proj: float32 [768], P(('dp', 'sp'))
Inputs may be any that keep to these rules, and one draw needn't show every extreme that they name: seq_cut[m, g] is where the second sequence of pack g in micro-batch m begins; the value 512 means that the pack holds one sequence.
All inputs are finite; a program needn't handle non-finite values.
Results may differ from a plain program's by a relative error of at most 0.014.
Values may be sent and summed in bfloat16 or wider, within the bound.
A program may use at most 256 MiB of HBM per device.

v0:
```python
import jax
import jax.numpy as jnp
from jax import lax
from jax.sharding import PartitionSpec as P

HEADS = 12
HEAD = 64


EPSILON = 1e-05
BRANCH = 24.0 ** (-0.5)
NEGATIVE = -1e30


def norm_rows(rows, gain, offset):
    center = jnp.mean(rows, axis=-1, keepdims=True)
    centred = rows - center
    spread = jnp.mean(centred * centred, axis=-1, keepdims=True)
    return centred * lax.rsqrt(spread + EPSILON) * gain + offset


def gelu_tanh(values):
    return jax.nn.gelu(values, approximate=True)


def allowed_mask(query_pos, key_pos, split_at):
    causal = key_pos[None, :] <= query_pos[:, None]
    same_doc = (key_pos[None, :] >= split_at) == (query_pos[:, None] >= split_at)
    return causal & same_doc


def block_scores(query_block, key_heads, positions, first_row, last_key, split_at):
    scores = jnp.einsum(
        "hdq,hdk->hqk", query_block, key_heads[:, :, :last_key], preferred_element_type=jnp.float32
    ) * HEAD ** (-0.5)
    allowed = allowed_mask(positions[first_row:last_key], positions[:last_key], split_at)
    return jnp.where(allowed[None], scores, NEGATIVE)


def attend(query_heads, key_heads, value_heads, split_at, head_count):
    length = query_heads.shape[1]
    block_rows = min(512, length // 2)
    queries = query_heads.reshape(head_count, HEAD, length)
    keys_all = key_heads.reshape(head_count, HEAD, length)
    values_all = value_heads.reshape(head_count, HEAD, length)
    positions = lax.iota(jnp.int32, length)
    out_blocks = []
    lse_blocks = []
    for block_index in range(length // block_rows):
        first_row = block_index * block_rows
        last_key = first_row + block_rows
        scores = block_scores(
            queries[:, :, first_row:last_key], keys_all, positions, first_row, last_key, split_at
        )
        row_max = jnp.max(scores, axis=-1, keepdims=True)
        exponent = jnp.exp(scores - row_max)
        totals = jnp.sum(exponent, axis=-1, keepdims=True)
        prob_low = (exponent / totals).astype(jnp.bfloat16)
        out_blocks.append(
            jnp.einsum(
                "hqk,hdk->hdq",
                prob_low,
                values_all[:, :, :last_key],
                preferred_element_type=jnp.float32,
            )
        )
        lse_blocks.append((row_max + jnp.log(totals))[:, :, 0])
    attn_wide = jnp.concatenate(out_blocks, axis=2).reshape(head_count * HEAD, length)
    return (attn_wide, jnp.concatenate(lse_blocks, axis=1))


def attend_back(
    query_heads, key_heads, value_heads, attn_wide, log_sums, grad_attn, split_at, head_count
):
    length = query_heads.shape[1]
    block_rows = min(512, length // 2)
    scale = HEAD ** (-0.5)
    queries = query_heads.reshape(head_count, HEAD, length)
    keys_all = key_heads.reshape(head_count, HEAD, length)
    values_all = value_heads.reshape(head_count, HEAD, length)
    grad_heads = grad_attn.reshape(head_count, HEAD, length)
    row_delta = jnp.sum(grad_heads * attn_wide.reshape(head_count, HEAD, length), axis=1)
    positions = lax.iota(jnp.int32, length)
    grad_keys = jnp.zeros((head_count, HEAD, length), jnp.float32)
    grad_values = jnp.zeros((head_count, HEAD, length), jnp.float32)
    query_grads = []
    for block_index in range(length // block_rows):
        first_row = block_index * block_rows
        last_key = first_row + block_rows
        query_block = queries[:, :, first_row:last_key]
        scores = block_scores(query_block, keys_all, positions, first_row, last_key, split_at)
        prob_wide = jnp.exp(scores - log_sums[:, first_row:last_key, None])
        grad_block = grad_heads[:, :, first_row:last_key]
        grad_prob = jnp.einsum(
            "hdq,hdk->hqk",
            grad_block,
            values_all[:, :, :last_key],
            preferred_element_type=jnp.float32,
        )
        grad_scores = (prob_wide * (grad_prob - row_delta[:, first_row:last_key, None])).astype(
            jnp.bfloat16
        )
        query_grads.append(
            jnp.einsum(
                "hqk,hdk->hdq",
                grad_scores,
                keys_all[:, :, :last_key],
                preferred_element_type=jnp.float32,
            )
            * scale
        )
        grad_keys = grad_keys.at[:, :, :last_key].add(
            jnp.einsum("hqk,hdq->hdk", grad_scores, query_block, preferred_element_type=jnp.float32)
            * scale
        )
        grad_values = grad_values.at[:, :, :last_key].add(
            jnp.einsum(
                "hqk,hdq->hdk",
                prob_wide.astype(jnp.bfloat16),
                grad_block,
                preferred_element_type=jnp.float32,
            )
        )
    grad_queries = jnp.concatenate(query_grads, axis=2)
    width = head_count * HEAD
    return (
        grad_queries.reshape(width, length).astype(jnp.bfloat16),
        grad_keys.reshape(width, length).astype(jnp.bfloat16),
        grad_values.reshape(width, length).astype(jnp.bfloat16),
    )


def forward_pass(inputs, weights, split_at, head_count):
    (
        gain_one,
        bias_one,
        w_joint,
        bias_query,
        bias_value,
        w_mix,
        bias_mix,
        gain_two,
        bias_two,
        w_up,
        bias_up,
        w_down,
        bias_down,
    ) = weights
    width = inputs.shape[1]
    normed_one = norm_rows(inputs, gain_one.astype(jnp.float32), bias_one.astype(jnp.float32))
    normed_low = normed_one.astype(jnp.bfloat16)
    joint = jnp.einsum("dc,td->ct", w_joint, normed_low, preferred_element_type=jnp.float32)
    joint_bias = jnp.concatenate([bias_query, jnp.zeros_like(bias_query), bias_value]).astype(
        jnp.float32
    )
    joint_low = (joint + joint_bias[:, None]).astype(jnp.bfloat16)
    query_heads, key_heads, value_heads = (
        lax.all_to_all(joint_low[:width], "sp", split_axis=0, concat_axis=1, tiled=True),
        lax.all_to_all(joint_low[width : 2 * width], "sp", split_axis=0, concat_axis=1, tiled=True),
        lax.all_to_all(joint_low[2 * width :], "sp", split_axis=0, concat_axis=1, tiled=True),
    )
    attn_wide, log_sums = attend(query_heads, key_heads, value_heads, split_at, head_count)
    attn_seq = lax.all_to_all(
        attn_wide.astype(jnp.bfloat16), "sp", split_axis=1, concat_axis=0, tiled=True
    )
    mixed = jnp.einsum(
        "it,ij->tj", attn_seq, w_mix, preferred_element_type=jnp.float32
    ) + bias_mix.astype(jnp.float32)
    hidden_one = inputs + BRANCH * mixed
    normed_two = norm_rows(hidden_one, gain_two.astype(jnp.float32), bias_two.astype(jnp.float32))
    normed_two_low = normed_two.astype(jnp.bfloat16)
    pre_act = jnp.dot(normed_two_low, w_up, preferred_element_type=jnp.float32) + bias_up.astype(
        jnp.float32
    )
    act_low = gelu_tanh(pre_act).astype(jnp.bfloat16)
    layer_value = hidden_one + BRANCH * (
        jnp.dot(act_low, w_down, preferred_element_type=jnp.float32) + bias_down.astype(jnp.float32)
    )
    saved = (
        normed_low,
        query_heads,
        key_heads,
        value_heads,
        attn_wide,
        log_sums,
        attn_seq,
        hidden_one,
        normed_two_low,
        pre_act,
        act_low,
    )
    return (layer_value.astype(jnp.bfloat16), saved)


def backward_pass(inputs, cotangent_rows, weights, saved, split_at, head_count):
    (
        gain_one,
        bias_one,
        w_joint,
        bias_query,
        bias_value,
        w_mix,
        bias_mix,
        gain_two,
        bias_two,
        w_up,
        bias_up,
        w_down,
        bias_down,
    ) = weights
    (
        normed_low,
        query_heads,
        key_heads,
        value_heads,
        attn_wide,
        log_sums,
        attn_seq,
        hidden_one,
        normed_two_low,
        pre_act,
        act_low,
    ) = saved
    grad_output = cotangent_rows.astype(jnp.float32)
    grad_mlp = (BRANCH * grad_output).astype(jnp.bfloat16)
    grad_w_down = jnp.einsum("tf,tj->fj", act_low, grad_mlp, preferred_element_type=jnp.float32)
    grad_bias_down = jnp.sum(grad_mlp.astype(jnp.float32), axis=0)
    grad_act = jnp.einsum("tj,fj->tf", grad_mlp, w_down, preferred_element_type=jnp.float32)
    unused_act, gelu_pull = jax.vjp(gelu_tanh, pre_act)
    grad_pre = gelu_pull(grad_act)[0].astype(jnp.bfloat16)
    grad_w_up = jnp.einsum(
        "td,tf->df", normed_two_low, grad_pre, preferred_element_type=jnp.float32
    )
    grad_bias_up = jnp.sum(grad_pre.astype(jnp.float32), axis=0)
    grad_normed_two = jnp.einsum("tf,df->td", grad_pre, w_up, preferred_element_type=jnp.float32)
    unused_two, second_pull = jax.vjp(
        norm_rows, hidden_one, gain_two.astype(jnp.float32), bias_two.astype(jnp.float32)
    )
    grad_hidden_ln, grad_gain_two, grad_bias_two = second_pull(grad_normed_two)
    grad_hidden = grad_output + grad_hidden_ln
    grad_branch = (BRANCH * grad_hidden).astype(jnp.bfloat16)
    grad_w_mix = jnp.einsum("it,tj->ij", attn_seq, grad_branch, preferred_element_type=jnp.float32)
    grad_bias_mix = jnp.sum(grad_branch.astype(jnp.float32), axis=0)
    grad_attn_seq = jnp.einsum(
        "ij,tj->it", w_mix, grad_branch, preferred_element_type=jnp.float32
    ).astype(jnp.bfloat16)
    grad_attn = lax.all_to_all(grad_attn_seq, "sp", split_axis=0, concat_axis=1, tiled=True)
    grad_query_h, grad_key_h, grad_value_h = attend_back(
        query_heads, key_heads, value_heads, attn_wide, log_sums, grad_attn, split_at, head_count
    )
    seq_query, seq_key, seq_value = (
        lax.all_to_all(grad_query_h, "sp", split_axis=1, concat_axis=0, tiled=True),
        lax.all_to_all(grad_key_h, "sp", split_axis=1, concat_axis=0, tiled=True),
        lax.all_to_all(grad_value_h, "sp", split_axis=1, concat_axis=0, tiled=True),
    )
    grad_joint = jnp.concatenate([seq_query, seq_key, seq_value], axis=0)
    grad_w_joint = jnp.einsum(
        "td,ct->dc", normed_low, grad_joint, preferred_element_type=jnp.float32
    )
    grad_bias_query = jnp.sum(seq_query.astype(jnp.float32), axis=1)
    grad_bias_value = jnp.sum(seq_value.astype(jnp.float32), axis=1)
    grad_normed_one = jnp.einsum(
        "ct,dc->td", grad_joint, w_joint, preferred_element_type=jnp.float32
    )
    unused_one, first_pull = jax.vjp(
        norm_rows, inputs, gain_one.astype(jnp.float32), bias_one.astype(jnp.float32)
    )
    grad_inputs_ln, grad_gain_one, grad_bias_one = first_pull(grad_normed_one)
    grads = (
        grad_gain_one,
        grad_bias_one,
        grad_w_joint,
        grad_bias_query,
        grad_bias_value,
        grad_w_mix,
        grad_bias_mix,
        grad_gain_two,
        grad_bias_two,
        grad_w_up,
        grad_bias_up,
        grad_w_down,
        grad_bias_down,
    )
    return (grad_hidden + grad_inputs_ln, grads)


def local(
    tokens,
    cotangent,
    seq_cut,
    ln1_gain,
    ln1_bias,
    w_qkv,
    b_query,
    b_value,
    w_out,
    b_out,
    ln2_gain,
    ln2_bias,
    w_fc,
    b_fc,
    w_proj,
    b_proj,
):
    head_count = HEADS // lax.axis_size("sp")
    device_count = lax.axis_size(("dp", "sp"))
    sharded_all = (
        ln1_gain,
        ln1_bias,
        w_qkv,
        b_query,
        b_value,
        w_out,
        b_out,
        ln2_gain,
        ln2_bias,
        w_fc,
        b_fc,
        w_proj,
        b_proj,
    )
    accum = tuple(
        (
            jnp.zeros((sharded.shape[0] * device_count,) + sharded.shape[1:], jnp.float32)
            for sharded in sharded_all
        )
    )
    outputs = []
    input_grads = []
    for micro_index in range(tokens.shape[0]):
        weights = (
            lax.all_gather(ln1_gain, ("dp", "sp"), axis=0, tiled=True),
            lax.all_gather(ln1_bias, ("dp", "sp"), axis=0, tiled=True),
            lax.all_gather(w_qkv, ("dp", "sp"), axis=0, tiled=True),
            lax.all_gather(b_query, ("dp", "sp"), axis=0, tiled=True),
            lax.all_gather(b_value, ("dp", "sp"), axis=0, tiled=True),
            lax.all_gather(w_out, ("dp", "sp"), axis=0, tiled=True),
            lax.all_gather(b_out, ("dp", "sp"), axis=0, tiled=True),
            lax.all_gather(ln2_gain, ("dp", "sp"), axis=0, tiled=True),
            lax.all_gather(ln2_bias, ("dp", "sp"), axis=0, tiled=True),
            lax.all_gather(w_fc, ("dp", "sp"), axis=0, tiled=True),
            lax.all_gather(b_fc, ("dp", "sp"), axis=0, tiled=True),
            lax.all_gather(w_proj, ("dp", "sp"), axis=0, tiled=True),
            lax.all_gather(b_proj, ("dp", "sp"), axis=0, tiled=True),
        )
        inputs = tokens[micro_index].astype(jnp.float32)
        split_at = seq_cut[micro_index, 0]
        layer_value, saved = forward_pass(inputs, weights, split_at, head_count)
        back_weights = (
            lax.all_gather(ln1_gain, ("dp", "sp"), axis=0, tiled=True),
            lax.all_gather(ln1_bias, ("dp", "sp"), axis=0, tiled=True),
            lax.all_gather(w_qkv, ("dp", "sp"), axis=0, tiled=True),
            lax.all_gather(b_query, ("dp", "sp"), axis=0, tiled=True),
            lax.all_gather(b_value, ("dp", "sp"), axis=0, tiled=True),
            lax.all_gather(w_out, ("dp", "sp"), axis=0, tiled=True),
            lax.all_gather(b_out, ("dp", "sp"), axis=0, tiled=True),
            lax.all_gather(ln2_gain, ("dp", "sp"), axis=0, tiled=True),
            lax.all_gather(ln2_bias, ("dp", "sp"), axis=0, tiled=True),
            lax.all_gather(w_fc, ("dp", "sp"), axis=0, tiled=True),
            lax.all_gather(b_fc, ("dp", "sp"), axis=0, tiled=True),
            lax.all_gather(w_proj, ("dp", "sp"), axis=0, tiled=True),
            lax.all_gather(b_proj, ("dp", "sp"), axis=0, tiled=True),
        )
        grad_inputs, grads = backward_pass(
            inputs, cotangent[micro_index], back_weights, saved, split_at, head_count
        )
        accum = tuple((earlier + latest for earlier, latest in zip(accum, grads)))
        outputs.append(layer_value)
        input_grads.append(grad_inputs)
    summed = (
        lax.psum_scatter(accum[0], ("dp", "sp"), scatter_dimension=0, tiled=True),
        lax.psum_scatter(accum[1], ("dp", "sp"), scatter_dimension=0, tiled=True),
        lax.psum_scatter(accum[2], ("dp", "sp"), scatter_dimension=0, tiled=True),
        lax.psum_scatter(accum[3], ("dp", "sp"), scatter_dimension=0, tiled=True),
        lax.psum_scatter(accum[4], ("dp", "sp"), scatter_dimension=0, tiled=True),
        lax.psum_scatter(accum[5], ("dp", "sp"), scatter_dimension=0, tiled=True),
        lax.psum_scatter(accum[6], ("dp", "sp"), scatter_dimension=0, tiled=True),
        lax.psum_scatter(accum[7], ("dp", "sp"), scatter_dimension=0, tiled=True),
        lax.psum_scatter(accum[8], ("dp", "sp"), scatter_dimension=0, tiled=True),
        lax.psum_scatter(accum[9], ("dp", "sp"), scatter_dimension=0, tiled=True),
        lax.psum_scatter(accum[10], ("dp", "sp"), scatter_dimension=0, tiled=True),
        lax.psum_scatter(accum[11], ("dp", "sp"), scatter_dimension=0, tiled=True),
        lax.psum_scatter(accum[12], ("dp", "sp"), scatter_dimension=0, tiled=True),
    )
    return (jnp.stack(outputs), jnp.stack(input_grads)) + tuple(summed)


def solution(mesh):
    return jax.shard_map(
        local,
        mesh=mesh,
        in_specs=(
            P(None, ("dp", "sp"), None),
            P(None, ("dp", "sp"), None),
            P(None, "dp"),
            P(("dp", "sp")),
            P(("dp", "sp")),
            P(("dp", "sp"), None),
            P(("dp", "sp")),
            P(("dp", "sp")),
            P(("dp", "sp"), None),
            P(("dp", "sp")),
            P(("dp", "sp")),
            P(("dp", "sp")),
            P(("dp", "sp"), None),
            P(("dp", "sp")),
            P(("dp", "sp"), None),
            P(("dp", "sp")),
        ),
        out_specs=(
            P(None, ("dp", "sp"), None),
            P(None, ("dp", "sp"), None),
            P(("dp", "sp")),
            P(("dp", "sp")),
            P(("dp", "sp"), None),
            P(("dp", "sp")),
            P(("dp", "sp")),
            P(("dp", "sp"), None),
            P(("dp", "sp")),
            P(("dp", "sp")),
            P(("dp", "sp")),
            P(("dp", "sp"), None),
            P(("dp", "sp")),
            P(("dp", "sp"), None),
            P(("dp", "sp")),
        ),
        check_vma=False,
    )
```

profile of v0, /device:TPU:0, one launch (start us, length us, event | category | flops | bytes accessed | tf_op | source)
XLA Modules:
  0.0 1036.2 jit_solution(12130181705662546807)
XLA Ops:
  17.4 42.9 %all-reduce.27 = (bf16[768]{0:T(1024)(128)(2,1)S(1)}, bf16[768]{0:T(1024)(128)(2,1)S(1)}, bf16[768]{0:T(1024)(128)(2,1)S(1)}, bf16[768]{0:T(1024)(128)(2,1)S(1)}...) all-reduce(bf16[768]{0:T(1024)(128)(2,1)S(1)} %dynamic-update-slice, ...), channel_id=1, replica_groups=mesh['dp'=8,'sp'=4] {'dp','sp'}, use_global_device_ids=true, to_apply=%add.11 | all-reduce | flops 9216 | bytes 36864
  64.7 9.1 all-gather.5.cloned.1.call-done
  79.3 4.0 all-to-all-start.5
  89.0 4.0 all-to-all-start.6
  98.4 4.1 all-to-all-start.4
  107.9 4.0 all-to-all-start.9
  117.9 4.0 all-to-all-start.10
  127.2 3.4 all-to-all-start.8
  135.9 3.4 all-to-all-start.13
  141.3 4.2 all-to-all-done.13
  145.6 3.4 all-to-all-start.14
  154.2 3.9 all-to-all-start.12
  171.4 3.4 all-to-all-start.15
  185.8 4.0 all-to-all-start.11
  195.1 4.2 all-to-all-start.7
  208.5 4.5 convolution_add_fusion.6
  212.9 49.0 %all-gather.11.cloned.1.call-done = bf16[3072,768]{1,0:T(8,128)(2,1)} async-done(((bf16[96,768]{1,0:T(8,128)(2,1)}), bf16[3072,768]{1,0:T(8,128)(2,1)}) %all-gather.11.cloned.1.call-update) | async-done | bytes 4718608 | tf_op jit(solution)/shard_map/all_gather | solution.py:343
  261.9 5.6 convert_reduce_fusion.2
  286.9 4.0 all-to-all-start.20
  298.7 4.0 all-to-all-start.24
  323.2 4.0 all-to-all-start.28
  350.4 4.0 all-to-all-start.23
  368.1 3.4 all-to-all-start.21
  372.5 4.3 all-to-all-done.21
  376.7 4.0 all-to-all-start.27
  382.6 3.5 all-to-all-done.27
  386.1 4.0 all-to-all-start.25
  392.0 3.5 all-to-all-done.25
  395.5 3.4 all-to-all-start.31
  405.5 3.4 all-to-all-start.29
  410.8 3.4 all-to-all-done.29
  414.2 3.4 all-to-all-start.30
  422.8 3.4 all-to-all-start.26
  426.2 4.1 fusion.200
  431.5 3.8 all-to-all-start.22
  435.3 3.5 fusion.202
  440.6 5.0 fusion.171
  455.9 3.4 all-to-all-start.2
  464.5 3.4 all-to-all-start
  467.9 5.1 fusion.203
  483.4 4.2 all-to-all-start.3
  488.8 4.0 all-to-all-done.3
  497.9 5.5 convert_reduce_fusion.3
  514.4 5.0 add_add_fusion.3
  524.2 3.4 all-to-all-start.19
  532.9 3.4 all-to-all-start.17
  537.3 4.2 all-to-all-done.17
  541.5 3.4 all-to-all-start.18
  545.2 5.6 fusion.201
  554.4 7.5 add_add_fusion.2
  566.1 5.3 fusion.218
  571.4 5.3 fusion.224
  576.7 11.4 %add_add_fusion = f32[3072,768]{1,0:T(8,128)} fusion(f32[3072,768]{1,0:T(8,128)S(1)} %fusion.212, f32[3072,768]{1,0:T(8,128)} %fusion.224, f32[3072,768]{1,0:T(8,128)} %fusion.218, bf16[4,128,768]{2,1,0:T(8,128)(2,1)S(1)} %copy-done.33, f32[128,3072]{1,0:T(8,128)S(1)} %copy-done.45), kind=kOutput, calls=%fused_computation | convolution fusion | flops 614891520 | bytes 39518208 | tf_op jit(solution)/shard_map/tf,tj->fj/dot_general | solution.py:226
  591.0 5.2 fusion.324
  596.3 5.0 fusion.322
  601.3 12.2 %add_add_fusion.1 = f32[768,3072]{1,0:T(8,128)} fusion(f32[768,3072]{1,0:T(8,128)} %fusion.324, f32[768,3072]{1,0:T(8,128)} %fusion.322, f32[768,3072]{1,0:T(8,128)S(1)} %fusion.323, bf16[128,3072]{1,0:T(8,128)(2,1)S(1)} %copy-done.68, f32[128,768]{1,0:T(8,128)S(1)} %copy-done.24, f32[128]{0:T(128)S(1)} %copy-done.220, f32[128]{0:T(128)S(1)} %copy-done.197, ...), kind=kOutput, calls=%fused_computation.1 | convolution fusion | flops 611549184 | bytes 38935552 | tf_op jit(solution)/shard_map/td,tf->df/dot_general | solution.py:231
  614.8 3.6 fusion.89
  618.4 3.6 fusion.90
  622.1 3.6 fusion.91
  642.4 4.0 fusion.158
  647.3 42.9 %all-reduce.26 = (f32[768]{0:T(1024)S(1)}, f32[768]{0:T(1024)S(1)}, f32[768]{0:T(1024)S(1)}, f32[768]{0:T(1024)S(1)}, f32[768]{0:T(1024)S(1)}, /*index=5*/f32[76...) all-reduce(f32[768]{0:T(1024)S(1)} %add_add_fusion.20, ...), channel_id=2, replica_groups=mesh['dp'=8,'sp'=4] {'dp','sp'}, use_global_device_ids=true, to_apply=%region_56.57.clone | all-reduce | flops 9216 | bytes 73728
  700.6 44.7 %reduce-scatter.5.cloned.1.call-done = f32[24,2304]{1,0:T(8,128)} async-done(((f32[768,2304]{1,0:T(8,128)}), f32[24,2304]{1,0:T(8,128)}) %reduce-scatter.5.cloned.1.call-update) | async-done | bytes 221200 | tf_op jit(solution)/shard_map/reduce_scatter | solution.py:373
  745.3 141.9 %reduce-scatter.11.cloned.1.call-done = f32[96,768]{1,0:T(8,128)} async-done(((f32[3072,768]{1,0:T(8,128)}), f32[96,768]{1,0:T(8,128)}) %reduce-scatter.11.cloned.1.call-update) | async-done | bytes 294928 | tf_op jit(solution)/shard_map/reduce_scatter | solution.py:382
  887.2 141.6 %reduce-scatter.9.cloned.1.call-done = f32[24,3072]{1,0:T(8,128)} async-done(((f32[768,3072]{1,0:T(8,128)}), f32[24,3072]{1,0:T(8,128)}) %reduce-scatter.9.cloned.1.call-update) | async-done | bytes 294928 | tf_op jit(solution)/shard_map/reduce_scatter | solution.py:380
  (926 shorter events, 297.0 us)
Async XLA Ops:
  7.3 66.5 %all-gather.5.cloned.1.call-start = ((), (), s32[]{:S(2)}) async-start(), calls=%async_computation.36 | async-start | bytes 3649536 | tf_op jit(solution)/shard_map/all_gather | solution.py:334
  8.0 181.8 %all-gather.7.cloned.1.call-start = ((), (), s32[]{:S(2)}) async-start(), calls=%async_computation.37 | async-start | bytes 1216512 | tf_op jit(solution)/shard_map/all_gather | solution.py:337
  8.8 199.7 %all-gather.9.cloned.1.call-start = ((), (), s32[]{:S(2)}) async-start(), calls=%async_computation.38 | async-start | bytes 4866048 | tf_op jit(solution)/shard_map/all_gather | solution.py:341
  9.5 252.4 %all-gather.11.cloned.1.call-start = ((), (), s32[]{:S(2)}) async-start(), calls=%async_computation.39 | async-start | bytes 4866048 | tf_op jit(solution)/shard_map/all_gather | solution.py:343
  13.4 63.4 %copy-start.185 = (f32[128]{0:T(128)}, f32[128]{0:T(128)S(1)}, u32[]{:S(2)}) copy-start(f32[128]{0:T(128)S(1)} %broadcast_multiply_fusion.5) | copy-start | bytes 1540
  13.4 46.9 %copy-start.208 = (f32[128]{0:T(128)}, f32[128]{0:T(128)S(1)}, u32[]{:S(2)}) copy-start(f32[128]{0:T(128)S(1)} %get-tuple-element.445) | copy-start | bytes 1540
  13.4 79.6 %copy-start.148 = (f32[128]{0:T(128)}, f32[128]{0:T(128)S(1)}, u32[]{:S(2)}) copy-start(f32[128]{0:T(128)S(1)} %get-tuple-element.446) | copy-start | bytes 1540
  14.2 50.5 %copy-start.251 = (f32[128]{0:T(128)}, f32[128]{0:T(128)S(1)}, u32[]{:S(2)}) copy-start(f32[128]{0:T(128)S(1)} %get-tuple-element.305) | copy-start | bytes 1540
  14.2 50.5 %copy-start.253 = (f32[128]{0:T(128)}, f32[128]{0:T(128)S(1)}, u32[]{:S(2)}) copy-start(f32[128]{0:T(128)S(1)} %get-tuple-element.304) | copy-start | bytes 1540
  73.8 19.2 %copy-start.2 = (bf16[768,2304]{1,0:T(8,128)(2,1)S(1)}, bf16[768,2304]{1,0:T(8,128)(2,1)}, u32[]{:S(2)}) copy-start(bf16[768,2304]{1,0:T(8,128)(2,1)} %all-gather.5.cloned.1.call-done) | copy-start | bytes 10616836
  79.3 9.6 all-to-all-start.5
  89.0 9.4 all-to-all-start.6
  95.5 18.3 %copy-start.222 = (s32[512]{0:T(512)S(1)}, s32[512]{0:T(512)}, u32[]{:S(2)}) copy-start(s32[512]{0:T(512)} %copy-done.221) | copy-start | bytes 6148
  98.4 23.5 %copy-start.209 = (f32[128]{0:T(128)S(1)}, f32[128]{0:T(128)}, u32[]{:S(2)}) copy-start(f32[128]{0:T(128)} %copy-done.208) | copy-start | bytes 1540
  98.4 9.5 all-to-all-start.4
  107.9 10.0 all-to-all-start.9
  117.9 9.4 all-to-all-start.10
  127.2 8.6 all-to-all-start.8
  130.6 18.3 %slice-start.4 = ((s32[512]{0:T(512)}), s32[256]{0:T(256)S(1)}, s32[]{:S(2)}) async-start(s32[512]{0:T(512)} %copy-done.216), calls=%async_computation.48 | async-start | bytes 2048 | tf_op jit(solution)/shard_map/slice | solution.py:36
  130.6 18.3 %copy-start.225 = (pred[256]{0:T(512)(128)(4,1)S(1)}, pred[256]{0:T(512)(128)(4,1)}, u32[]{:S(2)}) copy-start(pred[256]{0:T(512)(128)(4,1)} %get-tuple-element.447) | copy-start | bytes 772
  130.6 18.3 %copy-start.226 = (pred[256]{0:T(512)(128)(4,1)S(1)}, pred[256]{0:T(512)(128)(4,1)}, u32[]{:S(2)}) copy-start(pred[256]{0:T(512)(128)(4,1)} %get-tuple-element.448) | copy-start | bytes 772
  130.6 18.3 %copy-start.227 = (pred[256]{0:T(512)(128)(4,1)S(1)}, pred[256]{0:T(512)(128)(4,1)}, u32[]{:S(2)}) copy-start(pred[256]{0:T(512)(128)(4,1)} %get-tuple-element.449) | copy-start | bytes 772
  130.6 18.3 %copy-start.228 = (pred[256]{0:T(512)(128)(4,1)S(1)}, pred[256]{0:T(512)(128)(4,1)}, u32[]{:S(2)}) copy-start(pred[256]{0:T(512)(128)(4,1)} %get-tuple-element.450) | copy-start | bytes 772
  130.6 19.2 %copy-start.236 = (bf16[768]{0:T(1024)(128)(2,1)S(1)}, bf16[768]{0:T(1024)(128)(2,1)}, u32[]{:S(2)}) copy-start(bf16[768]{0:T(1024)(128)(2,1)} %get-tuple-element.332) | copy-start | bytes 4612
  130.7 19.2 %copy-start.235 = (bf16[768]{0:T(1024)(128)(2,1)S(1)}, bf16[768]{0:T(1024)(128)(2,1)}, u32[]{:S(2)}) copy-start(bf16[768]{0:T(1024)(128)(2,1)} %get-tuple-element.331) | copy-start | bytes 4612
  130.7 19.3 %copy-start.234 = (bf16[768]{0:T(1024)(128)(2,1)S(1)}, bf16[768]{0:T(1024)(128)(2,1)}, u32[]{:S(2)}) copy-start(bf16[768]{0:T(1024)(128)(2,1)} %get-tuple-element.328) | copy-start | bytes 4612
  130.7 19.8 %copy-start.223 = (bf16[3072]{0:T(1024)(128)(2,1)S(1)}, bf16[3072]{0:T(1024)(128)(2,1)}, u32[]{:S(2)}) copy-start(bf16[3072]{0:T(1024)(128)(2,1)} %get-tuple-element.330) | copy-start | bytes 18436
  131.9 26.3 %copy-start.256 = (f32[128]{0:T(128)S(1)}, f32[128]{0:T(128)}, u32[]{:S(2)}) copy-start(f32[128]{0:T(128)} %get-tuple-element.300) | copy-start | bytes 1540
  135.9 9.7 all-to-all-start.13
  145.6 8.6 all-to-all-start.14
  154.2 11.5 %all-to-all-start.12 = ((bf16[4,192,128]{2,1,0:T(8,128)(2,1)}), bf16[4,192,128]{2,1,0:T(8,128)(2,1)S(1)}, u32[]{:S(2)}, u32[]{:S(2)}) async-start(bf16[4,192,128]{2,1,0:T(8,128)(2,1)} %bitcast.38), calls=%async_computation.12 | async-start | bytes 393216 | tf_op jit(solution)/shard_map/all_to_all | solution.py:160
  159.9 19.0 %copy-start.101 = (bf16[3,64,512]{2,1,0:T(8,128)(2,1)}, bf16[3,64,512]{2,1,0:T(8,128)(2,1)S(1)}, u32[]{:S(2)}) copy-start(bf16[3,64,512]{2,1,0:T(8,128)(2,1)S(1)} %reshape.1523) | copy-start | bytes 589828
  162.4 17.9 %copy-start.109 = (bf16[3,64,512]{2,1,0:T(8,128)(2,1)}, bf16[3,64,512]{2,1,0:T(8,128)(2,1)S(1)}, u32[]{:S(2)}) copy-start(bf16[3,64,512]{2,1,0:T(8,128)(2,1)S(1)} %reshape.1522) | copy-start | bytes 589828
  171.4 14.4 %all-to-all-start.15 = ((bf16[192,4,128]{2,0,1:T(8,128)(2,1)}), bf16[192,4,128]{2,0,1:T(8,128)(2,1)S(1)}, u32[]{:S(2)}, u32[]{:S(2)}) async-start(bf16[192,4,128]{2,0,1:T(8,128)(2,1)} %copy.166), calls=%async_computation.15 | async-start | bytes 393216 | tf_op jit(solution)/shard_map/all_to_all | solution.py:163
  185.8 9.4 all-to-all-start.11
  195.1 9.4 all-to-all-start.7
  286.9 11.8 %all-to-all-start.20 = ((bf16[4,192,128]{2,1,0:T(8,128)(2,1)}), bf16[4,192,128]{2,1,0:T(8,128)(2,1)}, u32[]{:S(2)}, u32[]{:S(2)}) async-start(bf16[4,192,128]{2,1,0:T(8,128)(2,1)} %bitcast.444), calls=%async_computation.20 | async-start | bytes 393216 | tf_op jit(solution)/shard_map/all_to_all | solution.py:247
  298.7 24.5 %all-to-all-start.24 = ((bf16[4,192,128]{2,1,0:T(8,128)(2,1)}), bf16[4,192,128]{2,1,0:T(8,128)(2,1)}, u32[]{:S(2)}, u32[]{:S(2)}) async-start(bf16[4,192,128]{2,1,0:T(8,128)(2,1)} %bitcast.434), calls=%async_computation.24 | async-start | bytes 393216 | tf_op jit(solution)/shard_map/all_to_all | solution.py:247
  323.2 27.2 %all-to-all-start.28 = ((bf16[4,192,128]{2,1,0:T(8,128)(2,1)}), bf16[4,192,128]{2,1,0:T(8,128)(2,1)}, u32[]{:S(2)}, u32[]{:S(2)}) async-start(bf16[4,192,128]{2,1,0:T(8,128)(2,1)} %bitcast.431), calls=%async_computation.28 | async-start | bytes 393216 | tf_op jit(solution)/shard_map/all_to_all | solution.py:247
  350.4 17.7 %all-to-all-start.23 = ((bf16[192,4,128]{2,0,1:T(8,128)(2,1)}), bf16[192,4,128]{2,0,1:T(8,128)(2,1)}, u32[]{:S(2)}, u32[]{:S(2)}) async-start(bf16[192,4,128]{2,0,1:T(8,128)(2,1)} %copy.184), calls=%async_computation.23 | async-start | bytes 393216 | tf_op jit(solution)/shard_map/all_to_all | solution.py:254
  368.1 8.6 all-to-all-start.21
  376.7 18.7 %copy-start.84 = (bf16[192,4,128]{2,0,1:T(8,128)(2,1)}, bf16[192,4,128]{2,0,1:T(8,128)(2,1)S(1)}, u32[]{:S(2)}) copy-start(bf16[192,4,128]{2,0,1:T(8,128)(2,1)S(1)} %all-to-all-done.21) | copy-start | bytes 589828
  376.7 9.4 all-to-all-start.27
  386.1 9.4 all-to-all-start.25
  395.5 10.1 all-to-all-start.31
  405.5 20.7 %copy-start.76 = (bf16[192,4,128]{2,0,1:T(8,128)(2,1)}, bf16[192,4,128]{2,0,1:T(8,128)(2,1)S(1)}, u32[]{:S(2)}) copy-start(bf16[192,4,128]{2,0,1:T(8,128)(2,1)S(1)} %all-to-all-done.31) | copy-start | bytes 589828
  405.5 8.6 all-to-all-start.29
  414.2 8.6 all-to-all-start.30
  422.8 8.6 all-to-all-start.26
  431.5 9.0 all-to-all-start.22
  447.2 8.6 all-to-all-start.1
  455.9 8.6 all-to-all-start.2
  464.5 9.0 all-to-all-start
  483.4 9.5 all-to-all-start.3
  510.9 8.6 all-to-all-start.16
  514.3 186.3 %reduce-scatter.7.cloned.1.call-start = ((), (), s32[]{:S(2)}) async-start(), calls=%async_computation.41 | async-start | bytes 2433024 | tf_op jit(solution)/shard_map/reduce_scatter | solution.py:376
  524.2 8.6 all-to-all-start.19
  532.9 8.6 all-to-all-start.17
  541.5 9.3 all-to-all-start.18
  544.9 200.4 %reduce-scatter.5.cloned.1.call-start = ((), (), s32[]{:S(2)}) async-start(), calls=%async_computation.40 | async-start | bytes 7299072 | tf_op jit(solution)/shard_map/reduce_scatter | solution.py:373
  561.9 325.3 %reduce-scatter.11.cloned.1.call-start = ((), (), s32[]{:S(2)}) async-start(), calls=%async_computation.43 | async-start | bytes 9732096 | tf_op jit(solution)/shard_map/reduce_scatter | solution.py:382
  588.2 440.7 %reduce-scatter.9.cloned.1.call-start = ((), (), s32[]{:S(2)}) async-start(), calls=%async_computation.42 | async-start | bytes 9732096 | tf_op jit(solution)/shard_map/reduce_scatter | solution.py:380
  646.5 50.3 %copy-start.8 = (bf16[4,128,768]{2,1,0:T(8,128)(2,1)S(1)}, bf16[4,128,768]{2,1,0:T(8,128)(2,1)}, u32[]{:S(2)}) copy-start(bf16[4,128,768]{2,1,0:T(8,128)(2,1)} %param.64) | copy-start | bytes 2359300
  646.5 50.3 %copy-start.54 = (f32[128,768]{1,0:T(8,128)S(1)}, f32[128,768]{1,0:T(8,128)}, u32[]{:S(2)}) copy-start(f32[128,768]{1,0:T(8,128)} %copy-done.53) | copy-start | bytes 1179652
  (263 other events, 1195.6 us)
Sparse Core Ops, SparseCore 0:
  11.0 62.7 all-gather.4
  76.7 52.8 all-gather.6
  132.5 64.6 all-gather.8
  200.0 61.9 all-gather.10
  520.7 99.3 reduce-scatter.6
  626.2 119.0 reduce-scatter.4
  751.8 135.4 reduce-scatter.10
  893.7 135.1 reduce-scatter.8
where the time goes:
time: 1050 us; the launch traced here: 1040 us
  waiting for transfers between devices  445 us (42%)
  matrix products  213 us (20%)
  starting transfers between devices  119 us (11%)
  local copies, waits for them, and re-layouts  96.8 us (9%)
  blocking collectives  85.8 us (8%)
  other arithmetic  57.9 us (6%)
  between operations  18.4 us (2%)
    reduce_scatter x1, waiting for transfers between devices, local(): lax.psum_scatter(accum[11], ('dp', 'sp'), scatter_dimension=0, tiled=True)  142 us
    reduce_scatter x1, waiting for transfers between devices, local(): lax.psum_scatter(accum[9], ('dp', 'sp'), scatter_dimension=0, tiled=True)  142 us
    unnamed x2, blocking collectives  85.8 us
    all_gather x1, waiting for transfers between devices, local(): lax.all_gather(w_proj, ('dp', 'sp'), axis=0, tiled=True)  49 us
    reduce_scatter x1, waiting for transfers between devices, local(): lax.psum_scatter(accum[2], ('dp', 'sp'), scatter_dimension=0, tiled=True)  44.7 us
    dot_general x4, matrix products, backward_pass(): jnp.einsum('tf,tj->fj', act_low, grad_mlp, preferred_element_type=jnp.flo...  25 us
    dot_general x4, matrix products, backward_pass(): jnp.einsum('td,tf->df', normed_two_low, grad_pre, preferred_element_type=...  24 us
  transfers between devices with their start and end apart: 40, of which 27 were waited for; matrix products, arithmetic and copies ran while one was open for 29% of the time, Pallas kernels for 0%

commit v1 on v0

v1 whole, which is shorter than its diff:
```python
import jax
import jax.numpy as jnp
from jax import lax
from jax.sharding import PartitionSpec as P

HEADS = 12
HEAD = 64
EPSILON = 1e-05
BRANCH = 24.0 ** (-0.5)
NEGATIVE = -1e30
GELU_A = 0.7978845608028654
GELU_B = 0.044715
AXES = ("dp", "sp")
F32 = jnp.float32
BF16 = jnp.bfloat16


def dot(a, b, dims):
    return lax.dot_general(a, b, (dims, ((), ())), preferred_element_type=F32)


def mm(a, b):
    return dot(a, b, ((1,), (0,)))


def mm_nt(a, b):
    return dot(a, b, ((1,), (1,)))


def mm_tn(a, b):
    return dot(a, b, ((0,), (0,)))


def norm_stats(rows):
    center = jnp.mean(rows, axis=-1, keepdims=True)
    centred = rows - center
    inverse = lax.rsqrt(jnp.mean(centred * centred, axis=-1, keepdims=True) + EPSILON)
    return centred * inverse, inverse


def norm_back(xhat, inverse, grad):
    mean_grad = jnp.mean(grad, axis=-1, keepdims=True)
    mean_proj = jnp.mean(grad * xhat, axis=-1, keepdims=True)
    return inverse * (grad - mean_grad - xhat * mean_proj)


def split_heads(rows):
    return rows.reshape(rows.shape[0], HEADS, HEAD).transpose(1, 0, 2)


def join_heads(heads):
    return heads.transpose(1, 0, 2).reshape(heads.shape[1], HEADS * HEAD)


def layer(x16, dy16, cut, big, small):
    w_qkv, w_out, w_fc, w_proj = big
    g1, o1, bq, bv, bo, g2, o2, bf, bp = [v.astype(F32)[None] for v in small]
    length = x16.shape[0]
    x = x16.astype(F32)
    xhat1, inv1 = norm_stats(x)
    h1 = (xhat1 * g1 + o1).astype(BF16)
    bias = jnp.concatenate([bq, jnp.zeros_like(bq), bv], axis=1)
    qkv = (mm(h1, w_qkv) + bias).astype(BF16)
    width = HEADS * HEAD
    q, k, v = (split_heads(qkv[:, i * width : (i + 1) * width]) for i in range(3))
    pos = lax.iota(jnp.int32, length)
    allowed = (pos[None, :] <= pos[:, None]) & ((pos[None, :] >= cut) == (pos[:, None] >= cut))
    scale = HEAD ** (-0.5)
    scores = jnp.einsum("hqd,hkd->hqk", q, k, preferred_element_type=F32) * scale
    scores = jnp.where(allowed[None], scores, NEGATIVE)
    top = jnp.max(scores, axis=-1, keepdims=True)
    expo = jnp.exp(scores - top)
    prob32 = expo / jnp.sum(expo, axis=-1, keepdims=True)
    prob = prob32.astype(BF16)
    attn32 = jnp.einsum("hqk,hkd->hqd", prob, v, preferred_element_type=F32)
    attn = join_heads(attn32).astype(BF16)
    x1 = x + BRANCH * (mm(attn, w_out) + bo)
    xhat2, inv2 = norm_stats(x1)
    h2 = (xhat2 * g2 + o2).astype(BF16)
    pre = mm(h2, w_fc) + bf
    t = jnp.tanh(GELU_A * (pre + GELU_B * pre * pre * pre))
    act = (0.5 * pre * (1 + t)).astype(BF16)
    slope = 0.5 * (1 + t) + 0.5 * pre * (1 - t * t) * (GELU_A * (1 + 3 * GELU_B * pre * pre))
    out = (x1 + BRANCH * (mm(act, w_proj) + bp)).astype(BF16)

    dy = dy16.astype(F32)
    d_mlp = (dy * BRANCH).astype(BF16)
    g_w_proj = mm_tn(act, d_mlp)
    g_b_proj = jnp.sum(d_mlp.astype(F32), axis=0)
    d_pre = (mm_nt(d_mlp, w_proj) * slope).astype(BF16)
    g_w_fc = mm_tn(h2, d_pre)
    g_b_fc = jnp.sum(d_pre.astype(F32), axis=0)
    d_h2 = mm_nt(d_pre, w_fc)
    g_g2 = jnp.sum(d_h2 * xhat2, axis=0)
    g_o2 = jnp.sum(d_h2, axis=0)
    d_x1 = dy + norm_back(xhat2, inv2, d_h2 * g2)
    d_branch = (d_x1 * BRANCH).astype(BF16)
    g_w_out = mm_tn(attn, d_branch)
    g_b_out = jnp.sum(d_branch.astype(F32), axis=0)
    d_attn = split_heads(mm_nt(d_branch, w_out).astype(BF16))
    delta = jnp.sum(d_attn.astype(F32) * attn32, axis=-1, keepdims=True)
    d_prob = jnp.einsum("hqd,hkd->hqk", d_attn, v, preferred_element_type=F32)
    d_scores = (prob32 * (d_prob - delta)).astype(BF16)
    d_q = jnp.einsum("hqk,hkd->hqd", d_scores, k, preferred_element_type=F32) * scale
    d_k = jnp.einsum("hqk,hqd->hkd", d_scores, q, preferred_element_type=F32) * scale
    d_v = jnp.einsum("hqk,hqd->hkd", prob, d_attn, preferred_element_type=F32)
    d_qkv = jnp.concatenate([join_heads(d_q), join_heads(d_k), join_heads(d_v)], axis=1).astype(BF16)
    g_w_qkv = mm_tn(h1, d_qkv)
    g_b_qkv = jnp.sum(d_qkv.astype(F32), axis=0)
    d_h1 = mm_nt(d_qkv, w_qkv)
    g_g1 = jnp.sum(d_h1 * xhat1, axis=0)
    g_o1 = jnp.sum(d_h1, axis=0)
    d_x = d_x1 + norm_back(xhat1, inv1, d_h1 * g1)
    big_grads = (g_w_qkv, g_w_out, g_w_fc, g_w_proj)
    small_grads = (g_g1, g_o1, g_b_qkv[:width], g_b_qkv[2 * width :], g_b_out, g_g2, g_o2, g_b_fc, g_b_proj)
    return out, d_x, big_grads, small_grads


def local(tokens, cotangent, seq_cut, g1, o1, w_qkv, bq, bv, w_out, bo, g2, o2, w_fc, bf, w_proj, bp):
    ways = lax.axis_size("sp")
    devices = ways * lax.axis_size("dp")
    small = (g1, o1, bq, bv, bo, g2, o2, bf, bp)
    sizes = [v.shape[0] for v in small]
    big = [lax.all_gather(w, AXES, axis=0, tiled=True) for w in (w_qkv, w_out, w_fc, w_proj)]
    packed = lax.all_gather(jnp.concatenate(small), AXES, axis=0)
    cuts = [sum(sizes[:i]) for i in range(len(sizes) + 1)]
    vectors = [packed[:, a:b].reshape(-1) for a, b in zip(cuts[:-1], cuts[1:])]
    x16 = lax.all_to_all(tokens, "sp", split_axis=0, concat_axis=1, tiled=True)
    dy16 = lax.all_to_all(cotangent, "sp", split_axis=0, concat_axis=1, tiled=True)
    packs = x16.shape[0]
    first = lax.axis_index("sp") * packs
    outs, grads_in, big_sum, small_sum = [], [], None, None
    for i in range(packs):
        cut = lax.dynamic_slice(seq_cut, (first + i, 0), (1, 1))[0, 0]
        out, d_x, bigs, smalls = layer(x16[i], dy16[i], cut, big, vectors)
        outs.append(out)
        grads_in.append(d_x)
        big_sum = bigs if big_sum is None else [a + b for a, b in zip(big_sum, bigs)]
        small_sum = smalls if small_sum is None else [a + b for a, b in zip(small_sum, smalls)]
    out = lax.all_to_all(jnp.stack(outs), "sp", split_axis=1, concat_axis=0, tiled=True)
    d_x = lax.all_to_all(jnp.stack(grads_in), "sp", split_axis=1, concat_axis=0, tiled=True)
    big_out = [
        lax.psum_scatter(g.astype(BF16), AXES, scatter_dimension=0, tiled=True).astype(F32) for g in big_sum
    ]
    small_pack = jnp.concatenate([g.reshape(devices, -1) for g in small_sum], axis=1)
    small_out = lax.psum_scatter(small_pack, AXES, scatter_dimension=0, tiled=True)[0]
    s = [small_out[a:b] for a, b in zip(cuts[:-1], cuts[1:])]
    return (out, d_x, s[0], s[1], big_out[0], s[2], s[3], big_out[1], s[4], s[5], s[6], big_out[2], s[7], big_out[3], s[8])


def solution(mesh):
    row = P(AXES, None)
    vec = P(AXES)
    act = P(None, AXES, None)
    return jax.shard_map(
        local,
        mesh=mesh,
        in_specs=(act, act, P(None, "dp"), vec, vec, row, vec, vec, row, vec, vec, vec, row, vec, row, vec),
        out_specs=(act, act, vec, vec, row, vec, vec, row, vec, vec, vec, row, vec, row, vec),
        check_vma=False,
    )
```

time: 1050 us -> 732 us (0.70)
  matrix products: 213 us -> 93.9 us
  starting transfers between devices: 119 us -> 16.2 us
  local copies, waits for them, and re-layouts: 96.8 us -> 35.2 us
  other arithmetic: 57.9 us -> 28.7 us
    dot_general x96 -> x17, matrix products: 213 us -> 86 us  [the longest x12 63.6 us: dot(): return lax.dot_general(a, b, (dims, ((), ())), preferred_element_type=F32)]
    all_to_all x32 -> x4, starting transfers between devices: 118 us -> 15.8 us  [the longest x1 4.25 us: local(): x16 = lax.all_to_all(tokens, 'sp', split_axis=0, concat_axis=1, tiled=True)]
    all_gather x4, waiting for transfers between devices: 58.1 us -> 140 us  [local(): lax.all_gather(w, AXES, axis=0, tiled=True)]
    all_to_all x32 -> x4, waiting for transfers between devices: 56.2 us -> 14.7 us  [the longest x1 11 us: local(): lax.all_to_all(cotangent, 'sp', split_axis=0, concat_axis=1, tiled=True)]
    reduce_scatter x4, waiting for transfers between devices: 328 us -> 287 us  [local(): lax.psum_scatter(g.astype(BF16), AXES, scatter_dimension=0, tiled=True)]
    convert_element_type x36 -> x10, local copies, waits for them, and re-layouts: 34.6 us -> 3.04 us  [the longest x1 2.31 us: layer(): d_attn = split_heads(mm_nt(d_branch, w_out).astype(BF16))]
    slice x24 -> x7, local copies, waits for them, and re-layouts: 22 us -> 3.09 us  [the longest x4 1.88 us: layer(): q, k, v = (split_heads(qkv[:, i * width:(i + 1) * width]) for i in range(3))]
    reduce_sum x31 -> x7, other arithmetic: 20.3 us -> 5.11 us  [the longest x1 1.76 us: layer(): g_b_qkv = jnp.sum(d_qkv.astype(F32), axis=0)]
  transfers between devices with their start and end apart: 40 -> 12, of which waited for: 27 -> 8; matrix products, arithmetic and copies ran while one was open for 29% -> 17% of each run, Pallas kernels for 0% -> 0%
where the time goes in v1:
time: 732 us; the launch traced here: 726 us
  waiting for transfers between devices  445 us (61%)
  matrix products  93.9 us (13%)
  blocking collectives  92.2 us (13%)
  local copies, waits for them, and re-layouts  35.2 us (5%)
  other arithmetic  28.7 us (4%)
  starting transfers between devices  16.2 us (2%)
  between operations  15 us (2%)
    reduce_scatter x4, waiting for transfers between devices, local(): lax.psum_scatter(g.astype(BF16), AXES, scatter_dimension=0, tiled=True)  287 us
    all_gather x4, waiting for transfers between devices, local(): lax.all_gather(w, AXES, axis=0, tiled=True)  140 us
    unnamed x2, blocking collectives  92.2 us
    dot_general x12, matrix products, dot(): return lax.dot_general(a, b, (dims, ((), ())), preferred_element_type=F32)  63.6 us
    unnamed x65, local copies, waits for them, and re-layouts  16.3 us
  transfers between devices with their start and end apart: 12, of which 8 were waited for; matrix products, arithmetic and copies ran while one was open for 17% of the time, Pallas kernels for 0%

profile of v1, /device:TPU:0, one launch (start us, length us, event | category | flops | bytes accessed | tf_op | source)
XLA Modules:
  0.0 725.9 jit_solution(14948380876119199890)
XLA Ops:
  7.2 0.7 all-gather.6.cloned.1.call-update
  8.0 0.7 all-gather.8.cloned.1.call-update
  8.7 0.7 all-gather.10.cloned.1.call-update
  9.5 0.5 all-gather.12.cloned.1.call-update
  10.0 4.2 all-to-all-start
  14.2 6.1 concatenate.13
  20.6 42.4 %all-reduce = bf16[9216]{0:T(1024)(128)(2,1)S(1)} all-reduce(bf16[9216]{0:T(1024)(128)(2,1)S(1)} %dynamic-update-slice), channel_id=2, replica_groups=mesh['dp'=8,'sp'=4] {'dp','sp'}, use_global_device_ids=true, to_apply=%add | all-reduce | flops 9216 | bytes 36864
  64.0 0.6 constant_dynamic-slice_fusion
  64.6 0.7 iota_compare_fusion.1
  65.5 3.8 all-to-all-start.2
  69.8 11.0 %all-to-all-done.2 = bf16[4,128,768]{2,1,0:T(8,128)(2,1)S(1)} async-done(((bf16[4,128,768]{2,1,0:T(8,128)(2,1)}), bf16[4,128,768]{2,1,0:T(8,128)(2,1)S(1)}, u32[]{:S(2)}, u32[]{:S(2)}) %all-to-all-start.2) | async-done | bytes 786464 | tf_op jit(solution)/shard_map/all_to_all | solution.py:129
  80.9 1.2 fusion.16
  82.5 0.9 copy-done.22
  83.3 4.0 fusion.14
  87.5 1.2 copy.62
  89.3 7.9 %fusion.44 = (f32[12,512]{1,0:T(8,128)S(1)}, f32[12,512,512]{1,2,0:T(8,128)}) fusion(pred[512,512]{0,1:T(8,128)(4,1)S(1)} %fusion.34, bf16[12,512,64]{1,2,0:T(8,128)(2,1)S(1)} %bitcast.138, bf16[12,512,64]{1,2,0:T(8,128)(2,1)S(1)} %bitcast.122), kind=kOutput, calls=%fused_computation.111 | convolution fusion | flops 415236608 | bytes 14442496 | tf_op jit(solution)/shard_map/sub | solution.py:72
  97.2 6.5 fusion.13
  103.7 2.6 copy-done.2
  106.2 3.7 fusion.45
  109.9 19.9 %all-gather.8.cloned.1.call-done = bf16[768,768]{1,0:T(8,128)(2,1)} async-done(((bf16[24,768]{1,0:T(8,128)(2,1)}), bf16[768,768]{1,0:T(8,128)(2,1)}) %all-gather.8.cloned.1.call-update) | async-done | bytes 1179664 | tf_op jit(solution)/shard_map/all_gather | solution.py:124
  129.8 2.7 fusion.46
  132.9 62.4 %all-gather.10.cloned.1.call-done = bf16[768,3072]{1,0:T(8,128)(2,1)} async-done(((bf16[24,3072]{1,0:T(8,128)(2,1)}), bf16[768,3072]{1,0:T(8,128)(2,1)}) %all-gather.10.cloned.1.call-update) | async-done | bytes 4718608 | tf_op jit(solution)/shard_map/all_gather | solution.py:124
  195.3 7.0 fusion.41
  202.3 57.7 %all-gather.12.cloned.1.call-done = bf16[3072,768]{1,0:T(8,128)(2,1)} async-done(((bf16[96,768]{1,0:T(8,128)(2,1)}), bf16[3072,768]{1,0:T(8,128)(2,1)}) %all-gather.12.cloned.1.call-update) | async-done | bytes 4718608 | tf_op jit(solution)/shard_map/all_gather | solution.py:124
  260.0 9.3 %convert_reduce_fusion = (f32[3072]{0:T(1024)S(1)}, bf16[512,3072]{1,0:T(8,128)(2,1)S(1)}) fusion(f32[512,3072]{1,0:T(8,128)} %fusion.41, f32[3072]{0:T(1024)S(1)} %reshape.361, bf16[512,768]{1,0:T(8,128)(2,1)S(1)} %copy-done.21, bf16[3072,768]{1,0:T(8,128)(2,1)} %all-gather.12.cloned.1.call-done), kind=kOutput, calls=%fused_computation.15 | convolution fusion | flops 2450519040 | bytes 14966784 | tf_op jit(solution)/shard_map/dot_general | solution.py:19
  269.3 3.1 multiply_reduce_fusion
  272.4 0.7 convert_reduce_fusion.4
  273.5 1.8 convolution_convert_fusion.3
  275.3 3.2 convolution_convert_fusion.4
  278.5 2.3 copy.65
  280.8 1.6 multiply_reduce_fusion.1
  282.4 7.6 %multiply_convert_fusion = bf16[12,512,512]{1,2,0:T(8,128)(2,1)} fusion(f32[12,512]{1,0:T(8,128)S(1)} %multiply_reduce_fusion.1, f32[12,512,512]{1,2,0:T(8,128)} %get-tuple-element.49, f32[12,512]{1,0:T(8,128)S(1)} %get-tuple-element.48, bf16[12,512,64]{1,2,0:T(8,128)(2,1)S(1)} %bitcast.120, bf16[12,512,64]{1,2,0:T(8,128)(2,1)S(1)} %bitcast.130), kind=kOutput, calls=%fused_computation.1 | convolution fusion | flops 415236096 | bytes 20496384 | tf_op jit(solution)/shard_map/hqd,hkd->hqk/dot_general | solution.py:102
  290.1 4.0 multiply_convert_fusion.3
  294.1 5.2 convolution_convert_fusion.5
  299.3 2.0 multiply_convert_fusion.2
  301.4 0.9 copy-done.26
  302.2 3.9 convolution_convert_fusion.2
  306.2 1.3 copy-done.19
  307.5 6.4 convolution_convert_fusion.1
  314.2 8.9 %convolution_convert_fusion = bf16[3072,768]{1,0:T(8,128)(2,1)} fusion(bf16[512,768]{1,0:T(8,128)(2,1)} %fusion.16, f32[512,3072]{1,0:T(8,128)} %fusion.41, f32[3072]{0:T(1024)S(1)} %reshape.361), kind=kOutput, calls=%fused_computation.22 | convolution fusion | flops 2434007040 | bytes 11808768 | tf_op jit(solution)/shard_map/dot_general | solution.py:19
  323.2 8.2 %fusion.33 = bf16[1,512,768]{2,1,0:T(8,128)(2,1)S(1)} fusion(f32[512,768]{1,0:T(8,128)S(1)} %copy-done.19, bf16[3072,768]{1,0:T(8,128)(2,1)} %all-gather.12.cloned.1.call-done, f32[768]{0:T(1024)S(1)} %reshape.362, f32[512,3072]{1,0:T(8,128)} %fusion.41, f32[3072]{0:T(1024)S(1)} %reshape.361), kind=kOutput, calls=%fused_computation.70 | convolution fusion | flops 2433220608 | bytes 13384704 | tf_op jit(solution)/shard_map/dot_general | solution.py:19
  331.4 2.4 copy.79
  334.3 7.7 %reduce.13 = bf16[512,768]{1,0:T(8,128)(2,1)} reduce(bf16[512,1,768]{2,1,0:T(2,128)(2,1)} %bitcast.131, bf16[]{:T(256)} %broadcast.186), dimensions={1}, to_apply=%bitcast.118.reduce_sub_computation | reduce | bytes 1572866
  342.0 2.0 reshape.374
  344.0 4.2 all-to-all-start.1
  348.2 5.1 fusion.30
  353.3 0.6 fusion.29
  353.9 2.8 copy.70
  356.7 3.7 all-to-all-done.1
  360.4 3.6 all-to-all-start.3
  364.4 1.8 convert_reduce_fusion.1
  366.8 49.8 %all-reduce.1 = f32[32,288]{1,0:T(8,128)S(1)} all-reduce(f32[32,288]{1,0:T(8,128)S(1)} %concatenate.16), channel_id=3, replica_groups=mesh['dp'=8,'sp'=4] {'dp','sp'}, use_global_device_ids=true, to_apply=%region_19.20.clone | all-reduce | flops 9216 | bytes 73728
  416.6 0.6 dynamic-slice_bitcast_fusion.1
  417.2 0.6 dynamic-slice_bitcast_fusion
  417.8 3.7 reshape.375
  421.5 2.4 copy.76
  424.0 1.2 copy.77
  425.2 1.4 convert_element_type.252
  426.6 66.7 %reduce-scatter.5.cloned.1.call-done = bf16[24,2304]{1,0:T(8,128)(2,1)} async-done(((bf16[768,2304]{1,0:T(8,128)(2,1)}), bf16[24,2304]{1,0:T(8,128)(2,1)}) %reduce-scatter.5.cloned.1.call-update) | async-done | bytes 110608 | tf_op jit(solution)/shard_map/reduce_scatter | solution.py:143
  493.4 1.6 convert_element_type.250
  495.0 110.3 %reduce-scatter.9.cloned.1.call-done = bf16[24,3072]{1,0:T(8,128)(2,1)} async-done(((bf16[768,3072]{1,0:T(8,128)(2,1)}), bf16[24,3072]{1,0:T(8,128)(2,1)}) %reduce-scatter.9.cloned.1.call-update) | async-done | bytes 147472 | tf_op jit(solution)/shard_map/reduce_scatter | solution.py:143
  605.2 1.6 convert_element_type.254
  606.9 110.3 %reduce-scatter.11.cloned.1.call-done = bf16[96,768]{1,0:T(8,128)(2,1)} async-done(((bf16[3072,768]{1,0:T(8,128)(2,1)}), bf16[96,768]{1,0:T(8,128)(2,1)}) %reduce-scatter.11.cloned.1.call-update) | async-done | bytes 147472 | tf_op jit(solution)/shard_map/reduce_scatter | solution.py:143
  717.1 1.6 convert_element_type.256
  (115 shorter events, 6.0 us)
Async XLA Ops:
  7.2 56.8 %copy-start = (s32[4,1]{0,1:T(1,128)S(1)}, s32[4,1]{0,1:T(1,128)}, u32[]{:S(2)}) copy-start(s32[4,1]{0,1:T(1,128)} %param.18) | copy-start | bytes 52
  7.2 75.3 %all-gather.6.cloned.1.call-start = ((), (), s32[]{:S(2)}) async-start(), calls=%async_computation.8 | async-start | bytes 3649536 | tf_op jit(solution)/shard_map/all_gather | solution.py:124
  7.9 121.9 %all-gather.8.cloned.1.call-start = ((), (), s32[]{:S(2)}) async-start(), calls=%async_computation.9 | async-start | bytes 1216512 | tf_op jit(solution)/shard_map/all_gather | solution.py:124
  8.7 186.6 %all-gather.10.cloned.1.call-start = ((), (), s32[]{:S(2)}) async-start(), calls=%async_computation.10 | async-start | bytes 4866048 | tf_op jit(solution)/shard_map/all_gather | solution.py:124
  9.4 250.6 %all-gather.12.cloned.1.call-start = ((), (), s32[]{:S(2)}) async-start(), calls=%async_computation.11 | async-start | bytes 4866048 | tf_op jit(solution)/shard_map/all_gather | solution.py:124
  10.0 55.5 %all-to-all-start = ((bf16[4,128,768]{2,1,0:T(8,128)(2,1)}), bf16[4,128,768]{2,1,0:T(8,128)(2,1)S(1)}, u32[]{:S(2)}, u32[]{:S(2)}) async-start(bf16[4,128,768]{2,1,0:T(8,128)(2,1)} %param.16), calls=%async_computation | async-start | bytes 1572864 | tf_op jit(solution)/shard_map/all_to_all | solution.py:128
  65.5 16.6 %copy-start.4 = (bf16[4,128,768]{2,1,0:T(8,128)(2,1)}, bf16[4,128,768]{2,1,0:T(8,128)(2,1)S(1)}, u32[]{:S(2)}) copy-start(bf16[4,128,768]{2,1,0:T(8,128)(2,1)S(1)} %all-to-all-done) | copy-start | bytes 2359300
  65.5 15.4 %all-to-all-start.2 = ((bf16[4,128,768]{2,1,0:T(8,128)(2,1)}), bf16[4,128,768]{2,1,0:T(8,128)(2,1)S(1)}, u32[]{:S(2)}, u32[]{:S(2)}) async-start(bf16[4,128,768]{2,1,0:T(8,128)(2,1)} %param.17), calls=%async_computation.2 | async-start | bytes 1572864 | tf_op jit(solution)/shard_map/all_to_all | solution.py:129
  69.3 356.0 %reduce-scatter.7.cloned.1.call-start = ((), (), s32[]{:S(2)}) async-start(), calls=%async_computation.13 | async-start | bytes 1216512 | tf_op jit(solution)/shard_map/reduce_scatter | solution.py:143
  80.9 6.5 copy-start.7
  82.4 0.9 copy-start.22
  89.0 8.2 %copy-start.24 = (bf16[512,768]{0,1:T(8,128)(2,1)}, bf16[512,768]{0,1:T(8,128)(2,1)S(1)}, u32[]{:S(2)}) copy-start(bf16[512,768]{0,1:T(8,128)(2,1)S(1)} %copy.60) | copy-start | bytes 2359300
  89.3 7.9 %copy-start.12 = (bf16[512,768]{0,1:T(8,128)(2,1)}, bf16[512,768]{0,1:T(8,128)(2,1)S(1)}, u32[]{:S(2)}) copy-start(bf16[512,768]{0,1:T(8,128)(2,1)S(1)} %copy.61) | copy-start | bytes 2359300
  103.6 2.6 copy-start.2
  132.5 139.9 %copy-start.18 = (f32[512,768]{1,0:T(8,128)}, f32[512,768]{1,0:T(8,128)S(1)}, u32[]{:S(2)}) copy-start(f32[512,768]{1,0:T(8,128)S(1)} %get-tuple-element.53) | copy-start | bytes 4718596
  132.9 127.1 %copy-start.21 = (bf16[512,768]{1,0:T(8,128)(2,1)S(1)}, bf16[512,768]{1,0:T(8,128)(2,1)}, u32[]{:S(2)}) copy-start(bf16[512,768]{1,0:T(8,128)(2,1)} %fusion.16) | copy-start | bytes 2359300
  260.0 9.3 %copy-start.27 = (bf16[768,3072]{1,0:T(8,128)(2,1)S(1)}, bf16[768,3072]{1,0:T(8,128)(2,1)}, u32[]{:S(2)}) copy-start(bf16[768,3072]{1,0:T(8,128)(2,1)} %all-gather.10.cloned.1.call-done) | copy-start | bytes 14155780
  269.3 3.1 copy-start.28
  269.3 3.1 copy-start.8
  272.4 1.1 copy-start.16
  275.3 5.5 copy-start.6
  280.8 1.6 copy-start.10
  280.8 1.6 copy-start.17
  282.4 7.7 %copy-start.13 = (bf16[512,768]{0,1:T(8,128)(2,1)S(1)}, bf16[512,768]{0,1:T(8,128)(2,1)}, u32[]{:S(2)}) copy-start(bf16[512,768]{0,1:T(8,128)(2,1)} %copy-done.12) | copy-start | bytes 2359300
  290.0 4.1 copy-start.11
  290.0 203.3 %reduce-scatter.5.cloned.1.call-start = ((), (), s32[]{:S(2)}) async-start(), calls=%async_computation.12 | async-start | bytes 3649536 | tf_op jit(solution)/shard_map/reduce_scatter | solution.py:143
  294.1 7.2 copy-start.14
  294.1 5.2 copy-start.3
  294.1 5.2 copy-start.25
  299.3 2.0 copy-start.20
  299.3 2.9 copy-start.23
  301.3 0.9 copy-start.26
  306.1 1.4 copy-start.19
  306.1 299.1 %reduce-scatter.9.cloned.1.call-start = ((), (), s32[]{:S(2)}) async-start(), calls=%async_computation.14 | async-start | bytes 4866048 | tf_op jit(solution)/shard_map/reduce_scatter | solution.py:143
  314.0 403.2 %reduce-scatter.11.cloned.1.call-start = ((), (), s32[]{:S(2)}) async-start(), calls=%async_computation.15 | async-start | bytes 4866048 | tf_op jit(solution)/shard_map/reduce_scatter | solution.py:143
  334.3 13.9 %copy-start.5 = (bf16[4,128,768]{2,1,0:T(8,128)(2,1)S(1)}, bf16[4,128,768]{2,1,0:T(8,128)(2,1)}, u32[]{:S(2)}) copy-start(bf16[4,128,768]{2,1,0:T(8,128)(2,1)} %copy-done.4) | copy-start | bytes 2359300
  334.3 13.9 %copy-start.15 = (bf16[12,512,64]{1,2,0:T(8,128)(2,1)S(1)}, bf16[12,512,64]{1,2,0:T(8,128)(2,1)}, u32[]{:S(2)}) copy-start(bf16[12,512,64]{1,2,0:T(8,128)(2,1)} %copy-done.14) | copy-start | bytes 2359300
  344.0 16.4 %all-to-all-start.1 = ((bf16[4,2,49152]{2,1,0:T(2,128)(2,1)}), bf16[4,2,49152]{2,1,0:T(2,128)(2,1)}, u32[]{:S(2)}, u32[]{:S(2)}) async-start(bf16[4,2,49152]{2,1,0:T(2,128)(2,1)} %reshape.374), calls=%async_computation.1 | async-start | bytes 1572864 | tf_op jit(solution)/shard_map/all_to_all | solution.py:140
  356.7 7.2 copy-start.9
  360.4 63.6 %all-to-all-start.3 = ((f32[1,512,768]{2,0,1:T(1,128)}), f32[1,512,768]{2,0,1:T(1,128)S(1)}, u32[]{:S(2)}, u32[]{:S(2)}) async-start(f32[1,512,768]{2,0,1:T(1,128)} %copy.70), calls=%async_computation.3 | async-start | bytes 3145728 | tf_op jit(solution)/shard_map/all_to_all | solution.py:141
  421.5 297.3 %copy-start.1 = (s32[4,1]{0,1:T(1,128)S(1)}, s32[4,1]{0,1:T(1,128)}, u32[]{:S(2)}) copy-start(s32[4,1]{0,1:T(1,128)} %param.18) | copy-start | bytes 52
Sparse Core Ops, SparseCore 0:
  10.9 63.2 all-gather.5
  77.1 52.6 all-gather.7
  132.7 62.4 all-gather.9
  198.0 61.9 all-gather.11
  290.2 95.4 reduce-scatter.6
  390.9 102.4 reduce-scatter.4
  498.8 106.3 reduce-scatter.8
  610.7 106.3 reduce-scatter.10

commit v2 on v1

--- a/solution.py
+++ b/solution.py
@@ -1,6 +1,10 @@
+import functools
+
 import jax
 import jax.numpy as jnp
 from jax import lax
+from jax.experimental import pallas as pl
+from jax.experimental.pallas import tpu as pltpu
 from jax.sharding import PartitionSpec as P
 
 HEADS = 12
@@ -13,7 +17,7 @@
 AXES = ("dp", "sp")
 F32 = jnp.float32
 BF16 = jnp.bfloat16
-
+MESH = pl.DeviceIdType.MESH
 
 def dot(a, b, dims):
     return lax.dot_general(a, b, (dims, ((), ())), preferred_element_type=F32)
@@ -147,13 +151,892 @@
     s = [small_out[a:b] for a, b in zip(cuts[:-1], cuts[1:])]
     return (out, d_x, s[0], s[1], big_out[0], s[2], s[3], big_out[1], s[4], s[5], s[6], big_out[2], s[7], big_out[3], s[8])
 
+T, D, FF, HALF = 512, 768, 3072, 384
+ZS = 4
+ZA = 3
+ROWS = 32
+
+
+class Bag:
+    pass
+
+
+def rows_loop(count, step, body):
+    def one(i, carry):
+        body(pl.multiple_of(i * step, step))
+        return carry
+
+    lax.fori_loop(0, count // step, one, 0)
+
+
+def fold8(values):
+    return jnp.sum(values.reshape(values.shape[0] // 8, 8, values.shape[1]), axis=0)
+
+
+def zero_sums(count):
+    return tuple(jnp.zeros((8, D), F32) for _ in range(count))
+
+
+NAMES = (
+    "tok", "cot", "cut", "wq", "wo", "wf", "wp", "small", "out_o", "dx_o", "gq_o", "go_o", "gf_o", "gp_o", "gs_o",
+    "W", "Wp", "Sw", "sq", "so", "sf", "sp_", "ssm", "vec", "G", "Gp", "rA1", "rB1", "pA1", "pB1", "rA2", "rB2",
+    "pA2", "pB2", "rz", "pz", "tot", "ptot", "fr", "pfr", "xb", "cb", "h1c", "qkvb", "attnc", "x1", "h2c", "actc",
+    "slope", "dpre_p", "acc", "dbr", "dbr_p", "dml", "dml_p", "dat", "dqp", "ob", "mask", "lse", "lseT", "gsm", "gs",
+    "gr", "ssem", "rsem", "lsem",
+)
+SEMS = 220
+
+
+def scratch_shapes():
+    v = pltpu.VMEM
+    return [
+        v((8, 2, ZS, 2, 2, 48, HALF), BF16),
+        v((2, ZS, 2, 2, 192, HALF), BF16),
+        v((2, ZS, 2, 2, 16, HALF), BF16),
+        v((24, 3 * D), BF16),
+        v((24, D), BF16),
+        v((24, FF), BF16),
+        v((96, D), BF16),
+        v((16, D), BF16),
+        v((16, D), F32),
+        v((8, ZS, 2, 2, 48, HALF), BF16),
+        v((ZS, 2, 2, 192, HALF), BF16),
+        v((8, ZA, 2, 48, HALF), BF16),
+        v((8, ZS - ZA, 2, 48, HALF), BF16),
+        v((ZA, 2, 192, HALF), BF16),
+        v((ZS - ZA, 2, 192, HALF), BF16),
+        v((8, ZA, 48, HALF), BF16),
+        v((8, ZS - ZA, 48, HALF), BF16),
+        v((ZA, 192, HALF), BF16),
+        v((ZS - ZA, 192, HALF), BF16),
+        v((8, 3, 48, HALF), BF16),
+        v((3, 192, HALF), BF16),
+        v((8, 48, HALF), F32),
+        v((192, HALF), F32),
+        v((8, 24, HALF), F32),
+        v((96, HALF), F32),
+        v((4, 128, D), BF16),
+        v((4, 128, D), BF16),
+        v((2, T, D), BF16),
+        v((6, T, HALF), BF16),
+        v((2, T, D), BF16),
+        v((T, D), F32),
+        v((2, T, D), BF16),
+        v((2, T, FF), BF16),
+        v((T, FF), BF16),
+        v((T, FF // 2), BF16),
+        v((T, D), F32),
+        v((T, D), BF16),
+        v((T, HALF), BF16),
+        v((T, D), BF16),
+        v((T, HALF), BF16),
+        v((T, D), BF16),
+        v((3, T, HALF), BF16),
+        v((T, D), BF16),
+        v((T, T), F32),
+        v((T, 128), F32),
+        v((128, T), F32),
+        v((16, D), F32),
+        v((3, 16, D), F32),
+        v((6, 16, D), F32),
+        pltpu.SemaphoreType.DMA((SEMS,)),
+        pltpu.SemaphoreType.DMA((SEMS,)),
+        pltpu.SemaphoreType.DMA((4,)),
+    ]
+
+
+def mega(*refs):
+    r = Bag()
+    assert len(refs) == len(NAMES), (len(refs), len(NAMES))
+    for name, ref in zip(NAMES, refs):
+        setattr(r, name, ref)
+    dp, sp = lax.axis_index("dp"), lax.axis_index("sp")
+    z, y = dp // 2, lax.rem(dp, 2)
+    x, c = sp // 2, lax.rem(sp, 2)
+    nx, ny, nc = 1 - x, 1 - y, 1 - c
+    partner = {"dp": dp, "sp": x * 2 + nc}
+    xpeer = {"dp": dp, "sp": nx * 2 + c}
+    ypeer = {"dp": z * 2 + ny, "sp": sp}
+    every, low_z, high_z = pl.ds(0, ZS), pl.ds(0, ZA), pl.ds(ZA, ZS - ZA)
+    both = pl.ds(0, 2)
+
+    def zshift(k):
+        return lax.rem(z + k, ZS)
+
+    def zpeer(k):
+        return {"dp": zshift(k) * 2 + y, "sp": sp}
+
+    def speer(k):
+        return lax.rem(sp + k, 4)
+
+    table = {}
+    started = {}
+
+    def slot(key):
+        return table.setdefault(key, len(table))
+
+    def send(key, src, dst, device):
+        i = slot(key)
+        copy = pltpu.make_async_remote_copy(
+            src_ref=src, dst_ref=dst, send_sem=r.ssem.at[i], recv_sem=r.rsem.at[i], device_id=device, device_id_type=MESH
+        )
+        copy.start()
+        started[key] = copy
+        return copy
+
+    def arrive(key, dst):
+        i = slot(key)
+        pltpu.make_async_remote_copy(
+            src_ref=dst, dst_ref=dst, send_sem=r.ssem.at[i], recv_sem=r.rsem.at[i], device_id=partner, device_id_type=MESH
+        ).wait_recv()
+
+    barrier = pltpu.get_barrier_semaphore()
+    peers = [{"dp": dp, "sp": speer(k)} for k in (1, 2, 3)] + [ypeer] + [zpeer(k) for k in (1, 2, 3)]
+    for peer in peers:
+        pl.semaphore_signal(barrier, inc=1, device_id=peer, device_id_type=MESH)
+    pl.semaphore_wait(barrier, len(peers))
+
+    def view(u, h, zs, ys, xs):
+        kind, first, count = u
+        if kind == "s":
+            return r.Sw.at[h, zs, ys, xs]
+        if kind == "p":
+            return r.Wp.at[h, zs, ys, xs, pl.ds(first, count), :]
+        return r.W.at[pl.ds(first, count), h, zs, ys, xs]
+
+    def ag1(u):
+        for k in (1, 2, 3):
+            v = view(u, c, z, y, x)
+            send((u, "z", k), v, v, zpeer(k))
+
+    def ag2(u):
+        for k in (1, 2, 3):
+            arrive((u, "z", k), view(u, c, zshift(ZS - k), y, x))
+        v = view(u, c, low_z, y, x)
+        send((u, "2a"), v, v, xpeer)
+        v = view(u, c, high_z, y, x)
+        send((u, "2b"), v, v, ypeer)
+        v = view(u, c, every, y, x)
+        send((u, "c0"), v, v, partner)
+
+    def ag3(u):
+        arrive((u, "2a"), view(u, c, low_z, y, nx))
+        v = view(u, c, low_z, y, both)
+        send((u, "3a"), v, v, ypeer)
+        arrive((u, "2b"), view(u, c, high_z, ny, x))
+        v = view(u, c, high_z, both, x)
+        send((u, "3b"), v, v, xpeer)
+        v = view(u, c, low_z, y, nx)
+        send((u, "c1"), v, v, partner)
+        v = view(u, c, high_z, ny, x)
+        send((u, "c2"), v, v, partner)
+
+    def ag4(u):
+        v = view(u, c, low_z, ny, both)
+        arrive((u, "3a"), v)
+        send((u, "c3"), v, v, partner)
+        v = view(u, c, high_z, both, nx)
+        arrive((u, "3b"), v)
+        send((u, "c4"), v, v, partner)
+
+    def ag5(u):
+        arrive((u, "c0"), view(u, nc, every, y, x))
+        arrive((u, "c1"), view(u, nc, low_z, y, nx))
+        arrive((u, "c2"), view(u, nc, high_z, ny, x))
+        arrive((u, "c3"), view(u, nc, low_z, ny, both))
+        arrive((u, "c4"), view(u, nc, high_z, both, nx))
+
+    US = ("s", 0, 16)
+    UQ = [("w", i, 1) for i in range(3)]
+    UO = ("w", 3, 1)
+    UF = [("w", 4, 2), ("w", 6, 2)]
+    UP = [("p", 0, 96), ("p", 96, 96)]
+
+    swaps = [("small", r.small, r.ssm), ("wq", r.wq, r.sq), ("wo", r.wo, r.so), ("wf", r.wf, r.sf), ("wp", r.wp, r.sp_)]
+    for key, src, dst in swaps:
+        send(key, src, dst, partner)
+
+    def send_pack(key, src, dst):
+        for k in (1, 2, 3):
+            send((key, k), src.at[speer(k)], dst.at[sp], {"dp": dp, "sp": speer(k)})
+
+    send_pack("tok", r.tok, r.xb)
+    own_tok = pltpu.make_async_copy(r.tok.at[sp], r.xb.at[sp], r.lsem.at[0])
+    own_tok.start()
+    own_cot = pltpu.make_async_copy(r.cot.at[sp], r.cb.at[sp], r.lsem.at[1])
+    own_cot.start()
+    first_core = c == 0
+
+    def pair_rows(own, other, col, width):
+        a = own[:, pl.ds(pl.multiple_of(col, 128), width)].astype(F32)
+        b = other[:, pl.ds(pl.multiple_of(col, 128), width)].astype(F32)
+        return jnp.concatenate([jnp.where(first_core, a, b), jnp.where(first_core, b, a)], axis=0).astype(BF16)
+
+    arrive("small", r.ssm)
+    cols = pl.ds(pl.multiple_of(c * HALF, 128), HALF)
+    r.Sw[c, z, y, x] = (r.small[:, cols].astype(F32) + r.ssm[:, cols].astype(F32)).astype(BF16)
+    ag1(US)
+    arrive("wq", r.sq)
+    for i in range(3):
+        for j in range(3):
+            r.W[i, c, z, y, x, :, pl.ds(128 * j, 128)] = pair_rows(r.wq, r.sq, j * D + 128 * (3 * c + i), 128)
+        ag1(UQ[i])
+    arrive("wo", r.so)
+    r.W[3, c, z, y, x] = pair_rows(r.wo, r.so, c * HALF, HALF)
+    ag1(UO)
+    arrive("wf", r.sf)
+    for i in range(4):
+        r.W[4 + i, c, z, y, x] = pair_rows(r.wf, r.sf, c * (FF // 2) + i * HALF, HALF)
+    ag1(UF[0])
+    ag1(UF[1])
+    arrive("wp", r.sp_)
+    r.Wp[c, z, y, x, pl.ds(pl.multiple_of(96 * c, 32), 96), :] = r.wp[:, cols]
+    r.Wp[c, z, y, x, pl.ds(pl.multiple_of(96 * nc, 32), 96), :] = r.sp_[:, cols]
+    ag1(UP[0])
+    ag1(UP[1])
+
+    def dot(a, b, ca, cb):
+        return lax.dot_general(a, b, (((ca,), (cb,)), ((), ())), preferred_element_type=F32)
+
+    def wide(item):
+        return jnp.concatenate([r.W[item, h].reshape(D, HALF) for h in (0, 1)], axis=1)
+
+    def tile_x(buf, row):
+        return buf[row // 128, pl.ds(pl.multiple_of(lax.rem(row, 128), ROWS), ROWS), :].astype(F32)
+
+    def vrow(i):
+        return r.vec[i : i + 1, :]
+
+    def stats(v):
+        center = jnp.mean(v, axis=-1, keepdims=True)
+        centred = v - center
+        inverse = lax.rsqrt(jnp.mean(centred * centred, axis=-1, keepdims=True) + EPSILON)
+        return centred * inverse, inverse
+
+    def norm_back(xhat, inverse, grad):
+        return inverse * (grad - jnp.mean(grad, axis=-1, keepdims=True) - xhat * jnp.mean(grad * xhat, axis=-1, keepdims=True))
+
+    def build_mask():
+        def body(row):
+            q = lax.broadcasted_iota(jnp.int32, (ROWS, T), 0) + row
+            k = lax.broadcasted_iota(jnp.int32, (ROWS, T), 1)
+            cut = r.cut[sp, 0]
+            ok = (k <= q) & ((k >= cut) == (q >= cut))
+            r.mask[pl.ds(row, ROWS), :] = jnp.where(ok, 0.0, NEGATIVE)
+
+        rows_loop(T, ROWS, body)
+
+    def build_mask_t():
+        def body(row):
+            k = lax.broadcasted_iota(jnp.int32, (ROWS, T), 0) + row
+            q = lax.broadcasted_iota(jnp.int32, (ROWS, T), 1)
+            cut = r.cut[sp, 0]
+            ok = (k <= q) & ((k >= cut) == (q >= cut))
+            r.mask[pl.ds(row, ROWS), :] = jnp.where(ok, 0.0, NEGATIVE)
+
+        rows_loop(T, ROWS, body)
+
+    def small_vectors():
+        for h in (0, 1):
+            total = jnp.zeros((16, HALF), F32)
+            for zz in range(ZS):
+                for yy in (0, 1):
+                    for xx in (0, 1):
+                        total = total + r.Sw[h, zz, yy, xx].astype(F32)
+            r.vec[:, pl.ds(h * HALF, HALF)] = total
+
+    def norm_one():
+        def body(row):
+            xhat, _ = stats(tile_x(r.xb, row))
+            r.h1c[0, pl.ds(row, ROWS), :] = (xhat * vrow(0) + vrow(1)).astype(BF16)
+
+        rows_loop(T, ROWS, body)
+
+    def qkv_item(i):
+        res = dot(r.h1c[0], wide(i), 1, 0)
+        for h in (0, 1):
+            p = 3 * h + i
+            q = res[:, h * HALF : h * HALF + 128] + r.vec[2:3, 128 * p : 128 * p + 128]
+            k = res[:, h * HALF + 128 : h * HALF + 256]
+            v = res[:, h * HALF + 256 : h * HALF + 384] + r.vec[3:4, 128 * p : 128 * p + 128]
+            r.qkvb[p, :, 0:128] = (q.astype(BF16).astype(F32) * (HEAD**-0.5)).astype(BF16)
+            r.qkvb[p, :, 128:256] = k.astype(BF16)
+            r.qkvb[p, :, 256:384] = v.astype(BF16)
+
+    QB = 256
+
+    def lane_masks(rows):
+        lane = lax.broadcasted_iota(jnp.int32, (rows, 128), 1)
+        return lane
+
+    def attend_pair(p):
+        lane = lane_masks(QB)
+
+        def block(qb):
+            keys = QB * (qb + 1)
+            rows = pl.ds(QB * qb, QB)
+            q2 = r.qkvb[p, rows, 0:128]
+            k2 = r.qkvb[p, 0:keys, 128:256]
+            v2 = r.qkvb[p, 0:keys, 256:384]
+            outs = []
+            for hh in (0, 1):
+                mine = (lane < HEAD) if hh == 0 else (lane >= HEAD)
+                qm = jnp.where(mine, q2, jnp.zeros_like(q2))
+                s = dot(qm, k2, 1, 1) + r.mask[rows, 0:keys]
+                top = jnp.max(s, axis=1, keepdims=True)
+                e = jnp.exp(s - top)
+                total = jnp.sum(e, axis=1, keepdims=True)
+                outs.append(dot(e.astype(BF16), v2, 1, 0) / total)
+                r.lse[rows, :] = jnp.where(lane == 2 * p + hh, top + jnp.log(total), r.lse[rows, :])
+            both_heads = jnp.where(lane < HEAD, outs[0], outs[1]).astype(BF16)
+            r.attnc[0, rows, pl.ds(pl.multiple_of(128 * p, 128), 128)] = both_heads
+
+        for qb in range(T // QB):
+            block(qb)
+
+    def out_proj():
+        r.acc[...] = dot(r.attnc[0], wide(3), 1, 0)
+
+        def body(row):
+            v = tile_x(r.xb, row) + BRANCH * (r.acc[pl.ds(row, ROWS), :] + vrow(4))
+            r.x1[pl.ds(row, ROWS), :] = v
+            xhat, _ = stats(v)
+            r.h2c[0, pl.ds(row, ROWS), :] = (xhat * vrow(5) + vrow(6)).astype(BF16)
+
+        rows_loop(T, ROWS, body)
+
+    def up_item(i):
+        r.acc[...] = dot(r.h2c[0], wide(4 + i), 1, 0)
+        for h in (0, 1):
+            col = pl.multiple_of(h * (FF // 2) + i * HALF, 128)
+            at = h * 2 + i // 2
+            bias = r.vec[pl.ds(8 + at, 1), pl.ds(pl.multiple_of(lax.rem(i, 2) * HALF, 128), HALF)]
+
+            def body(row):
+                pre = r.acc[pl.ds(row, ROWS), pl.ds(h * HALF, HALF)] + bias
+                square = pre * pre
+                t = jnp.tanh(pre * (GELU_A + (GELU_A * GELU_B) * square))
+                half_one = 0.5 * (1.0 + t)
+                r.actc[0, pl.ds(row, ROWS), pl.ds(col, HALF)] = (pre * half_one).astype(BF16)
+                inner = GELU_A + (3.0 * GELU_A * GELU_B) * square
+                r.slope[pl.ds(row, ROWS), pl.ds(col, HALF)] = (
+                    half_one + (0.5 * pre) * (1.0 - t * t) * inner
+                ).astype(BF16)
+
+            rows_loop(T, ROWS, body)
+
+    def wp_group(g):
+        return jnp.concatenate([r.Wp[h, g].reshape(D, HALF) for h in (0, 1)], axis=1)
+
+    def group_cols(g):
+        return pl.ds(pl.multiple_of(g * D, 128), D)
+
+    def mlp_grad_rows():
+        def body(row, sums):
+            d = (tile_x(r.cb, row) * BRANCH).astype(BF16)
+            r.dml[pl.ds(row, ROWS), :] = d
+            return sums + fold8(d.astype(F32))
+
+        sums = lax.fori_loop(0, T // ROWS, lambda i, s: body(pl.multiple_of(i * ROWS, ROWS), s), jnp.zeros((8, D), F32))
+        r.gsm[7:8, :] = jnp.sum(sums, axis=0, keepdims=True)
+
+    def layer_out():
+        r.acc[...] = dot(r.actc[0, :, 0:D], wp_group(0), 1, 0)
+
+        def group(g, carry):
+            r.acc[...] += dot(r.actc[0, :, group_cols(g)], wp_group(g), 1, 0)
+            return carry
+
+        lax.fori_loop(1, 4, group, 0)
+
+        def body(row):
+            v = r.x1[pl.ds(row, ROWS), :] + BRANCH * (r.acc[pl.ds(row, ROWS), :] + vrow(7))
+            r.ob[pl.ds(row, ROWS), :] = v.astype(BF16)
+
+        rows_loop(T, ROWS, body)
+
+    def send_rows(key, dst, sem):
+        for k in (1, 2, 3):
+            src = r.ob.at[pl.ds(pl.multiple_of(128 * speer(k), 128), 128), :]
+            send((key, k), src, dst.at[sp], {"dp": dp, "sp": speer(k)})
+        own = pltpu.make_async_copy(r.ob.at[pl.ds(pl.multiple_of(128 * sp, 128), 128), :], dst.at[sp], r.lsem.at[sem])
+        own.start()
+        return own
+
+    def down_back():
+        def group(g, carry):
+            r.acc[...] = dot(r.dml[...], wp_group(g), 1, 1)
+
+            def body(i, sums):
+                row = pl.multiple_of(i * ROWS, ROWS)
+                here = (pl.ds(row, ROWS), group_cols(g))
+                d = (r.acc[pl.ds(row, ROWS), :] * r.slope[here].astype(F32)).astype(BF16)
+                r.slope[here] = d
+                return sums + fold8(d.astype(F32))
+
+            sums = lax.fori_loop(0, T // ROWS, body, jnp.zeros((8, D), F32))
+            r.gsm[pl.ds(8 + g, 1), :] = jnp.sum(sums, axis=0, keepdims=True)
+            return carry
+
+        lax.fori_loop(0, 4, group, 0)
+
+    def up_back():
+        def one(i):
+            lhs = jnp.concatenate(
+                [r.slope[:, pl.ds(pl.multiple_of(h * (FF // 2) + i * HALF, 128), HALF)] for h in (0, 1)], axis=1
+            )
+            return dot(lhs, wide(4 + i), 1, 1)
+
+        r.acc[...] = one(0)
+
+        def item(i, carry):
+            r.acc[...] += one(i)
+            return carry
+
+        lax.fori_loop(1, 4, item, 0)
+
+    def half_cols(ref, core):
+        return ref.at[:, pl.ds(pl.multiple_of(core * HALF, 128), HALF)]
+
+    def proj_grad():
+        def chunk(f, carry):
+            at = pl.ds(pl.multiple_of(f * HALF, 128), HALF)
+            res = dot(r.actc[0, :, at], half_cols(r.dml, c)[...], 0, 0) + dot(r.actc[1, :, at], r.dml_p[...], 0, 0)
+            r.Gp[f // 2, lax.rem(f, 2)] = res.astype(BF16).reshape(2, 192, HALF)
+            return carry
+
+        lax.fori_loop(0, 8, chunk, 0)
+
+    def up_grad(u):
+        own = r.slope[:, pl.ds(pl.multiple_of(c * (FF // 2) + u * D, 128), D)]
+        res = dot(r.h2c[0], own, 0, 0) + dot(r.h2c[1], r.dpre_p[:, u * D : u * D + D], 0, 0)
+        for k in (0, 1):
+            r.G[4 + 2 * u + k] = res[:, k * HALF : k * HALF + HALF].astype(BF16).reshape(ZS, 2, 2, 48, HALF)
+
+    def norm_two_back():
+        def body(i, sums):
+            row = pl.multiple_of(i * ROWS, ROWS)
+            here = pl.ds(row, ROWS)
+            xhat, inverse = stats(r.x1[here, :])
+            d_h2 = r.acc[here, :]
+            d_x1 = tile_x(r.cb, row) + norm_back(xhat, inverse, d_h2 * vrow(5))
+            r.x1[here, :] = d_x1
+            d_branch = (d_x1 * BRANCH).astype(BF16)
+            r.dbr[here, :] = d_branch
+            return (
+                sums[0] + fold8(d_h2 * xhat),
+                sums[1] + fold8(d_h2),
+                sums[2] + fold8(d_branch.astype(F32)),
+            )
+
+        sums = lax.fori_loop(0, T // ROWS, body, zero_sums(3))
+        for k, at in enumerate((5, 6, 4)):
+            r.gsm[at : at + 1, :] = jnp.sum(sums[k], axis=0, keepdims=True)
+
+    def out_back():
+        r.dat[...] = dot(r.dbr[...], wide(3), 1, 1).astype(BF16)
+
+    def out_grad():
+        res = dot(r.attnc[0], half_cols(r.dbr, c)[...], 0, 0) + dot(r.attnc[1], r.dbr_p[...], 0, 0)
+        r.G[3] = res.astype(BF16).reshape(ZS, 2, 2, 48, HALF)
+
+    def flip_lse():
+        r.lseT[...] = jnp.transpose(r.lse[...])
+
+    def attend_back_pair(p):
+        KB = 256
+        cols = pl.ds(pl.multiple_of(128 * p, 128), 128)
+        lane = lane_masks(KB)
+        da = r.dat[:, cols]
+        prod = da.astype(F32) * r.attnc[0, :, cols].astype(F32)
+        pick = jnp.where(
+            (lax.broadcasted_iota(jnp.int32, (8, 128), 1) // HEAD) == lax.broadcasted_iota(jnp.int32, (8, 128), 0), 1.0, 0.0
+        ).astype(F32)
+        delta = lax.dot_general(
+            pick, prod, (((1,), (1,)), ((), ())), preferred_element_type=F32, precision=lax.Precision.HIGHEST
+        )
+        q2 = r.qkvb[p, :, 0:128]
+        dq_parts = [None, None]
+        results = []
+        for kb in (0, 1):
+            first = KB * kb
+            keys = pl.ds(first, KB)
+            k2 = r.qkvb[p, keys, 128:256]
+            v2 = r.qkvb[p, keys, 256:384]
+            dks, dvs, dqs = [], [], []
+            for hh in (0, 1):
+                mine = (lane < HEAD) if hh == 0 else (lane >= HEAD)
+                km = jnp.where(mine, k2, jnp.zeros_like(k2))
+                vm = jnp.where(mine, v2, jnp.zeros_like(v2))
+                logs = r.lseT[pl.ds(2 * p + hh, 1), :]
+                s = dot(km, q2[first:], 1, 1) + r.mask[keys, first:]
+                prob = jnp.exp(s - logs[:, first:])
+                dprob = dot(vm, da[first:], 1, 1)
+                ds = (prob * (dprob - delta[hh : hh + 1, first:])).astype(BF16)
+                dvs.append(dot(prob.astype(BF16), da[first:], 1, 0))
+                dks.append(dot(ds, q2[first:], 1, 0))
+                dqs.append(dot(ds, km, 0, 0))
+            dk = jnp.where(lane < HEAD, dks[0], dks[1]).astype(BF16)
+            dv = jnp.where(lane < HEAD, dvs[0], dvs[1]).astype(BF16)
+            results.append((dk, dv, dqs[0] + dqs[1]))
+        (dk0, dv0, dq0), (dk1, dv1, dq1) = results
+        scale = HEAD**-0.5
+        dq_low = (dq0[:KB] * scale).astype(BF16)
+        dq_high = ((dq0[KB:] + dq1) * scale).astype(BF16)
+        r.qkvb[p, 0:KB, 0:128] = dq_low
+        r.qkvb[p, KB:T, 0:128] = dq_high
+        r.qkvb[p, 0:KB, 128:256] = dk0
+        r.qkvb[p, KB:T, 128:256] = dk1
+        r.qkvb[p, 0:KB, 256:384] = dv0
+        r.qkvb[p, KB:T, 256:384] = dv1
+        at = pl.ds(pl.multiple_of(128 * p, 128), 128)
+        r.gsm[2:3, at] = jnp.sum(dq_low.astype(F32), axis=0, keepdims=True) + jnp.sum(
+            dq_high.astype(F32), axis=0, keepdims=True
+        )
+        r.gsm[3:4, at] = jnp.sum(dv0.astype(F32), axis=0, keepdims=True) + jnp.sum(
+            dv1.astype(F32), axis=0, keepdims=True
+        )
+
+    def qkv_grad(i):
+        res = dot(r.h1c[0], r.qkvb[3 * c + i], 0, 0) + dot(r.h1c[1], r.dqp[i], 0, 0)
+        r.G[i] = res.astype(BF16).reshape(ZS, 2, 2, 48, HALF)
+
+    def qkv_back():
+        def one(i):
+            lhs = jnp.concatenate([r.qkvb[i], r.qkvb[3 + i]], axis=1)
+            return dot(lhs, wide(i), 1, 1)
+
+        r.acc[...] = one(0)
+
+        def item(i, carry):
+            r.acc[...] += one(i)
+            return carry
+
+        lax.fori_loop(1, 3, item, 0)
+
+    def norm_one_back():
+        def body(i, sums):
+            row = pl.multiple_of(i * ROWS, ROWS)
+            here = pl.ds(row, ROWS)
+            xhat, inverse = stats(tile_x(r.xb, row))
+            d_h1 = r.acc[here, :]
+            d_x = r.x1[here, :] + norm_back(xhat, inverse, d_h1 * vrow(0))
+            r.ob[here, :] = d_x.astype(BF16)
+            return (sums[0] + fold8(d_h1 * xhat), sums[1] + fold8(d_h1))
+
+        sums = lax.fori_loop(0, T // ROWS, body, zero_sums(2))
+        for k, at in enumerate((0, 1)):
+            r.gsm[at : at + 1, :] = jnp.sum(sums[k], axis=0, keepdims=True)
+
+    def gview(u, zs, ys, xs):
+        kind, first, count = u
+        if kind == "p":
+            return r.Gp.at[zs, ys, xs, pl.ds(first, count), :]
+        return r.G.at[pl.ds(first, count), zs, ys, xs]
+
+    def rview(u, plain, proj):
+        kind, first, count = u
+        if kind == "p":
+            at = (pl.ds(0, proj.shape[0]),) + (pl.ds(0, 2),) * (len(proj.shape) - 3) + (pl.ds(first, count), slice(None))
+            return proj.at[at]
+        return plain.at[pl.ds(first, count)]
+
+    def add_into(dst, extra):
+        dst[...] = (dst[...].astype(F32) + extra[...].astype(F32)).astype(BF16)
+
+    def rs1(u):
+        send((u, "r1a"), gview(u, low_z, ny, both), rview(u, r.rA1, r.pA1), ypeer)
+        send((u, "r1b"), gview(u, high_z, both, nx), rview(u, r.rB1, r.pB1), xpeer)
+
+    def rs2(u):
+        va, vb = rview(u, r.rA1, r.pA1), rview(u, r.rB1, r.pB1)
+        arrive((u, "r1a"), va)
+        add_into(gview(u, low_z, y, both), va)
+        send((u, "r2a"), gview(u, low_z, y, nx), rview(u, r.rA2, r.pA2), xpeer)
+        arrive((u, "r1b"), vb)
+        add_into(gview(u, high_z, both, x), vb)
+        send((u, "r2b"), gview(u, high_z, ny, x), rview(u, r.rB2, r.pB2), ypeer)
+
+    def zslot(u, k):
+        kind, first, count = u
+        if kind == "p":
+            return r.pz.at[k - 1, pl.ds(first, count), :]
+        return r.rz.at[pl.ds(first, count), k - 1]
+
+    def rs3(u):
+        va, vb = rview(u, r.rA2, r.pA2), rview(u, r.rB2, r.pB2)
+        arrive((u, "r2a"), va)
+        add_into(gview(u, low_z, y, x), va)
+        arrive((u, "r2b"), vb)
+        add_into(gview(u, high_z, y, x), vb)
+        for k in (1, 2, 3):
+            send((u, "rz", k), gview(u, zshift(k), y, x), zslot(u, k), zpeer(k))
+
+    def rs4(u):
+        kind, first, count = u
+        for k in (1, 2, 3):
+            arrive((u, "rz", k), zslot(u, k))
+        total = gview(u, z, y, x)[...].astype(F32)
+        for k in (1, 2, 3):
+            total = total + zslot(u, k)[...].astype(F32)
+        if kind == "p":
+            r.ptot[pl.ds(first, count), :] = total
+        else:
+            r.tot[pl.ds(first, count)] = total
+            give = pl.ds(pl.multiple_of(24 * nc, 8), 24)
+            send((u, "fin"), r.tot.at[pl.ds(first, count), give, :], r.fr.at[pl.ds(first, count)], partner)
+
+    def rs5(u):
+        kind, first, count = u
+        arrive((u, "fin"), r.fr.at[pl.ds(first, count)])
+        keep = pl.ds(pl.multiple_of(24 * c, 8), 24)
+        for it in range(first, first + count):
+            for core, part in ((c, r.tot[it, keep, :]), (nc, r.fr[it])):
+                if it < 3:
+                    for j in range(3):
+                        at = pl.multiple_of(j * D + 128 * (3 * core + it), 128)
+                        r.gq_o[:, pl.ds(at, 128)] = part[:, 128 * j : 128 * j + 128]
+                elif it == 3:
+                    r.go_o[:, pl.ds(pl.multiple_of(core * HALF, 128), HALF)] = part
+                else:
+                    at = pl.multiple_of(core * (FF // 2) + (it - 4) * HALF, 128)
+                    r.gf_o[:, pl.ds(at, HALF)] = part
+
+    def rs_proj_send():
+        give = pl.ds(pl.multiple_of(96 * nc, 32), 96)
+        send("pfin", r.ptot.at[give, :], r.pfr, partner)
+
+    def rs_proj_done():
+        arrive("pfin", r.pfr)
+        keep = pl.ds(pl.multiple_of(96 * c, 32), 96)
+        r.gp_o[:, pl.ds(pl.multiple_of(c * HALF, 128), HALF)] = r.ptot[keep, :]
+        r.gp_o[:, pl.ds(pl.multiple_of(nc * HALF, 128), HALF)] = r.pfr[...]
+
+    def small_send(key, src, at, peer):
+        send(("small", key), src, r.gr.at[at], peer)
+
+    def small_add(keys, first, into):
+        total = r.gsm[...] if into is None else r.gs[into]
+        for n, key in enumerate(keys):
+            arrive(("small", key), r.gr.at[first + n])
+            total = total + r.gr[first + n]
+        return total
+
+    ag2(US)
+    ag2(UQ[0])
+    build_mask()
+    ag3(US)
+    ag2(UQ[1])
+    ag3(UQ[0])
+    ag4(US)
+    ag5(US)
+    small_vectors()
+    for k in (1, 2, 3):
+        arrive(("tok", k), r.xb.at[lax.rem(sp + 4 - k, 4)])
+    own_tok.wait()
+    norm_one()
+    send("h1", r.h1c.at[0], r.h1c.at[1], partner)
+    ag2(UQ[2])
+    ag3(UQ[1])
+    ag4(UQ[0])
+    ag2(UO)
+    ag3(UQ[2])
+    ag4(UQ[1])
+    ag5(UQ[0])
+
+    def pairs(body, i):
+        def one(h, carry):
+            body(3 * h + i)
+            return carry
+
+        lax.fori_loop(0, 2, one, 0)
+
+    qkv_item(0)
+    pairs(attend_pair, 0)
+    ag2(UF[0])
+    ag3(UO)
+    ag4(UQ[2])
+    ag5(UQ[1])
+    qkv_item(1)
+    pairs(attend_pair, 1)
+    ag2(UF[1])
+    ag3(UF[0])
+    ag4(UO)
+    ag5(UQ[2])
+    send_pack("cot", r.cot, r.cb)
+    qkv_item(2)
+    pairs(attend_pair, 2)
+    send("attn", r.attnc.at[0], r.attnc.at[1], partner)
+    ag2(UP[0])
+    ag3(UF[1])
+    ag4(UF[0])
+    ag5(UO)
+    out_proj()
+    send("h2", r.h2c.at[0], r.h2c.at[1], partner)
+    flip_lse()
+    build_mask_t()
+    ag2(UP[1])
+    ag3(UP[0])
+    ag4(UF[1])
+    ag5(UF[0])
+    for k in (1, 2, 3):
+        arrive(("cot", k), r.cb.at[lax.rem(sp + 4 - k, 4)])
+    own_cot.wait()
+    mlp_grad_rows()
+    send("dml", half_cols(r.dml, nc), r.dml_p, partner)
+
+    def up_two(first):
+        def one(i, carry):
+            up_item(i)
+            return carry
+
+        lax.fori_loop(first, first + 2, one, 0)
+
+    up_two(0)
+    ag3(UP[1])
+    ag4(UP[0])
+    ag5(UF[1])
+    up_two(2)
+    send("act", r.actc.at[0], r.actc.at[1], partner)
+    ag4(UP[1])
+    arrive("dml", r.dml_p)
+    arrive("act", r.actc.at[1])
+    proj_grad()
+    rs1(UP[0])
+    rs1(UP[1])
+    ag5(UP[0])
+    ag5(UP[1])
+    layer_out()
+    own_out = send_rows("out", r.out_o, 2)
+    down_back()
+    send("dpre", r.slope.at[:, pl.ds(pl.multiple_of(nc * (FF // 2), 128), FF // 2)], r.dpre_p, partner)
+    rs2(UP[0])
+    up_back()
+    rs2(UP[1])
+    rs3(UP[0])
+    arrive("h2", r.h2c.at[1])
+    arrive("dpre", r.dpre_p)
+    up_grad(0)
+    rs1(UF[0])
+    rs3(UP[1])
+    up_grad(1)
+    rs1(UF[1])
+    norm_two_back()
+    send("dbr", half_cols(r.dbr, nc), r.dbr_p, partner)
+    rs2(UF[0])
+    rs4(UP[0])
+    out_back()
+    rs2(UF[1])
+    rs3(UF[0])
+    rs4(UP[1])
+    rs_proj_send()
+    arrive("attn", r.attnc.at[1])
+    arrive("dbr", r.dbr_p)
+    out_grad()
+    rs1(UO)
+    arrive("h1", r.h1c.at[1])
+
+    def give_qkv(i):
+        send(("dq", i), r.qkvb.at[3 * nc + i], r.dqp.at[i], partner)
+
+    pairs(attend_back_pair, 0)
+    give_qkv(0)
+    rs3(UF[1])
+    rs2(UO)
+    rs4(UF[0])
+    pairs(attend_back_pair, 1)
+    give_qkv(1)
+    arrive(("dq", 0), r.dqp.at[0])
+    qkv_grad(0)
+    rs1(UQ[0])
+    rs3(UO)
+    rs4(UF[1])
+    pairs(attend_back_pair, 2)
+    give_qkv(2)
+    arrive(("dq", 1), r.dqp.at[1])
+    qkv_grad(1)
+    rs1(UQ[1])
+    rs2(UQ[0])
+    arrive(("dq", 2), r.dqp.at[2])
+    qkv_grad(2)
+    rs1(UQ[2])
+    rs2(UQ[1])
+    rs3(UQ[0])
+    rs4(UO)
+    qkv_back()
+    rs2(UQ[2])
+    rs3(UQ[1])
+    own_out.wait()
+    for k in (1, 2, 3):
+        started.pop(("out", k)).wait_send()
+    norm_one_back()
+    own_dx = send_rows("dx", r.dx_o, 3)
+    r.gsm[12:16, :] = jnp.zeros((4, D), F32)
+    small_send("core", r.gsm, 0, partner)
+    rs3(UQ[2])
+    rs4(UQ[0])
+    r.gs[0] = small_add(["core"], 0, None)
+    small_send("x", r.gs.at[0], 1, xpeer)
+    rs5(UF[0])
+    rs5(UF[1])
+    r.gs[1] = small_add(["x"], 1, 0)
+    small_send("y", r.gs.at[1], 2, ypeer)
+    rs4(UQ[1])
+    rs5(UO)
+    rs_proj_done()
+    r.gs[2] = small_add(["y"], 2, 1)
+    for k in (1, 2, 3):
+        small_send(("z", k), r.gs.at[2], 2 + k, zpeer(k))
+    rs4(UQ[2])
+    rs5(UQ[0])
+    rs5(UQ[1])
+    r.gs_o[...] = small_add([("z", 1), ("z", 2), ("z", 3)], 3, 2)
+    rs5(UQ[2])
+    for name, dst in (("out", r.out_o), ("dx", r.dx_o)):
+        for k in (1, 2, 3):
+            arrive((name, k), dst.at[lax.rem(sp + 4 - k, 4)])
+    own_dx.wait()
+    for copy in started.values():
+        copy.wait_send()
+    assert len(table) <= SEMS, len(table)
+
+
+def fused(tokens, cotangent, seq_cut, g1, o1, w_qkv, bq, bv, w_out, bo, g2, o2, w_fc, bf, w_proj, bp):
+    device = lax.axis_index("dp") * 4 + lax.axis_index("sp")
+    small = jnp.zeros((16, D), BF16)
+    small = lax.dynamic_update_slice(small, jnp.stack([g1, o1, bq, bv, bo, g2, o2, bp]), (0, 24 * device))
+    small = lax.dynamic_update_slice(small, bf[None], (8 + device // 8, 96 * (device % 8)))
+    vmem = pl.BlockSpec(memory_space=pltpu.VMEM)
+    anywhere = pl.BlockSpec(memory_space=pl.ANY)
+    s = jax.ShapeDtypeStruct
+    out, d_x, gq, go, gf, gp, gs = pl.pallas_call(
+        mega,
+        out_shape=(
+            s((4, 128, D), BF16),
+            s((4, 128, D), BF16),
+            s((24, 3 * D), F32),
+            s((24, D), F32),
+            s((24, FF), F32),
+            s((96, D), F32),
+            s((16, D), F32),
+        ),
+        in_specs=[anywhere, anywhere, pl.BlockSpec(memory_space=pltpu.SMEM)] + [vmem] * 5,
+        out_specs=(anywhere, anywhere) + (vmem,) * 5,
+        scratch_shapes=scratch_shapes(),
+        compiler_params=pltpu.CompilerParams(collective_id=0, has_side_effects=True, vmem_limit_bytes=67043328),
+    )(tokens, cotangent, seq_cut, w_qkv, w_out, w_fc, w_proj, small)
+    rows = lax.dynamic_slice(gs, (0, 24 * device), (8, 24))
+    g_bf = lax.dynamic_slice(gs, (8 + device // 8, 96 * (device % 8)), (1, 96))[0]
+    return (out, d_x.astype(F32), rows[0], rows[1], gq, rows[2], rows[3], go, rows[4], rows[5], rows[6], gf, g_bf, gp, rows[7])
+
 
 def solution(mesh):
     row = P(AXES, None)
     vec = P(AXES)
     act = P(None, AXES, None)
+    body = fused if dict(mesh.shape) == {"dp": 8, "sp": 4} else local
     return jax.shard_map(
-        local,
+        body,
         mesh=mesh,
         in_specs=(act, act, P(None, "dp"), vec, vec, row, vec, vec, row, vec, vec, vec, row, vec, row, vec),
         out_specs=(act, act, vec, vec, row, vec, vec, row, vec, vec, vec, row, vec, row, vec),

time: 732 us -> 217 us (0.30)
  waiting for transfers between devices: 445 us -> 0 us
  Pallas kernels: 0 us -> 200 us
  matrix products: 93.9 us -> 0 us
  blocking collectives: 92.2 us -> 0 us
  other arithmetic: 28.7 us -> 2.45 us
  local copies, waits for them, and re-layouts: 35.2 us -> 12.9 us
  starting transfers between devices: 16.2 us -> 0 us
  between operations: 15 us -> 0.71 us
    reduce_scatter x4 -> x0, waiting for transfers between devices: 287 us -> none  [local(): lax.psum_scatter(g.astype(BF16), AXES, scatter_dimension=0, tiled=True)]
    pallas_call x0 -> x1, Pallas kernels: none -> 200 us  [fused(): pl.pallas_call(mega, out_shape=(s((4, 128, D), BF16), s((4, 128, D), BF16...]
    all_gather x4 -> x0, waiting for transfers between devices: 140 us -> none  [local(): lax.all_gather(w, AXES, axis=0, tiled=True)]
    unnamed x2 -> x0, blocking collectives: 92.2 us -> none
    dot_general x17 -> x0, matrix products: 86 us -> none  [the longest x12 63.6 us: dot(): return lax.dot_general(a, b, (dims, ((), ())), preferred_element_type=F32)]
    all_to_all x4 -> x0, starting transfers between devices: 15.8 us -> none  [the longest x1 4.25 us: local(): x16 = lax.all_to_all(tokens, 'sp', split_axis=0, concat_axis=1, tiled=True)]
    all_to_all x4 -> x0, waiting for transfers between devices: 14.7 us -> none  [the longest x1 11 us: local(): lax.all_to_all(cotangent, 'sp', split_axis=0, concat_axis=1, tiled=True)]
    convert_element_type x9 -> x1, other arithmetic: 14.4 us -> 2.45 us  [fused(): d_x.astype(F32)]
  transfers between devices with their start and end apart: 12 -> 0, of which waited for: 8 -> 0; matrix products, arithmetic and copies ran while one was open for 17% -> 0% of each run, Pallas kernels for 0% -> 0%
where the time goes in v2:
time: 217 us; the launch traced here: 216 us
  Pallas kernels  200 us (92%)
  local copies, waits for them, and re-layouts  12.9 us (6%)
  other arithmetic  2.45 us (1%)
    pallas_call x1, Pallas kernels, fused(): pl.pallas_call(mega, out_shape=(s((4, 128, D), BF16), s((4, 128, D), BF16...  200 us
    unnamed x16, local copies, waits for them, and re-layouts  4.96 us

profile of v2, /device:TPU:0, one launch (start us, length us, event | category | flops | bytes accessed | tf_op | source)
XLA Modules:
  0.0 216.2 jit_solution(7157710820588370721)
XLA Ops:
  0.7 1.3 copy.31.refs_2_
  2.0 0.8 stack.35
  2.8 0.6 broadcast_in_dim.6
  3.4 2.5 %dynamic_update_slice.6 = bf16[16,768]{1,0:T(8,128)(2,1)} dynamic-update-slice(bf16[16,768]{1,0:T(8,128)(2,1)} %broadcast_in_dim.6, bf16[8,24]{1,0:T(8,128)(2,1)S(1)} %stack.35, s32[]{:T(128)} %constant.39.clone.1, s32[]{:T(128)S(6)} %select_n.26) | dynamic-update-slice | bytes 772 | tf_op jit(solution)/shard_map/dynamic_update_slice | solution.py:1007
  5.9 1.3 dynamic_update_slice.7.refs_7_
  7.3 200.2 %shard_map.271 = (bf16[4,128,768]{2,1,0:T(8,128)(2,1)}, bf16[4,128,768]{2,1,0:T(8,128)(2,1)}, f32[24,2304]{1,0:T(8,128)}, f32[24,768]{1,0:T(8,128)}, f32[24,3072...) custom-call(bf16[4,128,768]{2,1,0:T(8,128)(2,1)} %refs_0_.1, bf16[4,128,768]{2,1,0:T(8,128)(2,1)} %refs_1_.1, ...), custom_call_target="tpu_custom_call" | custom-call | tf_op jit(solution)/shard_map/pallas_call | solution.py:1012
  207.5 0.0 copy-start
  207.5 1.4 dynamic-slice_bitcast_fusion
  208.8 0.8 constant_dynamic-slice_fusion
  209.6 0.5 slice_bitcast_fusion
  210.1 0.0 copy-start.3
  210.1 2.5 %convert_element_type.3 = f32[4,128,768]{2,1,0:T(8,128)} convert(bf16[4,128,768]{2,1,0:T(8,128)(2,1)} %get-tuple-element.23) | non-fusion elementwise | flops 393216 | bytes 2359296 | tf_op jit(solution)/shard_map/convert_element_type | solution.py:1030
  212.6 0.0 copy-done
  212.6 0.0 copy-start.4
  212.6 0.0 copy-start.2
  212.6 0.0 copy-start.1
  212.6 0.9 copy.39
  213.5 0.0 copy-done.3
  213.5 0.7 copy.40
  214.2 0.0 copy-done.4
  214.2 0.6 copy.41
  214.8 0.0 copy-done.2
  214.8 0.7 copy.42
  215.5 0.0 copy-done.1
  215.5 0.7 copy.43
Async XLA Ops:
  207.5 5.1 %copy-start = (bf16[4,128,768]{2,1,0:T(8,128)(2,1)S(1)}, bf16[4,128,768]{2,1,0:T(8,128)(2,1)}, u32[]{:S(2)}) copy-start(bf16[4,128,768]{2,1,0:T(8,128)(2,1)} %get-tuple-element.52) | copy-start | bytes 2359300
  210.1 3.4 %copy-start.3 = (f32[24,2304]{1,0:T(8,128)S(1)}, f32[24,2304]{1,0:T(8,128)}, u32[]{:S(2)}) copy-start(f32[24,2304]{1,0:T(8,128)} %get-tuple-element.56) | copy-start | bytes 663556
  212.6 1.6 copy-start.4
  212.6 2.2 %copy-start.2 = (f32[24,3072]{1,0:T(8,128)S(1)}, f32[24,3072]{1,0:T(8,128)}, u32[]{:S(2)}) copy-start(f32[24,3072]{1,0:T(8,128)} %get-tuple-element.63) | copy-start | bytes 884740
  212.6 2.9 %copy-start.1 = (f32[96,768]{1,0:T(8,128)S(1)}, f32[96,768]{1,0:T(8,128)}, u32[]{:S(2)}) copy-start(f32[96,768]{1,0:T(8,128)} %get-tuple-element.65) | copy-start | bytes 884740

commit v3 on v2

--- a/solution.py
+++ b/solution.py
@@ -180,7 +180,7 @@
 NAMES = (
     "tok", "cot", "cut", "wq", "wo", "wf", "wp", "small", "out_o", "dx_o", "gq_o", "go_o", "gf_o", "gp_o", "gs_o",
     "W", "Wp", "Sw", "sq", "so", "sf", "sp_", "ssm", "vec", "G", "Gp", "rA1", "rB1", "pA1", "pB1", "rA2", "rB2",
-    "pA2", "pB2", "rz", "pz", "tot", "ptot", "fr", "pfr", "xb", "cb", "h1c", "qkvb", "attnc", "x1", "h2c", "actc",
+    "pA2", "pB2", "rz", "pz", "zL", "yL", "xL", "tot", "ptot", "fr", "pfr", "xb", "cb", "h1c", "qkvb", "attnc", "x1", "h2c", "actc",
     "slope", "dpre_p", "acc", "dbr", "dbr_p", "dml", "dml_p", "dat", "dqp", "ob", "mask", "lse", "lseT", "gsm", "gs",
     "gr", "ssem", "rsem", "lsem",
 )
@@ -203,14 +203,17 @@
         v((ZS, 2, 2, 192, HALF), BF16),
         v((8, ZA, 2, 48, HALF), BF16),
         v((8, ZS - ZA, 2, 48, HALF), BF16),
-        v((ZA, 2, 192, HALF), BF16),
-        v((ZS - ZA, 2, 192, HALF), BF16),
+        v((ZA, 2, 96, HALF), BF16),
+        v((ZS - ZA, 2, 96, HALF), BF16),
         v((8, ZA, 48, HALF), BF16),
         v((8, ZS - ZA, 48, HALF), BF16),
-        v((ZA, 192, HALF), BF16),
-        v((ZS - ZA, 192, HALF), BF16),
+        v((ZA, 96, HALF), BF16),
+        v((ZS - ZA, 96, HALF), BF16),
         v((8, 3, 48, HALF), BF16),
-        v((3, 192, HALF), BF16),
+        v((3, 96, HALF), BF16),
+        v((3, 2, 2, 96, HALF), BF16),
+        v((2, 96, HALF), BF16),
+        v((96, HALF), BF16),
         v((8, 48, HALF), F32),
         v((192, HALF), F32),
         v((8, 24, HALF), F32),
@@ -300,7 +303,7 @@
         kind, first, count = u
         if kind == "s":
             return r.Sw.at[h, zs, ys, xs]
-        if kind == "p":
+        if kind in "pl":
             return r.Wp.at[h, zs, ys, xs, pl.ds(first, count), :]
         return r.W.at[pl.ds(first, count), h, zs, ys, xs]
 
@@ -319,22 +322,26 @@
         v = view(u, c, every, y, x)
         send((u, "c0"), v, v, partner)
 
-    def ag3(u):
+    def ag3a(u):
         arrive((u, "2a"), view(u, c, low_z, y, nx))
         v = view(u, c, low_z, y, both)
         send((u, "3a"), v, v, ypeer)
+        v = view(u, c, low_z, y, nx)
+        send((u, "c1"), v, v, partner)
+
+    def ag3b(u):
         arrive((u, "2b"), view(u, c, high_z, ny, x))
         v = view(u, c, high_z, both, x)
         send((u, "3b"), v, v, xpeer)
-        v = view(u, c, low_z, y, nx)
-        send((u, "c1"), v, v, partner)
         v = view(u, c, high_z, ny, x)
         send((u, "c2"), v, v, partner)
 
-    def ag4(u):
+    def ag4a(u):
         v = view(u, c, low_z, ny, both)
         arrive((u, "3a"), v)
         send((u, "c3"), v, v, partner)
+
+    def ag4b(u):
         v = view(u, c, high_z, both, nx)
         arrive((u, "3b"), v)
         send((u, "c4"), v, v, partner)
@@ -346,21 +353,48 @@
         arrive((u, "c3"), view(u, nc, low_z, ny, both))
         arrive((u, "c4"), view(u, nc, high_z, both, nx))
 
+    def late1(u):
+        v = view(u, c, z, y, x)
+        send((u, "lx"), v, v, xpeer)
+        send((u, "ly"), v, v, ypeer)
+
+    def late2(u):
+        v = view(u, c, z, y, nx)
+        arrive((u, "lx"), v)
+        send((u, "ld"), v, v, ypeer)
+
+    def late3(u):
+        arrive((u, "ly"), view(u, c, z, ny, x))
+        arrive((u, "ld"), view(u, c, z, ny, nx))
+        v = view(u, c, z, both, both)
+        for k in (1, 2, 3):
+            send((u, "lz", k), v, v, zpeer(k))
+        send((u, "c", 0), v, v, partner)
+
+    def late4(u, k):
+        v = view(u, c, zshift(ZS - k), both, both)
+        arrive((u, "lz", k), v)
+        send((u, "c", k), v, v, partner)
+
+    def late5(u):
+        for k in (0, 1, 2, 3):
+            arrive((u, "c", k), view(u, nc, zshift(ZS - k), both, both))
+
     US = ("s", 0, 16)
     UQ = [("w", i, 1) for i in range(3)]
     UO = ("w", 3, 1)
     UF = [("w", 4, 2), ("w", 6, 2)]
-    UP = [("p", 0, 96), ("p", 96, 96)]
-
-    swaps = [("small", r.small, r.ssm), ("wq", r.wq, r.sq), ("wo", r.wo, r.so), ("wf", r.wf, r.sf), ("wp", r.wp, r.sp_)]
+    UP = ("p", 0, 96)
+    UL = ("l", 96, 96)
+
+    swaps = [("small", r.small, r.ssm), ("wq", r.wq, r.sq), ("wp", r.wp, r.sp_), ("wo", r.wo, r.so), ("wf", r.wf, r.sf)]
     for key, src, dst in swaps:
         send(key, src, dst, partner)
 
     def send_pack(key, src, dst):
-        for k in (1, 2, 3):
+        for k in (2, 1, 3):
             send((key, k), src.at[speer(k)], dst.at[sp], {"dp": dp, "sp": speer(k)})
 
-    send_pack("tok", r.tok, r.xb)
     own_tok = pltpu.make_async_copy(r.tok.at[sp], r.xb.at[sp], r.lsem.at[0])
     own_tok.start()
     own_cot = pltpu.make_async_copy(r.cot.at[sp], r.cb.at[sp], r.lsem.at[1])
@@ -381,6 +415,9 @@
         for j in range(3):
             r.W[i, c, z, y, x, :, pl.ds(128 * j, 128)] = pair_rows(r.wq, r.sq, j * D + 128 * (3 * c + i), 128)
         ag1(UQ[i])
+    arrive("wp", r.sp_)
+    r.Wp[c, z, y, x, pl.ds(pl.multiple_of(96 * c, 32), 96), :] = r.wp[:, cols]
+    r.Wp[c, z, y, x, pl.ds(pl.multiple_of(96 * nc, 32), 96), :] = r.sp_[:, cols]
     arrive("wo", r.so)
     r.W[3, c, z, y, x] = pair_rows(r.wo, r.so, c * HALF, HALF)
     ag1(UO)
@@ -389,11 +426,7 @@
         r.W[4 + i, c, z, y, x] = pair_rows(r.wf, r.sf, c * (FF // 2) + i * HALF, HALF)
     ag1(UF[0])
     ag1(UF[1])
-    arrive("wp", r.sp_)
-    r.Wp[c, z, y, x, pl.ds(pl.multiple_of(96 * c, 32), 96), :] = r.wp[:, cols]
-    r.Wp[c, z, y, x, pl.ds(pl.multiple_of(96 * nc, 32), 96), :] = r.sp_[:, cols]
-    ag1(UP[0])
-    ag1(UP[1])
+    ag1(UP)
 
     def dot(a, b, ca, cb):
         return lax.dot_general(a, b, (((ca,), (cb,)), ((), ())), preferred_element_type=F32)
@@ -598,14 +631,14 @@
     def half_cols(ref, core):
         return ref.at[:, pl.ds(pl.multiple_of(core * HALF, 128), HALF)]
 
-    def proj_grad():
+    def proj_grad(first):
         def chunk(f, carry):
             at = pl.ds(pl.multiple_of(f * HALF, 128), HALF)
             res = dot(r.actc[0, :, at], half_cols(r.dml, c)[...], 0, 0) + dot(r.actc[1, :, at], r.dml_p[...], 0, 0)
             r.Gp[f // 2, lax.rem(f, 2)] = res.astype(BF16).reshape(2, 192, HALF)
             return carry
 
-        lax.fori_loop(0, 8, chunk, 0)
+        lax.fori_loop(first, first + 4, chunk, 0)
 
     def up_grad(u):
         own = r.slope[:, pl.ds(pl.multiple_of(c * (FF // 2) + u * D, 128), D)]
@@ -730,7 +763,7 @@
 
     def gview(u, zs, ys, xs):
         kind, first, count = u
-        if kind == "p":
+        if kind in "pl":
             return r.Gp.at[zs, ys, xs, pl.ds(first, count), :]
         return r.G.at[pl.ds(first, count), zs, ys, xs]
 
@@ -748,11 +781,14 @@
         send((u, "r1a"), gview(u, low_z, ny, both), rview(u, r.rA1, r.pA1), ypeer)
         send((u, "r1b"), gview(u, high_z, both, nx), rview(u, r.rB1, r.pB1), xpeer)
 
-    def rs2(u):
-        va, vb = rview(u, r.rA1, r.pA1), rview(u, r.rB1, r.pB1)
+    def rs2a(u):
+        va = rview(u, r.rA1, r.pA1)
         arrive((u, "r1a"), va)
         add_into(gview(u, low_z, y, both), va)
         send((u, "r2a"), gview(u, low_z, y, nx), rview(u, r.rA2, r.pA2), xpeer)
+
+    def rs2b(u):
+        vb = rview(u, r.rB1, r.pB1)
         arrive((u, "r1b"), vb)
         add_into(gview(u, high_z, both, x), vb)
         send((u, "r2b"), gview(u, high_z, ny, x), rview(u, r.rB2, r.pB2), ypeer)
@@ -802,6 +838,32 @@
                     at = pl.multiple_of(core * (FF // 2) + (it - 4) * HALF, 128)
                     r.gf_o[:, pl.ds(at, HALF)] = part
 
+    def back1(u):
+        for k in (1, 2, 3):
+            send((u, "b1", k), gview(u, zshift(k), both, both), r.zL.at[k - 1], zpeer(k))
+
+    def back2(u):
+        for k in (1, 2, 3):
+            arrive((u, "b1", k), r.zL.at[k - 1])
+        for yy in (0, 1):
+            for xx in (0, 1):
+                here = gview(u, z, yy, xx)
+                total = here[...].astype(F32)
+                for k in (1, 2, 3):
+                    total = total + r.zL[k - 1, yy, xx].astype(F32)
+                here[...] = total.astype(BF16)
+        send((u, "b2"), gview(u, z, ny, both), r.yL, ypeer)
+
+    def back3(u):
+        arrive((u, "b2"), r.yL)
+        add_into(gview(u, z, y, both), r.yL)
+        send((u, "b3"), gview(u, z, y, nx), r.xL, xpeer)
+
+    def back4(u):
+        kind, first, count = u
+        arrive((u, "b3"), r.xL)
+        r.ptot[pl.ds(first, count), :] = gview(u, z, y, x)[...].astype(F32) + r.xL[...].astype(F32)
+
     def rs_proj_send():
         give = pl.ds(pl.multiple_of(96 * nc, 32), 96)
         send("pfin", r.ptot.at[give, :], r.pfr, partner)
@@ -822,27 +884,7 @@
             total = total + r.gr[first + n]
         return total
 
-    ag2(US)
-    ag2(UQ[0])
-    build_mask()
-    ag3(US)
-    ag2(UQ[1])
-    ag3(UQ[0])
-    ag4(US)
-    ag5(US)
-    small_vectors()
-    for k in (1, 2, 3):
-        arrive(("tok", k), r.xb.at[lax.rem(sp + 4 - k, 4)])
-    own_tok.wait()
-    norm_one()
-    send("h1", r.h1c.at[0], r.h1c.at[1], partner)
-    ag2(UQ[2])
-    ag3(UQ[1])
-    ag4(UQ[0])
-    ag2(UO)
-    ag3(UQ[2])
-    ag4(UQ[1])
-    ag5(UQ[0])
+    tasks = {}
 
     def pairs(body, i):
         def one(h, carry):
@@ -851,151 +893,372 @@
 
         lax.fori_loop(0, 2, one, 0)
 
-    qkv_item(0)
-    pairs(attend_pair, 0)
-    ag2(UF[0])
-    ag3(UO)
-    ag4(UQ[2])
-    ag5(UQ[1])
-    qkv_item(1)
-    pairs(attend_pair, 1)
-    ag2(UF[1])
-    ag3(UF[0])
-    ag4(UO)
-    ag5(UQ[2])
-    send_pack("cot", r.cot, r.cb)
-    qkv_item(2)
-    pairs(attend_pair, 2)
-    send("attn", r.attnc.at[0], r.attnc.at[1], partner)
-    ag2(UP[0])
-    ag3(UF[1])
-    ag4(UF[0])
-    ag5(UO)
-    out_proj()
-    send("h2", r.h2c.at[0], r.h2c.at[1], partner)
-    flip_lse()
-    build_mask_t()
-    ag2(UP[1])
-    ag3(UP[0])
-    ag4(UF[1])
-    ag5(UF[0])
-    for k in (1, 2, 3):
-        arrive(("cot", k), r.cb.at[lax.rem(sp + 4 - k, 4)])
-    own_cot.wait()
-    mlp_grad_rows()
-    send("dml", half_cols(r.dml, nc), r.dml_p, partner)
-
-    def up_two(first):
-        def one(i, carry):
-            up_item(i)
-            return carry
-
-        lax.fori_loop(first, first + 2, one, 0)
-
-    up_two(0)
-    ag3(UP[1])
-    ag4(UP[0])
-    ag5(UF[1])
-    up_two(2)
-    send("act", r.actc.at[0], r.actc.at[1], partner)
-    ag4(UP[1])
-    arrive("dml", r.dml_p)
-    arrive("act", r.actc.at[1])
-    proj_grad()
-    rs1(UP[0])
-    rs1(UP[1])
-    ag5(UP[0])
-    ag5(UP[1])
-    layer_out()
-    own_out = send_rows("out", r.out_o, 2)
-    down_back()
-    send("dpre", r.slope.at[:, pl.ds(pl.multiple_of(nc * (FF // 2), 128), FF // 2)], r.dpre_p, partner)
-    rs2(UP[0])
-    up_back()
-    rs2(UP[1])
-    rs3(UP[0])
-    arrive("h2", r.h2c.at[1])
-    arrive("dpre", r.dpre_p)
-    up_grad(0)
-    rs1(UF[0])
-    rs3(UP[1])
-    up_grad(1)
-    rs1(UF[1])
-    norm_two_back()
-    send("dbr", half_cols(r.dbr, nc), r.dbr_p, partner)
-    rs2(UF[0])
-    rs4(UP[0])
-    out_back()
-    rs2(UF[1])
-    rs3(UF[0])
-    rs4(UP[1])
-    rs_proj_send()
-    arrive("attn", r.attnc.at[1])
-    arrive("dbr", r.dbr_p)
-    out_grad()
-    rs1(UO)
-    arrive("h1", r.h1c.at[1])
-
-    def give_qkv(i):
-        send(("dq", i), r.qkvb.at[3 * nc + i], r.dqp.at[i], partner)
-
-    pairs(attend_back_pair, 0)
-    give_qkv(0)
-    rs3(UF[1])
-    rs2(UO)
-    rs4(UF[0])
-    pairs(attend_back_pair, 1)
-    give_qkv(1)
-    arrive(("dq", 0), r.dqp.at[0])
-    qkv_grad(0)
-    rs1(UQ[0])
-    rs3(UO)
-    rs4(UF[1])
-    pairs(attend_back_pair, 2)
-    give_qkv(2)
-    arrive(("dq", 1), r.dqp.at[1])
-    qkv_grad(1)
-    rs1(UQ[1])
-    rs2(UQ[0])
-    arrive(("dq", 2), r.dqp.at[2])
-    qkv_grad(2)
-    rs1(UQ[2])
-    rs2(UQ[1])
-    rs3(UQ[0])
-    rs4(UO)
-    qkv_back()
-    rs2(UQ[2])
-    rs3(UQ[1])
-    own_out.wait()
-    for k in (1, 2, 3):
-        started.pop(("out", k)).wait_send()
-    norm_one_back()
-    own_dx = send_rows("dx", r.dx_o, 3)
-    r.gsm[12:16, :] = jnp.zeros((4, D), F32)
-    small_send("core", r.gsm, 0, partner)
-    rs3(UQ[2])
-    rs4(UQ[0])
-    r.gs[0] = small_add(["core"], 0, None)
-    small_send("x", r.gs.at[0], 1, xpeer)
-    rs5(UF[0])
-    rs5(UF[1])
-    r.gs[1] = small_add(["x"], 1, 0)
-    small_send("y", r.gs.at[1], 2, ypeer)
-    rs4(UQ[1])
-    rs5(UO)
-    rs_proj_done()
-    r.gs[2] = small_add(["y"], 2, 1)
-    for k in (1, 2, 3):
-        small_send(("z", k), r.gs.at[2], 2 + k, zpeer(k))
-    rs4(UQ[2])
-    rs5(UQ[0])
-    rs5(UQ[1])
-    r.gs_o[...] = small_add([("z", 1), ("z", 2), ("z", 3)], 3, 2)
-    rs5(UQ[2])
+    def comm(name, u):
+        tasks["2" + name] = lambda: ag2(u)
+        tasks["3a" + name] = lambda: ag3a(u)
+        tasks["3b" + name] = lambda: ag3b(u)
+        tasks["4a" + name] = lambda: ag4a(u)
+        tasks["4b" + name] = lambda: ag4b(u)
+        if name != "s":
+            tasks["r1" + name] = lambda: rs1(u)
+            tasks["r2a" + name] = lambda: rs2a(u)
+            tasks["r2b" + name] = lambda: rs2b(u)
+            tasks["r3" + name] = lambda: rs3(u)
+            tasks["r4" + name] = lambda: rs4(u)
+            if name != "p":
+                tasks["r5" + name] = lambda: rs5(u)
+
+    for name, u in (
+        ("s", US), ("q0", UQ[0]), ("q1", UQ[1]), ("q2", UQ[2]), ("o", UO), ("f0", UF[0]), ("f1", UF[1]), ("p", UP)
+    ):
+        comm(name, u)
+    tasks["l2"] = lambda: late2(UL)
+    tasks["l3"] = lambda: late3(UL)
+    tasks["l41"] = lambda: late4(UL, 1)
+    tasks["l42"] = lambda: late4(UL, 2)
+    tasks["l43"] = lambda: late4(UL, 3)
+    tasks["b1"] = lambda: back1(UL)
+    tasks["b2"] = lambda: back2(UL)
+    tasks["b3"] = lambda: back3(UL)
+    tasks["b4"] = lambda: back4(UL)
+
+    def task(body):
+        tasks[body.__name__] = body
+
+    @task
+    def mask():
+        build_mask()
+
+    @task
+    def first_norm():
+        ag5(US)
+        for k in (1, 2, 3):
+            arrive(("tok", k), r.xb.at[lax.rem(sp + 4 - k, 4)])
+        own_tok.wait()
+        small_vectors()
+        norm_one()
+        send("h1", r.h1c.at[0], r.h1c.at[1], partner)
+
+    def qkv(i):
+        def run():
+            ag5(UQ[i])
+            qkv_item(i)
+
+        return run
+
+    def attend(i):
+        return lambda: pairs(attend_pair, i)
+
+    def attend_back(i):
+        def run():
+            pairs(attend_back_pair, i)
+            send(("dq", i), r.qkvb.at[3 * nc + i], r.dqp.at[i], partner)
+
+        return run
+
+    def grad_qkv(i):
+        def run():
+            if i == 0:
+                arrive("h1", r.h1c.at[1])
+            arrive(("dq", i), r.dqp.at[i])
+            qkv_grad(i)
+
+        return run
+
+    for i in range(3):
+        tasks["qkv" + str(i)] = qkv(i)
+        tasks["attend" + str(i)] = attend(i)
+        tasks["attend_back" + str(i)] = attend_back(i)
+        tasks["qkv_grad" + str(i)] = grad_qkv(i)
+
+    @task
+    def send_tok():
+        send_pack("tok", r.tok, r.xb)
+
+    tasks["l1"] = lambda: late1(UL)
+
+    @task
+    def send_cot():
+        send_pack("cot", r.cot, r.cb)
+
+    @task
+    def out():
+        send("attn", r.attnc.at[0], r.attnc.at[1], partner)
+        ag5(UO)
+        out_proj()
+        send("h2", r.h2c.at[0], r.h2c.at[1], partner)
+
+    @task
+    def flip():
+        flip_lse()
+        build_mask_t()
+
+    @task
+    def rows():
+        for k in (1, 2, 3):
+            arrive(("cot", k), r.cb.at[lax.rem(sp + 4 - k, 4)])
+        own_cot.wait()
+        mlp_grad_rows()
+        send("dml", half_cols(r.dml, nc), r.dml_p, partner)
+
+    def act_cols(core, j, h):
+        return r.actc.at[core, :, pl.ds(h * (FF // 2) + j * D, D)]
+
+    def up(j):
+        def run():
+            ag5(UF[j])
+
+            def one(i, carry):
+                up_item(i)
+                return carry
+
+            lax.fori_loop(2 * j, 2 * j + 2, one, 0)
+            for h in (0, 1):
+                send(("act", j, h), act_cols(0, j, h), act_cols(1, j, h), partner)
+
+        return run
+
+    def proj(j):
+        def run():
+            if j == 0:
+                arrive("dml", r.dml_p)
+                for k in (0, 1):
+                    for h in (0, 1):
+                        arrive(("act", k, h), act_cols(1, k, h))
+            proj_grad(4 * j)
+
+        return run
+
+    def up_weight(j):
+        def run():
+            if j == 0:
+                arrive("h2", r.h2c.at[1])
+                arrive("dpre", r.dpre_p)
+            up_grad(j)
+
+        return run
+
+    for j in range(2):
+        tasks["up" + str(j)] = up(j)
+        tasks["proj" + str(j)] = proj(j)
+        tasks["up_grad" + str(j)] = up_weight(j)
+
+    @task
+    def whole():
+        ag5(UP)
+        late5(UL)
+
+    own = {}
+
+    @task
+    def final():
+        layer_out()
+        own["out"] = send_rows("out", r.out_o, 2)
+
+    @task
+    def down():
+        down_back()
+        send("dpre", r.slope.at[:, pl.ds(pl.multiple_of(nc * (FF // 2), 128), FF // 2)], r.dpre_p, partner)
+
+    @task
+    def up_input():
+        up_back()
+
+    @task
+    def second_norm():
+        norm_two_back()
+        send("dbr", half_cols(r.dbr, nc), r.dbr_p, partner)
+
+    @task
+    def out_input():
+        out_back()
+
+    @task
+    def out_weight():
+        arrive("attn", r.attnc.at[1])
+        arrive("dbr", r.dbr_p)
+        out_grad()
+
+    @task
+    def qkv_input():
+        qkv_back()
+
+    @task
+    def last_norm():
+        own["out"].wait()
+        for k in (1, 2, 3):
+            started.pop(("out", k)).wait_send()
+        norm_one_back()
+        r.gsm[12:16, :] = jnp.zeros((4, D), F32)
+        small_send("x", r.gsm, 0, xpeer)
+        own["dx"] = send_rows("dx", r.dx_o, 3)
+
+    @task
+    def small1():
+        r.gs[0] = small_add(["x"], 0, None)
+        small_send("core", r.gs.at[0], 1, partner)
+
+    @task
+    def small2():
+        r.gs[1] = small_add(["core"], 1, 0)
+        small_send("y", r.gs.at[1], 2, ypeer)
+
+    @task
+    def small3():
+        r.gs[2] = small_add(["y"], 2, 1)
+        for k in (1, 2, 3):
+            small_send(("z", k), r.gs.at[2], 2 + k, zpeer(k))
+
+    @task
+    def small4():
+        r.gs_o[...] = small_add([("z", 1), ("z", 2), ("z", 3)], 3, 2)
+
+    @task
+    def proj_send():
+        rs_proj_send()
+
+    @task
+    def proj_done():
+        rs_proj_done()
+
+    t = Bag()
+    for name, body in tasks.items():
+        setattr(t, "g" + name, body)
+    t.gsend_tok()
+    t.g2s()
+    t.gmask()
+    t.gl1()
+    t.g2q0()
+    t.g3bs()
+    t.g2q1()
+    t.g3bq0()
+    t.g3as()
+    t.g3bq1()
+    t.gl2()
+    t.g4as()
+    t.g4bs()
+    t.g3aq0()
+    t.g2q2()
+    t.g3aq1()
+    t.g4bq0()
+    t.g2o()
+    t.g4bq1()
+    t.gl3()
+    t.g4aq0()
+    t.gfirst_norm()
+    t.g3aq2()
+    t.gqkv0()
+    t.g3bq2()
+    t.g2f0()
+    t.g3ao()
+    t.g4aq1()
+    t.g3bo()
+    t.gsend_cot()
+    t.gqkv1()
+    t.gattend0()
+    t.gattend1()
+    t.g2f1()
+    t.g4bo()
+    t.g3af0()
+    t.g4bq2()
+    t.g4aq2()
+    t.g4ao()
+    t.gqkv2()
+    t.g3bf0()
+    t.gattend2()
+    t.gout()
+    t.g3af1()
+    t.g3bf1()
+    t.g2p()
+    t.g4af0()
+    t.g4bf0()
+    t.gflip()
+    t.gup0()
+    t.g4bf1()
+    t.g4af1()
+    t.gl41()
+    t.g3ap()
+    t.gl42()
+    t.grows()
+    t.g3bp()
+    t.gup1()
+    t.gl43()
+    t.g4bp()
+    t.gproj0()
+    t.g4ap()
+    t.gproj1()
+    t.gwhole()
+    t.gr1p()
+    t.gb1()
+    t.gdown()
+    t.gr2bp()
+    t.gfinal()
+    t.gup_input()
+    t.gr2ap()
+    t.gup_grad0()
+    t.gr1f0()
+    t.gsecond_norm()
+    t.gup_grad1()
+    t.gout_input()
+    t.gout_weight()
+    t.gr1f1()
+    t.gattend_back0()
+    t.gr2bf0()
+    t.gr2af0()
+    t.gattend_back1()
+    t.gr1o()
+    t.gr2bf1()
+    t.gr3p()
+    t.gqkv_grad0()
+    t.gattend_back2()
+    t.gr2af1()
+    t.gqkv_input()
+    t.gr3f0()
+    t.gr1q0()
+    t.gr2bo()
+    t.gqkv_grad1()
+    t.gqkv_grad2()
+    t.gr1q2()
+    t.gr1q1()
+    t.gr2ao()
+    t.glast_norm()
+    t.gr3f1()
+    t.gr2bq0()
+    t.gr2bq1()
+    t.gsmall1()
+    t.gr3o()
+    t.gb2()
+    t.gr2aq0()
+    t.gr4f1()
+    t.gr5f1()
+    t.gr2aq2()
+    t.gr2bq2()
+    t.gr3q0()
+    t.gr4f0()
+    t.gr2aq1()
+    t.gr3q2()
+    t.gr4p()
+    t.gr4o()
+    t.gr5f0()
+    t.gr5o()
+    t.gr3q1()
+    t.gb3()
+    t.gsmall2()
+    t.gsmall3()
+    t.gr4q2()
+    t.gb4()
+    t.gproj_send()
+    t.gr4q0()
+    t.gproj_done()
+    t.gr4q1()
+    t.gr5q2()
+    t.gr5q1()
+    t.gsmall4()
+    t.gr5q0()
     for name, dst in (("out", r.out_o), ("dx", r.dx_o)):
         for k in (1, 2, 3):
             arrive((name, k), dst.at[lax.rem(sp + 4 - k, 4)])
-    own_dx.wait()
+    own["dx"].wait()
     for copy in started.values():
         copy.wait_send()
     assert len(table) <= SEMS, len(table)

time: 217 us -> 188 us (0.87)
  Pallas kernels: 200 us -> 172 us
    pallas_call x1, Pallas kernels: 200 us -> 172 us  [fused(): pl.pallas_call(mega, out_shape=(s((4, 128, D), BF16), s((4, 128, D), BF16...]
where the time goes in v3:
time: 188 us
  Pallas kernels  172 us (91%)
  local copies, waits for them, and re-layouts  12.9 us (7%)
  other arithmetic  2.45 us (1%)
    pallas_call x1, Pallas kernels, fused(): pl.pallas_call(mega, out_shape=(s((4, 128, D), BF16), s((4, 128, D), BF16...  172 us
    unnamed x16, local copies, waits for them, and re-layouts  4.96 us

profile of v3, /device:TPU:0, one launch (start us, length us, event | category | flops | bytes accessed | tf_op | source)
XLA Modules:
  0.0 187.8 jit_solution(18328343450015841503)
XLA Ops:
  0.7 1.3 copy.31.refs_2_
  2.0 0.8 stack.35
  2.8 0.6 broadcast_in_dim.6
  3.4 2.5 %dynamic_update_slice.6 = bf16[16,768]{1,0:T(8,128)(2,1)} dynamic-update-slice(bf16[16,768]{1,0:T(8,128)(2,1)} %broadcast_in_dim.6, bf16[8,24]{1,0:T(8,128)(2,1)S(1)} %stack.35, s32[]{:T(128)} %constant.39.clone.1, s32[]{:T(128)S(6)} %select_n.26) | dynamic-update-slice | bytes 772 | tf_op jit(solution)/shard_map/dynamic_update_slice | solution.py:1270
  5.9 1.3 dynamic_update_slice.7.refs_7_
  7.3 171.7 %shard_map.271 = (bf16[4,128,768]{2,1,0:T(8,128)(2,1)}, bf16[4,128,768]{2,1,0:T(8,128)(2,1)}, f32[24,2304]{1,0:T(8,128)}, f32[24,768]{1,0:T(8,128)}, f32[24,3072...) custom-call(bf16[4,128,768]{2,1,0:T(8,128)(2,1)} %refs_0_.1, bf16[4,128,768]{2,1,0:T(8,128)(2,1)} %refs_1_.1, ...), custom_call_target="tpu_custom_call" | custom-call | tf_op jit(solution)/shard_map/pallas_call | solution.py:1275
  179.0 0.0 copy-start
  179.0 1.4 dynamic-slice_bitcast_fusion
  180.4 0.8 constant_dynamic-slice_fusion
  181.1 0.5 slice_bitcast_fusion
  181.7 0.0 copy-start.3
  181.7 2.5 %convert_element_type.3 = f32[4,128,768]{2,1,0:T(8,128)} convert(bf16[4,128,768]{2,1,0:T(8,128)(2,1)} %get-tuple-element.23) | non-fusion elementwise | flops 393216 | bytes 2359296 | tf_op jit(solution)/shard_map/convert_element_type | solution.py:1293
  184.1 0.0 copy-done
  184.1 0.0 copy-start.4
  184.1 0.0 copy-start.2
  184.1 0.0 copy-start.1
  184.1 0.9 copy.39
  185.0 0.0 copy-done.3
  185.0 0.7 copy.40
  185.7 0.0 copy-done.4
  185.7 0.6 copy.41
  186.4 0.0 copy-done.2
  186.4 0.7 copy.42
  187.1 0.0 copy-done.1
  187.1 0.7 copy.43
Async XLA Ops:
  179.0 5.1 %copy-start = (bf16[4,128,768]{2,1,0:T(8,128)(2,1)S(1)}, bf16[4,128,768]{2,1,0:T(8,128)(2,1)}, u32[]{:S(2)}) copy-start(bf16[4,128,768]{2,1,0:T(8,128)(2,1)} %get-tuple-element.52) | copy-start | bytes 2359300
  181.7 3.4 %copy-start.3 = (f32[24,2304]{1,0:T(8,128)S(1)}, f32[24,2304]{1,0:T(8,128)}, u32[]{:S(2)}) copy-start(f32[24,2304]{1,0:T(8,128)} %get-tuple-element.56) | copy-start | bytes 663556
  184.1 1.6 copy-start.4
  184.1 2.2 %copy-start.2 = (f32[24,3072]{1,0:T(8,128)S(1)}, f32[24,3072]{1,0:T(8,128)}, u32[]{:S(2)}) copy-start(f32[24,3072]{1,0:T(8,128)} %get-tuple-element.63) | copy-start | bytes 884740
  184.1 2.9 %copy-start.1 = (f32[96,768]{1,0:T(8,128)S(1)}, f32[96,768]{1,0:T(8,128)}, u32[]{:S(2)}) copy-start(f32[96,768]{1,0:T(8,128)} %get-tuple-element.65) | copy-start | bytes 884740

commit v4 on v3

--- a/solution.py
+++ b/solution.py
@@ -154,6 +154,7 @@
 T, D, FF, HALF = 512, 768, 3072, 384
 ZS = 4
 ZA = 3
+PZ = 3
 ROWS = 32
 
 
@@ -178,11 +179,11 @@
 
 
 NAMES = (
-    "tok", "cot", "cut", "wq", "wo", "wf", "wp", "small", "out_o", "dx_o", "gq_o", "go_o", "gf_o", "gp_o", "gs_o",
+    "tok", "cot", "cut", "wq", "wo", "wf", "wp", "flat", "out_o", "dx_o", "gq_o", "go_o", "gf_o", "gp_o", "gs_o",
     "W", "Wp", "Sw", "sq", "so", "sf", "sp_", "ssm", "vec", "G", "Gp", "rA1", "rB1", "pA1", "pB1", "rA2", "rB2",
     "pA2", "pB2", "rz", "pz", "zL", "yL", "xL", "tot", "ptot", "fr", "pfr", "xb", "cb", "h1c", "qkvb", "attnc", "x1", "h2c", "actc",
     "slope", "dpre_p", "acc", "dbr", "dbr_p", "dml", "dml_p", "dat", "dqp", "ob", "mask", "lse", "lseT", "gsm", "gs",
-    "gr", "ssem", "rsem", "lsem",
+    "gr", "small", "ssem", "rsem", "lsem",
 )
 SEMS = 220
 
@@ -203,12 +204,12 @@
         v((ZS, 2, 2, 192, HALF), BF16),
         v((8, ZA, 2, 48, HALF), BF16),
         v((8, ZS - ZA, 2, 48, HALF), BF16),
-        v((ZA, 2, 96, HALF), BF16),
-        v((ZS - ZA, 2, 96, HALF), BF16),
+        v((PZ, 2, 96, HALF), BF16),
+        v((ZS - PZ, 2, 96, HALF), BF16),
         v((8, ZA, 48, HALF), BF16),
         v((8, ZS - ZA, 48, HALF), BF16),
-        v((ZA, 96, HALF), BF16),
-        v((ZS - ZA, 96, HALF), BF16),
+        v((PZ, 96, HALF), BF16),
+        v((ZS - PZ, 96, HALF), BF16),
         v((8, 3, 48, HALF), BF16),
         v((3, 96, HALF), BF16),
         v((3, 2, 2, 96, HALF), BF16),
@@ -240,8 +241,9 @@
         v((T, 128), F32),
         v((128, T), F32),
         v((16, D), F32),
-        v((3, 16, D), F32),
+        v((4, 16, D), F32),
         v((6, 16, D), F32),
+        v((16, D), BF16),
         pltpu.SemaphoreType.DMA((SEMS,)),
         pltpu.SemaphoreType.DMA((SEMS,)),
         pltpu.SemaphoreType.DMA((4,)),
@@ -260,7 +262,15 @@
     partner = {"dp": dp, "sp": x * 2 + nc}
     xpeer = {"dp": dp, "sp": nx * 2 + c}
     ypeer = {"dp": z * 2 + ny, "sp": sp}
-    every, low_z, high_z = pl.ds(0, ZS), pl.ds(0, ZA), pl.ds(ZA, ZS - ZA)
+    every = pl.ds(0, ZS)
+
+    def low_z(u):
+        return pl.ds(0, PZ if u[0] == "p" else ZA)
+
+    def high_z(u):
+        first = PZ if u[0] == "p" else ZA
+        return pl.ds(first, ZS - first)
+
     both = pl.ds(0, 2)
 
     def zshift(k):
@@ -315,43 +325,43 @@
     def ag2(u):
         for k in (1, 2, 3):
             arrive((u, "z", k), view(u, c, zshift(ZS - k), y, x))
-        v = view(u, c, low_z, y, x)
+        v = view(u, c, low_z(u), y, x)
         send((u, "2a"), v, v, xpeer)
-        v = view(u, c, high_z, y, x)
+        v = view(u, c, high_z(u), y, x)
         send((u, "2b"), v, v, ypeer)
         v = view(u, c, every, y, x)
         send((u, "c0"), v, v, partner)
 
     def ag3a(u):
-        arrive((u, "2a"), view(u, c, low_z, y, nx))
-        v = view(u, c, low_z, y, both)
+        arrive((u, "2a"), view(u, c, low_z(u), y, nx))
+        v = view(u, c, low_z(u), y, both)
         send((u, "3a"), v, v, ypeer)
-        v = view(u, c, low_z, y, nx)
+        v = view(u, c, low_z(u), y, nx)
         send((u, "c1"), v, v, partner)
 
     def ag3b(u):
-        arrive((u, "2b"), view(u, c, high_z, ny, x))
-        v = view(u, c, high_z, both, x)
+        arrive((u, "2b"), view(u, c, high_z(u), ny, x))
+        v = view(u, c, high_z(u), both, x)
         send((u, "3b"), v, v, xpeer)
-        v = view(u, c, high_z, ny, x)
+        v = view(u, c, high_z(u), ny, x)
         send((u, "c2"), v, v, partner)
 
     def ag4a(u):
-        v = view(u, c, low_z, ny, both)
+        v = view(u, c, low_z(u), ny, both)
         arrive((u, "3a"), v)
         send((u, "c3"), v, v, partner)
 
     def ag4b(u):
-        v = view(u, c, high_z, both, nx)
+        v = view(u, c, high_z(u), both, nx)
         arrive((u, "3b"), v)
         send((u, "c4"), v, v, partner)
 
     def ag5(u):
         arrive((u, "c0"), view(u, nc, every, y, x))
-        arrive((u, "c1"), view(u, nc, low_z, y, nx))
-        arrive((u, "c2"), view(u, nc, high_z, ny, x))
-        arrive((u, "c3"), view(u, nc, low_z, ny, both))
-        arrive((u, "c4"), view(u, nc, high_z, both, nx))
+        arrive((u, "c1"), view(u, nc, low_z(u), y, nx))
+        arrive((u, "c2"), view(u, nc, high_z(u), ny, x))
+        arrive((u, "c3"), view(u, nc, low_z(u), ny, both))
+        arrive((u, "c4"), view(u, nc, high_z(u), both, nx))
 
     def late1(u):
         v = view(u, c, z, y, x)
@@ -387,12 +397,44 @@
     UP = ("p", 0, 96)
     UL = ("l", 96, 96)
 
-    swaps = [("small", r.small, r.ssm), ("wq", r.wq, r.sq), ("wp", r.wp, r.sp_), ("wo", r.wo, r.so), ("wf", r.wf, r.sf)]
+    device = dp * 4 + sp
+    low = 24 * device
+    wide_row, wide_low = device // 8, 96 * lax.rem(device, 8)
+
+    def build_small():
+        i = lax.broadcasted_iota(jnp.int32, (384, 1), 0)
+        part = sum((i >= 24 * m).astype(jnp.int32) for m in range(1, 8))
+        target = jnp.where(i < 192, low + i - 24 * part, wide_low + i - 192)
+        target = jnp.where(i < 288, target, -1)
+        j = lax.broadcasted_iota(jnp.int32, (384, D), 1)
+        place = jnp.where(j == target, 1.0, 0.0).astype(BF16)
+        row = lax.broadcasted_iota(jnp.int32, (16, 384), 0)
+        lane = lax.broadcasted_iota(jnp.int32, (16, 384), 1)
+        mine = (row < 8) & (lane >= 24 * row) & (lane < 24 * row + 24)
+        mine = mine | ((row == 8 + wide_row) & (lane >= 192))
+        values = jnp.where(mine, jnp.broadcast_to(r.flat[...].astype(F32), (16, 384)), 0.0).astype(BF16)
+        r.small[...] = lax.dot_general(values, place, (((1,), (0,)), ((), ())), preferred_element_type=F32).astype(BF16)
+
+    def pick_small():
+        j = lax.broadcasted_iota(jnp.int32, (D, 128), 0)
+        lane = lax.broadcasted_iota(jnp.int32, (D, 128), 1)
+        take = ((lane < 24) & (j == low + lane)) | ((lane >= 32) & (j == wide_low + lane - 32))
+        picked = lax.dot_general(
+            r.gs[3], jnp.where(take, 1.0, 0.0), (((1,), (0,)), ((), ())), preferred_element_type=F32,
+            precision=lax.Precision.HIGHEST,
+        )
+        row = lax.broadcasted_iota(jnp.int32, (16, 128), 0)
+        one = jnp.sum(jnp.where(row == 8 + wide_row, picked, 0.0), axis=0, keepdims=True)
+        r.gs_o[...] = jnp.where(row < 8, picked, one)
+
+    swaps = [("wq", r.wq, r.sq), ("wp", r.wp, r.sp_), ("wo", r.wo, r.so), ("wf", r.wf, r.sf)]
     for key, src, dst in swaps:
         send(key, src, dst, partner)
-
-    def send_pack(key, src, dst):
-        for k in (2, 1, 3):
+    build_small()
+    send("small", r.small, r.ssm, partner)
+
+    def send_pack(key, src, dst, shifts):
+        for k in shifts:
             send((key, k), src.at[speer(k)], dst.at[sp], {"dp": dp, "sp": speer(k)})
 
     own_tok = pltpu.make_async_copy(r.tok.at[sp], r.xb.at[sp], r.lsem.at[0])
@@ -453,7 +495,7 @@
         def body(row):
             q = lax.broadcasted_iota(jnp.int32, (ROWS, T), 0) + row
             k = lax.broadcasted_iota(jnp.int32, (ROWS, T), 1)
-            cut = r.cut[sp, 0]
+            cut = r.cut[pl.ds(sp, 1), :]
             ok = (k <= q) & ((k >= cut) == (q >= cut))
             r.mask[pl.ds(row, ROWS), :] = jnp.where(ok, 0.0, NEGATIVE)
 
@@ -463,7 +505,7 @@
         def body(row):
             k = lax.broadcasted_iota(jnp.int32, (ROWS, T), 0) + row
             q = lax.broadcasted_iota(jnp.int32, (ROWS, T), 1)
-            cut = r.cut[sp, 0]
+            cut = r.cut[pl.ds(sp, 1), :]
             ok = (k <= q) & ((k >= cut) == (q >= cut))
             r.mask[pl.ds(row, ROWS), :] = jnp.where(ok, 0.0, NEGATIVE)
 
@@ -588,10 +630,11 @@
 
         rows_loop(T, ROWS, body)
 
-    def send_rows(key, dst, sem):
-        for k in (1, 2, 3):
+    def send_rows(key, dst, shifts):
+        for k in shifts:
             src = r.ob.at[pl.ds(pl.multiple_of(128 * speer(k), 128), 128), :]
             send((key, k), src, dst.at[sp], {"dp": dp, "sp": speer(k)})
+    def keep_rows(dst, sem):
         own = pltpu.make_async_copy(r.ob.at[pl.ds(pl.multiple_of(128 * sp, 128), 128), :], dst.at[sp], r.lsem.at[sem])
         own.start()
         return own
@@ -632,13 +675,14 @@
         return ref.at[:, pl.ds(pl.multiple_of(core * HALF, 128), HALF)]
 
     def proj_grad(first):
-        def chunk(f, carry):
+        def chunk(n, carry):
+            f = 2 * first + lax.rem(n, 2) + 4 * (n // 2)
             at = pl.ds(pl.multiple_of(f * HALF, 128), HALF)
             res = dot(r.actc[0, :, at], half_cols(r.dml, c)[...], 0, 0) + dot(r.actc[1, :, at], r.dml_p[...], 0, 0)
             r.Gp[f // 2, lax.rem(f, 2)] = res.astype(BF16).reshape(2, 192, HALF)
             return carry
 
-        lax.fori_loop(first, first + 4, chunk, 0)
+        lax.fori_loop(0, 4, chunk, 0)
 
     def up_grad(u):
         own = r.slope[:, pl.ds(pl.multiple_of(c * (FF // 2) + u * D, 128), D)]
@@ -778,20 +822,20 @@
         dst[...] = (dst[...].astype(F32) + extra[...].astype(F32)).astype(BF16)
 
     def rs1(u):
-        send((u, "r1a"), gview(u, low_z, ny, both), rview(u, r.rA1, r.pA1), ypeer)
-        send((u, "r1b"), gview(u, high_z, both, nx), rview(u, r.rB1, r.pB1), xpeer)
+        send((u, "r1a"), gview(u, low_z(u), ny, both), rview(u, r.rA1, r.pA1), ypeer)
+        send((u, "r1b"), gview(u, high_z(u), both, nx), rview(u, r.rB1, r.pB1), xpeer)
 
     def rs2a(u):
         va = rview(u, r.rA1, r.pA1)
         arrive((u, "r1a"), va)
-        add_into(gview(u, low_z, y, both), va)
-        send((u, "r2a"), gview(u, low_z, y, nx), rview(u, r.rA2, r.pA2), xpeer)
+        add_into(gview(u, low_z(u), y, both), va)
+        send((u, "r2a"), gview(u, low_z(u), y, nx), rview(u, r.rA2, r.pA2), xpeer)
 
     def rs2b(u):
         vb = rview(u, r.rB1, r.pB1)
         arrive((u, "r1b"), vb)
-        add_into(gview(u, high_z, both, x), vb)
-        send((u, "r2b"), gview(u, high_z, ny, x), rview(u, r.rB2, r.pB2), ypeer)
+        add_into(gview(u, high_z(u), both, x), vb)
+        send((u, "r2b"), gview(u, high_z(u), ny, x), rview(u, r.rB2, r.pB2), ypeer)
 
     def zslot(u, k):
         kind, first, count = u
@@ -802,9 +846,9 @@
     def rs3(u):
         va, vb = rview(u, r.rA2, r.pA2), rview(u, r.rB2, r.pB2)
         arrive((u, "r2a"), va)
-        add_into(gview(u, low_z, y, x), va)
+        add_into(gview(u, low_z(u), y, x), va)
         arrive((u, "r2b"), vb)
-        add_into(gview(u, high_z, y, x), vb)
+        add_into(gview(u, high_z(u), y, x), vb)
         for k in (1, 2, 3):
             send((u, "rz", k), gview(u, zshift(k), y, x), zslot(u, k), zpeer(k))
 
@@ -971,15 +1015,14 @@
         tasks["attend_back" + str(i)] = attend_back(i)
         tasks["qkv_grad" + str(i)] = grad_qkv(i)
 
-    @task
-    def send_tok():
-        send_pack("tok", r.tok, r.xb)
+    tasks["tok2"] = lambda: send_pack("tok", r.tok, r.xb, (2,))
+    tasks["tok1"] = lambda: send_pack("tok", r.tok, r.xb, (1, 3))
+    tasks["dx2"] = lambda: send_rows("dx", r.dx_o, (2,))
+    tasks["dx1"] = lambda: send_rows("dx", r.dx_o, (1, 3))
+    tasks["cot2"] = lambda: send_pack("cot", r.cot, r.cb, (2,))
+    tasks["cot1"] = lambda: send_pack("cot", r.cot, r.cb, (1, 3))
 
     tasks["l1"] = lambda: late1(UL)
-
-    @task
-    def send_cot():
-        send_pack("cot", r.cot, r.cb)
 
     @task
     def out():
@@ -1022,10 +1065,9 @@
         def run():
             if j == 0:
                 arrive("dml", r.dml_p)
-                for k in (0, 1):
-                    for h in (0, 1):
-                        arrive(("act", k, h), act_cols(1, k, h))
-            proj_grad(4 * j)
+            for h in (0, 1):
+                arrive(("act", j, h), act_cols(1, j, h))
+            proj_grad(j)
 
         return run
 
@@ -1053,7 +1095,8 @@
     @task
     def final():
         layer_out()
-        own["out"] = send_rows("out", r.out_o, 2)
+        send_rows("out", r.out_o, (2, 1, 3))
+        own["out"] = keep_rows(r.out_o, 2)
 
     @task
     def down():
@@ -1091,7 +1134,7 @@
         norm_one_back()
         r.gsm[12:16, :] = jnp.zeros((4, D), F32)
         small_send("x", r.gsm, 0, xpeer)
-        own["dx"] = send_rows("dx", r.dx_o, 3)
+        own["dx"] = keep_rows(r.dx_o, 3)
 
     @task
     def small1():
@@ -1111,7 +1154,8 @@
 
     @task
     def small4():
-        r.gs_o[...] = small_add([("z", 1), ("z", 2), ("z", 3)], 3, 2)
+        r.gs[3] = small_add([("z", 1), ("z", 2), ("z", 3)], 3, 2)
+        pick_small()
 
     @task
     def proj_send():
@@ -1124,72 +1168,74 @@
     t = Bag()
     for name, body in tasks.items():
         setattr(t, "g" + name, body)
-    t.gsend_tok()
+    t.gtok2()
+    t.gl1()
+    t.gmask()
     t.g2s()
-    t.gmask()
-    t.gl1()
+    t.g3bs()
+    t.gl2()
+    t.g3as()
     t.g2q0()
-    t.g3bs()
+    t.gtok1()
+    t.g4bs()
+    t.g4as()
+    t.g3aq0()
     t.g2q1()
     t.g3bq0()
-    t.g3as()
-    t.g3bq1()
-    t.gl2()
-    t.g4as()
-    t.g4bs()
-    t.g3aq0()
+    t.gfirst_norm()
     t.g2q2()
     t.g3aq1()
+    t.g4aq0()
+    t.g3bq1()
     t.g4bq0()
     t.g2o()
+    t.g3bq2()
+    t.gqkv0()
+    t.g3aq2()
+    t.gattend0()
+    t.g4aq1()
     t.g4bq1()
+    t.g3ao()
+    t.g3bo()
+    t.gqkv1()
+    t.g2f0()
+    t.g4bq2()
     t.gl3()
-    t.g4aq0()
-    t.gfirst_norm()
-    t.g3aq2()
-    t.gqkv0()
-    t.g3bq2()
-    t.g2f0()
-    t.g3ao()
-    t.g4aq1()
-    t.g3bo()
-    t.gsend_cot()
-    t.gqkv1()
-    t.gattend0()
+    t.gcot2()
+    t.gcot1()
     t.gattend1()
+    t.g4aq2()
+    t.g4bo()
+    t.gqkv2()
+    t.gattend2()
     t.g2f1()
-    t.g4bo()
     t.g3af0()
-    t.g4bq2()
-    t.g4aq2()
+    t.g3bf0()
     t.g4ao()
-    t.gqkv2()
-    t.g3bf0()
-    t.gattend2()
+    t.gflip()
     t.gout()
+    t.g3bf1()
+    t.grows()
     t.g3af1()
-    t.g3bf1()
     t.g2p()
     t.g4af0()
     t.g4bf0()
-    t.gflip()
     t.gup0()
     t.g4bf1()
-    t.g4af1()
     t.gl41()
     t.g3ap()
-    t.gl42()
-    t.grows()
+    t.g4af1()
+    t.gproj0()
     t.g3bp()
     t.gup1()
+    t.gl42()
+    t.g4bp()
+    t.gproj1()
+    t.g4ap()
+    t.gb1()
+    t.gr1p()
     t.gl43()
-    t.g4bp()
-    t.gproj0()
-    t.g4ap()
-    t.gproj1()
     t.gwhole()
-    t.gr1p()
-    t.gb1()
     t.gdown()
     t.gr2bp()
     t.gfinal()
@@ -1197,64 +1243,66 @@
     t.gr2ap()
     t.gup_grad0()
     t.gr1f0()
+    t.gup_grad1()
+    t.gr1f1()
     t.gsecond_norm()
-    t.gup_grad1()
     t.gout_input()
+    t.gattend_back0()
+    t.gr3p()
+    t.gr2af0()
     t.gout_weight()
-    t.gr1f1()
-    t.gattend_back0()
     t.gr2bf0()
-    t.gr2af0()
+    t.gr1o()
     t.gattend_back1()
-    t.gr1o()
     t.gr2bf1()
-    t.gr3p()
     t.gqkv_grad0()
+    t.gr1q0()
     t.gattend_back2()
     t.gr2af1()
+    t.gqkv_grad1()
+    t.gr1q1()
     t.gqkv_input()
+    t.gb2()
     t.gr3f0()
-    t.gr1q0()
     t.gr2bo()
-    t.gqkv_grad1()
+    t.gr2bq0()
     t.gqkv_grad2()
     t.gr1q2()
-    t.gr1q1()
+    t.glast_norm()
+    t.gr4p()
+    t.gr3f1()
     t.gr2ao()
-    t.glast_norm()
-    t.gr3f1()
-    t.gr2bq0()
     t.gr2bq1()
+    t.gr2bq2()
+    t.gr2aq0()
     t.gsmall1()
-    t.gr3o()
-    t.gb2()
-    t.gr2aq0()
-    t.gr4f1()
-    t.gr5f1()
-    t.gr2aq2()
-    t.gr2bq2()
-    t.gr3q0()
+    t.gsmall2()
     t.gr4f0()
     t.gr2aq1()
-    t.gr3q2()
-    t.gr4p()
-    t.gr4o()
     t.gr5f0()
-    t.gr5o()
-    t.gr3q1()
     t.gb3()
-    t.gsmall2()
-    t.gsmall3()
-    t.gr4q2()
+    t.gr3o()
+    t.gr4f1()
+    t.gr3q0()
+    t.gr5f1()
     t.gb4()
     t.gproj_send()
+    t.gproj_done()
+    t.gr2aq2()
+    t.gdx2()
+    t.gdx1()
+    t.gr3q1()
+    t.gr4o()
+    t.gsmall3()
+    t.gr5o()
+    t.gr3q2()
     t.gr4q0()
-    t.gproj_done()
+    t.gr5q0()
     t.gr4q1()
-    t.gr5q2()
     t.gr5q1()
     t.gsmall4()
-    t.gr5q0()
+    t.gr4q2()
+    t.gr5q2()
     for name, dst in (("out", r.out_o), ("dx", r.dx_o)):
         for k in (1, 2, 3):
             arrive((name, k), dst.at[lax.rem(sp + 4 - k, 4)])
@@ -1265,10 +1313,7 @@
 
 
 def fused(tokens, cotangent, seq_cut, g1, o1, w_qkv, bq, bv, w_out, bo, g2, o2, w_fc, bf, w_proj, bp):
-    device = lax.axis_index("dp") * 4 + lax.axis_index("sp")
-    small = jnp.zeros((16, D), BF16)
-    small = lax.dynamic_update_slice(small, jnp.stack([g1, o1, bq, bv, bo, g2, o2, bp]), (0, 24 * device))
-    small = lax.dynamic_update_slice(small, bf[None], (8 + device // 8, 96 * (device % 8)))
+    flat = jnp.concatenate([v[None] for v in (g1, o1, bq, bv, bo, g2, o2, bp, bf)] + [jnp.zeros((1, 96), BF16)], axis=1)
     vmem = pl.BlockSpec(memory_space=pltpu.VMEM)
     anywhere = pl.BlockSpec(memory_space=pl.ANY)
     s = jax.ShapeDtypeStruct
@@ -1281,15 +1326,14 @@
             s((24, D), F32),
             s((24, FF), F32),
             s((96, D), F32),
-            s((16, D), F32),
+            s((16, 128), F32),
         ),
-        in_specs=[anywhere, anywhere, pl.BlockSpec(memory_space=pltpu.SMEM)] + [vmem] * 5,
+        in_specs=[anywhere, anywhere] + [vmem] * 6,
         out_specs=(anywhere, anywhere) + (vmem,) * 5,
         scratch_shapes=scratch_shapes(),
         compiler_params=pltpu.CompilerParams(collective_id=0, has_side_effects=True, vmem_limit_bytes=67043328),
-    )(tokens, cotangent, seq_cut, w_qkv, w_out, w_fc, w_proj, small)
-    rows = lax.dynamic_slice(gs, (0, 24 * device), (8, 24))
-    g_bf = lax.dynamic_slice(gs, (8 + device // 8, 96 * (device % 8)), (1, 96))[0]
+    )(tokens, cotangent, seq_cut, w_qkv, w_out, w_fc, w_proj, flat)
+    rows, g_bf = gs[:8, :24], gs[8, 32:]
     return (out, d_x.astype(F32), rows[0], rows[1], gq, rows[2], rows[3], go, rows[4], rows[5], rows[6], gf, g_bf, gp, rows[7])
 
 

time: 188 us -> 176 us (0.936)
  Pallas kernels: 172 us -> 163 us
  local copies, waits for them, and re-layouts: 12.9 us -> 9.24 us
    pallas_call x1, Pallas kernels: 172 us -> 163 us  [fused(): pl.pallas_call(mega, out_shape=(s((4, 128, D), BF16), s((4, 128, D), BF16...]
    dynamic_update_slice x2 -> x0, local copies, waits for them, and re-layouts: 3.87 us -> none  [the longest x1 2.55 us: fused(): lax.dynamic_update_slice(small, jnp.stack([g1, o1, bq, bv, bo, g2, o2, bp...]
where the time goes in v4:
time: 176 us; the launch traced here: 175 us
  Pallas kernels  163 us (93%)
  local copies, waits for them, and re-layouts  9.24 us (5%)
  other arithmetic  2.45 us (1%)
    pallas_call x1, Pallas kernels, fused(): pl.pallas_call(mega, out_shape=(s((4, 128, D), BF16), s((4, 128, D), BF16...  163 us
    unnamed x16, local copies, waits for them, and re-layouts  4.96 us

profile of v4, /device:TPU:0, one launch (start us, length us, event | category | flops | bytes accessed | tf_op | source)
XLA Modules:
  0.0 175.5 jit_solution(12232021944329449919)
XLA Ops:
  0.7 1.4 concatenate.3.refs_7_
  2.1 1.3 copy.31.refs_2_
  3.4 163.1 %shard_map.271 = (bf16[4,128,768]{2,1,0:T(8,128)(2,1)}, bf16[4,128,768]{2,1,0:T(8,128)(2,1)}, f32[24,2304]{1,0:T(8,128)}, f32[24,768]{1,0:T(8,128)}, f32[24,3072...) custom-call(bf16[4,128,768]{2,1,0:T(8,128)(2,1)} %refs_0_.1, bf16[4,128,768]{2,1,0:T(8,128)(2,1)} %refs_1_.1, ...), custom_call_target="tpu_custom_call" | custom-call | tf_op jit(solution)/shard_map/pallas_call | solution.py:1320
  166.5 0.0 copy-start
  166.5 1.3 slice_bitcast_fusion.1
  167.9 1.5 slice_bitcast_fusion
  169.4 0.0 copy-start.3
  169.4 2.5 %convert_element_type.3 = f32[4,128,768]{2,1,0:T(8,128)} convert(bf16[4,128,768]{2,1,0:T(8,128)(2,1)} %get-tuple-element.23) | non-fusion elementwise | flops 393216 | bytes 2359296 | tf_op jit(solution)/shard_map/convert_element_type | solution.py:1337
  171.8 0.0 copy-done
  171.8 0.0 copy-start.4
  171.8 0.0 copy-start.2
  171.8 0.0 copy-start.1
  171.9 0.9 copy.37
  172.7 0.0 copy-done.3
  172.7 0.7 copy.38
  173.4 0.0 copy-done.4
  173.4 0.6 copy.39
  174.1 0.0 copy-done.2
  174.1 0.7 copy.40
  174.8 0.0 copy-done.1
  174.8 0.7 copy.41
  (1 shorter events, 0.0 us)
Async XLA Ops:
  166.5 5.3 %copy-start = (bf16[4,128,768]{2,1,0:T(8,128)(2,1)S(1)}, bf16[4,128,768]{2,1,0:T(8,128)(2,1)}, u32[]{:S(2)}) copy-start(bf16[4,128,768]{2,1,0:T(8,128)(2,1)} %get-tuple-element.52) | copy-start | bytes 2359300
  169.4 3.4 %copy-start.3 = (f32[24,2304]{1,0:T(8,128)S(1)}, f32[24,2304]{1,0:T(8,128)}, u32[]{:S(2)}) copy-start(f32[24,2304]{1,0:T(8,128)} %get-tuple-element.56) | copy-start | bytes 663556
  171.8 1.6 copy-start.4
  171.8 2.2 %copy-start.2 = (f32[24,3072]{1,0:T(8,128)S(1)}, f32[24,3072]{1,0:T(8,128)}, u32[]{:S(2)}) copy-start(f32[24,3072]{1,0:T(8,128)} %get-tuple-element.63) | copy-start | bytes 884740
  171.8 2.9 %copy-start.1 = (f32[96,768]{1,0:T(8,128)S(1)}, f32[96,768]{1,0:T(8,128)}, u32[]{:S(2)}) copy-start(f32[96,768]{1,0:T(8,128)} %get-tuple-element.65) | copy-start | bytes 884740

commit v5 on v4

--- a/solution.py
+++ b/solution.py
@@ -156,6 +156,7 @@
 ZA = 3
 PZ = 3
 ROWS = 32
+NORM = 64
 
 
 class Bag:
@@ -476,8 +477,8 @@
     def wide(item):
         return jnp.concatenate([r.W[item, h].reshape(D, HALF) for h in (0, 1)], axis=1)
 
-    def tile_x(buf, row):
-        return buf[row // 128, pl.ds(pl.multiple_of(lax.rem(row, 128), ROWS), ROWS), :].astype(F32)
+    def tile_x(buf, row, size):
+        return buf[row // 128, pl.ds(pl.multiple_of(lax.rem(row, 128), size), size), :].astype(F32)
 
     def vrow(i):
         return r.vec[i : i + 1, :]
@@ -522,10 +523,10 @@
 
     def norm_one():
         def body(row):
-            xhat, _ = stats(tile_x(r.xb, row))
-            r.h1c[0, pl.ds(row, ROWS), :] = (xhat * vrow(0) + vrow(1)).astype(BF16)
-
-        rows_loop(T, ROWS, body)
+            xhat, _ = stats(tile_x(r.xb, row, NORM))
+            r.h1c[0, pl.ds(row, NORM), :] = (xhat * vrow(0) + vrow(1)).astype(BF16)
+
+        rows_loop(T, NORM, body)
 
     def qkv_item(i):
         res = dot(r.h1c[0], wide(i), 1, 0)
@@ -573,12 +574,12 @@
         r.acc[...] = dot(r.attnc[0], wide(3), 1, 0)
 
         def body(row):
-            v = tile_x(r.xb, row) + BRANCH * (r.acc[pl.ds(row, ROWS), :] + vrow(4))
-            r.x1[pl.ds(row, ROWS), :] = v
+            v = tile_x(r.xb, row, NORM) + BRANCH * (r.acc[pl.ds(row, NORM), :] + vrow(4))
+            r.x1[pl.ds(row, NORM), :] = v
             xhat, _ = stats(v)
-            r.h2c[0, pl.ds(row, ROWS), :] = (xhat * vrow(5) + vrow(6)).astype(BF16)
-
-        rows_loop(T, ROWS, body)
+            r.h2c[0, pl.ds(row, NORM), :] = (xhat * vrow(5) + vrow(6)).astype(BF16)
+
+        rows_loop(T, NORM, body)
 
     def up_item(i):
         r.acc[...] = dot(r.h2c[0], wide(4 + i), 1, 0)
@@ -608,7 +609,7 @@
 
     def mlp_grad_rows():
         def body(row, sums):
-            d = (tile_x(r.cb, row) * BRANCH).astype(BF16)
+            d = (tile_x(r.cb, row, ROWS) * BRANCH).astype(BF16)
             r.dml[pl.ds(row, ROWS), :] = d
             return sums + fold8(d.astype(F32))
 
@@ -692,11 +693,11 @@
 
     def norm_two_back():
         def body(i, sums):
-            row = pl.multiple_of(i * ROWS, ROWS)
-            here = pl.ds(row, ROWS)
+            row = pl.multiple_of(i * NORM, NORM)
+            here = pl.ds(row, NORM)
             xhat, inverse = stats(r.x1[here, :])
             d_h2 = r.acc[here, :]
-            d_x1 = tile_x(r.cb, row) + norm_back(xhat, inverse, d_h2 * vrow(5))
+            d_x1 = tile_x(r.cb, row, NORM) + norm_back(xhat, inverse, d_h2 * vrow(5))
             r.x1[here, :] = d_x1
             d_branch = (d_x1 * BRANCH).astype(BF16)
             r.dbr[here, :] = d_branch
@@ -706,7 +707,7 @@
                 sums[2] + fold8(d_branch.astype(F32)),
             )
 
-        sums = lax.fori_loop(0, T // ROWS, body, zero_sums(3))
+        sums = lax.fori_loop(0, T // NORM, body, zero_sums(3))
         for k, at in enumerate((5, 6, 4)):
             r.gsm[at : at + 1, :] = jnp.sum(sums[k], axis=0, keepdims=True)
 
@@ -793,15 +794,15 @@
 
     def norm_one_back():
         def body(i, sums):
-            row = pl.multiple_of(i * ROWS, ROWS)
-            here = pl.ds(row, ROWS)
-            xhat, inverse = stats(tile_x(r.xb, row))
+            row = pl.multiple_of(i * NORM, NORM)
+            here = pl.ds(row, NORM)
+            xhat, inverse = stats(tile_x(r.xb, row, NORM))
             d_h1 = r.acc[here, :]
             d_x = r.x1[here, :] + norm_back(xhat, inverse, d_h1 * vrow(0))
             r.ob[here, :] = d_x.astype(BF16)
             return (sums[0] + fold8(d_h1 * xhat), sums[1] + fold8(d_h1))
 
-        sums = lax.fori_loop(0, T // ROWS, body, zero_sums(2))
+        sums = lax.fori_loop(0, T // NORM, body, zero_sums(2))
         for k, at in enumerate((0, 1)):
             r.gsm[at : at + 1, :] = jnp.sum(sums[k], axis=0, keepdims=True)
 
@@ -1172,49 +1173,49 @@
     t.gl1()
     t.gmask()
     t.g2s()
+    t.gl2()
     t.g3bs()
-    t.gl2()
     t.g3as()
     t.g2q0()
     t.gtok1()
     t.g4bs()
     t.g4as()
-    t.g3aq0()
     t.g2q1()
     t.g3bq0()
+    t.g3aq0()
+    t.g3bq1()
+    t.g2q2()
     t.gfirst_norm()
-    t.g2q2()
     t.g3aq1()
     t.g4aq0()
-    t.g3bq1()
+    t.g2o()
     t.g4bq0()
-    t.g2o()
     t.g3bq2()
+    t.g4bq1()
     t.gqkv0()
     t.g3aq2()
     t.gattend0()
     t.g4aq1()
-    t.g4bq1()
     t.g3ao()
     t.g3bo()
-    t.gqkv1()
     t.g2f0()
-    t.g4bq2()
     t.gl3()
     t.gcot2()
     t.gcot1()
+    t.g4bq2()
+    t.gqkv1()
     t.gattend1()
     t.g4aq2()
     t.g4bo()
+    t.g2f1()
     t.gqkv2()
+    t.g3af0()
+    t.g4ao()
     t.gattend2()
-    t.g2f1()
-    t.g3af0()
     t.g3bf0()
-    t.g4ao()
+    t.g3bf1()
+    t.gout()
     t.gflip()
-    t.gout()
-    t.g3bf1()
     t.grows()
     t.g3af1()
     t.g2p()
@@ -1227,18 +1228,18 @@
     t.g4af1()
     t.gproj0()
     t.g3bp()
+    t.gl42()
     t.gup1()
-    t.gl42()
+    t.gl43()
     t.g4bp()
+    t.g4ap()
     t.gproj1()
-    t.g4ap()
     t.gb1()
     t.gr1p()
-    t.gl43()
     t.gwhole()
     t.gdown()
+    t.gfinal()
     t.gr2bp()
-    t.gfinal()
     t.gup_input()
     t.gr2ap()
     t.gup_grad0()
@@ -1259,43 +1260,43 @@
     t.gr1q0()
     t.gattend_back2()
     t.gr2af1()
+    t.gr2bo()
+    t.gr3f0()
     t.gqkv_grad1()
     t.gr1q1()
+    t.gr2bq0()
     t.gqkv_input()
     t.gb2()
-    t.gr3f0()
-    t.gr2bo()
-    t.gr2bq0()
     t.gqkv_grad2()
     t.gr1q2()
+    t.gr2ao()
     t.glast_norm()
-    t.gr4p()
     t.gr3f1()
-    t.gr2ao()
     t.gr2bq1()
     t.gr2bq2()
     t.gr2aq0()
+    t.gr4p()
+    t.gr3o()
     t.gsmall1()
     t.gsmall2()
+    t.gr2aq1()
+    t.gr3q0()
     t.gr4f0()
-    t.gr2aq1()
+    t.gb3()
     t.gr5f0()
-    t.gb3()
-    t.gr3o()
-    t.gr4f1()
-    t.gr3q0()
-    t.gr5f1()
     t.gb4()
     t.gproj_send()
-    t.gproj_done()
     t.gr2aq2()
     t.gdx2()
     t.gdx1()
     t.gr3q1()
+    t.gproj_done()
+    t.gr4f1()
+    t.gsmall3()
+    t.gr5f1()
     t.gr4o()
-    t.gsmall3()
+    t.gr3q2()
     t.gr5o()
-    t.gr3q2()
     t.gr4q0()
     t.gr5q0()
     t.gr4q1()
@@ -1310,6 +1311,12 @@
     for copy in started.values():
         copy.wait_send()
     assert len(table) <= SEMS, len(table)
+
+
+def finish(out, d_x, gq, go, gf, gp, out_o, dx_o, gq_o, go_o, gf_o, gp_o):
+    for src, dst in ((out, out_o), (gq, gq_o), (go, go_o), (gf, gf_o), (gp, gp_o)):
+        dst[...] = src[...]
+    dx_o[...] = d_x[...].astype(F32)
 
 
 def fused(tokens, cotangent, seq_cut, g1, o1, w_qkv, bq, bv, w_out, bo, g2, o2, w_fc, bf, w_proj, bp):
@@ -1333,8 +1340,21 @@
         scratch_shapes=scratch_shapes(),
         compiler_params=pltpu.CompilerParams(collective_id=0, has_side_effects=True, vmem_limit_bytes=67043328),
     )(tokens, cotangent, seq_cut, w_qkv, w_out, w_fc, w_proj, flat)
+    out, d_x, gq, go, gf, gp = pl.pallas_call(
+        finish,
+        out_shape=(
+            s((4, 128, D), BF16),
+            s((4, 128, D), F32),
+            s((24, 3 * D), F32),
+            s((24, D), F32),
+            s((24, FF), F32),
+            s((96, D), F32),
+        ),
+        in_specs=[vmem] * 6,
+        out_specs=(vmem,) * 6,
+    )(out, d_x, gq, go, gf, gp)
     rows, g_bf = gs[:8, :24], gs[8, 32:]
-    return (out, d_x.astype(F32), rows[0], rows[1], gq, rows[2], rows[3], go, rows[4], rows[5], rows[6], gf, g_bf, gp, rows[7])
+    return (out, d_x, rows[0], rows[1], gq, rows[2], rows[3], go, rows[4], rows[5], rows[6], gf, g_bf, gp, rows[7])
 
 
 def solution(mesh):

time: 176 us -> 171 us (0.972)
  local copies, waits for them, and re-layouts: 9.24 us -> 5.51 us
  other arithmetic: 2.45 us -> 0 us
  Pallas kernels: 163 us -> 165 us
    unnamed x16 -> x1, local copies, waits for them, and re-layouts: 4.96 us -> 1.31 us
    pallas_call x0 -> x1, Pallas kernels: none -> 3.41 us  [fused(): pl.pallas_call(finish, out_shape=(s((4, 128, D), BF16), s((4, 128, D), F3...]
    convert_element_type x1 -> x0, other arithmetic: 2.45 us -> none  [fused(): d_x.astype(F32)]
    pallas_call x1, Pallas kernels: 163 us -> 161 us  [fused(): pl.pallas_call(mega, out_shape=(s((4, 128, D), BF16), s((4, 128, D), BF16...]
where the time goes in v5:
time: 171 us
  Pallas kernels  165 us (96%)
  local copies, waits for them, and re-layouts  5.51 us (3%)
    pallas_call x1, Pallas kernels, fused(): pl.pallas_call(mega, out_shape=(s((4, 128, D), BF16), s((4, 128, D), BF16...  161 us

profile of v5, /device:TPU:0, one launch (start us, length us, event | category | flops | bytes accessed | tf_op | source)
XLA Modules:
  0.0 170.9 jit_solution(4558830912321253177)
XLA Ops:
  0.7 1.4 concatenate.3.refs_7_
  2.1 1.3 copy.31.refs_2_
  3.4 161.3 %shard_map.271 = (bf16[4,128,768]{2,1,0:T(8,128)(2,1)}, bf16[4,128,768]{2,1,0:T(8,128)(2,1)}, f32[24,2304]{1,0:T(8,128)}, f32[24,768]{1,0:T(8,128)}, f32[24,3072...) custom-call(bf16[4,128,768]{2,1,0:T(8,128)(2,1)} %refs_0_.1, bf16[4,128,768]{2,1,0:T(8,128)(2,1)} %refs_1_.1, ...), custom_call_target="tpu_custom_call" | custom-call | tf_op jit(solution)/shard_map/pallas_call | solution.py:1327
  164.8 1.2 slice_bitcast_fusion.1
  166.0 1.5 slice_bitcast_fusion
  167.5 3.4 %shard_map.272 = (bf16[4,128,768]{2,1,0:T(8,128)(2,1)}, f32[4,128,768]{2,1,0:T(8,128)}, f32[24,2304]{1,0:T(8,128)}, f32[24,768]{1,0:T(8,128)}, f32[24,3072]{1,0:T(8,128)}, /*index=5*/f32[96,768]{1,0:T(8,128)}) custom-call(bf16[4,128,768]{2,1,0:T(8,128)(2,1)} %get-tuple-element.28.out, bf16[4,128,768]{2,1,0:T(8,128)(2,1)} %get-tuple-element.29.d_x, ...), custom_call_target="tpu_custom_call" | custom-call | tf_op jit(solution)/shard_map/pallas_call | solution.py:1343
  (1 shorter events, 0.0 us)

commit v6 on v5

--- a/solution.py
+++ b/solution.py
@@ -1184,38 +1184,38 @@
     t.g3bq0()
     t.g3aq0()
     t.g3bq1()
+    t.gfirst_norm()
     t.g2q2()
-    t.gfirst_norm()
     t.g3aq1()
     t.g4aq0()
+    t.g4bq0()
     t.g2o()
-    t.g4bq0()
     t.g3bq2()
     t.g4bq1()
     t.gqkv0()
+    t.gattend0()
     t.g3aq2()
-    t.gattend0()
     t.g4aq1()
+    t.g3bo()
     t.g3ao()
-    t.g3bo()
+    t.g4bq2()
     t.g2f0()
     t.gl3()
     t.gcot2()
     t.gcot1()
-    t.g4bq2()
     t.gqkv1()
     t.gattend1()
+    t.g4bo()
     t.g4aq2()
-    t.g4bo()
     t.g2f1()
     t.gqkv2()
     t.g3af0()
+    t.gattend2()
     t.g4ao()
-    t.gattend2()
+    t.gflip()
     t.g3bf0()
+    t.gout()
     t.g3bf1()
-    t.gout()
-    t.gflip()
     t.grows()
     t.g3af1()
     t.g2p()
@@ -1226,12 +1226,12 @@
     t.gl41()
     t.g3ap()
     t.g4af1()
+    t.g3bp()
     t.gproj0()
-    t.g3bp()
     t.gl42()
     t.gup1()
+    t.g4bp()
     t.gl43()
-    t.g4bp()
     t.g4ap()
     t.gproj1()
     t.gb1()
@@ -1241,69 +1241,69 @@
     t.gfinal()
     t.gr2bp()
     t.gup_input()
+    t.gup_grad0()
     t.gr2ap()
-    t.gup_grad0()
     t.gr1f0()
     t.gup_grad1()
     t.gr1f1()
     t.gsecond_norm()
     t.gout_input()
     t.gattend_back0()
+    t.gout_weight()
+    t.gr1o()
+    t.gattend_back1()
     t.gr3p()
     t.gr2af0()
-    t.gout_weight()
+    t.gqkv_grad0()
     t.gr2bf0()
-    t.gr1o()
-    t.gattend_back1()
-    t.gr2bf1()
-    t.gqkv_grad0()
     t.gr1q0()
     t.gattend_back2()
+    t.gr2bf1()
+    t.gqkv_grad1()
+    t.gr2bo()
+    t.gr1q1()
+    t.gqkv_input()
+    t.gqkv_grad2()
     t.gr2af1()
-    t.gr2bo()
+    t.gr1q2()
+    t.glast_norm()
+    t.gr2bq0()
+    t.gr2ao()
+    t.gr2bq1()
     t.gr3f0()
-    t.gqkv_grad1()
-    t.gr1q1()
-    t.gr2bq0()
-    t.gqkv_input()
     t.gb2()
-    t.gqkv_grad2()
-    t.gr1q2()
-    t.gr2ao()
-    t.glast_norm()
+    t.gr2aq0()
+    t.gr2bq2()
+    t.gr4p()
+    t.gsmall1()
     t.gr3f1()
-    t.gr2bq1()
-    t.gr2bq2()
-    t.gr2aq0()
-    t.gr4p()
+    t.gsmall2()
     t.gr3o()
-    t.gsmall1()
-    t.gsmall2()
     t.gr2aq1()
-    t.gr3q0()
     t.gr4f0()
-    t.gb3()
     t.gr5f0()
-    t.gb4()
-    t.gproj_send()
     t.gr2aq2()
     t.gdx2()
     t.gdx1()
+    t.gr3q0()
     t.gr3q1()
-    t.gproj_done()
     t.gr4f1()
+    t.gb3()
+    t.gr5f1()
+    t.gr3q2()
     t.gsmall3()
-    t.gr5f1()
     t.gr4o()
-    t.gr3q2()
     t.gr5o()
     t.gr4q0()
     t.gr5q0()
+    t.gb4()
+    t.gproj_send()
     t.gr4q1()
+    t.gproj_done()
     t.gr5q1()
-    t.gsmall4()
     t.gr4q2()
     t.gr5q2()
+    t.gsmall4()
     for name, dst in (("out", r.out_o), ("dx", r.dx_o)):
         for k in (1, 2, 3):
             arrive((name, k), dst.at[lax.rem(sp + 4 - k, 4)])

time: 171 us -> 172 us (level)
  no operation moved by 1% of the time
where the time goes in v6:
time: 172 us; the launch traced here: 171 us
  Pallas kernels  165 us (96%)
  local copies, waits for them, and re-layouts  5.51 us (3%)
    pallas_call x1, Pallas kernels, fused(): pl.pallas_call(mega, out_shape=(s((4, 128, D), BF16), s((4, 128, D), BF16...  161 us

profile of v6, /device:TPU:0, one launch (start us, length us, event | category | flops | bytes accessed | tf_op | source)
XLA Modules:
  0.0 171.0 jit_solution(498208445936972064)
XLA Ops:
  0.7 1.4 concatenate.3.refs_7_
  2.1 1.3 copy.31.refs_2_
  3.4 161.4 %shard_map.271 = (bf16[4,128,768]{2,1,0:T(8,128)(2,1)}, bf16[4,128,768]{2,1,0:T(8,128)(2,1)}, f32[24,2304]{1,0:T(8,128)}, f32[24,768]{1,0:T(8,128)}, f32[24,3072...) custom-call(bf16[4,128,768]{2,1,0:T(8,128)(2,1)} %refs_0_.1, bf16[4,128,768]{2,1,0:T(8,128)(2,1)} %refs_1_.1, ...), custom_call_target="tpu_custom_call" | custom-call | tf_op jit(solution)/shard_map/pallas_call | solution.py:1327
  164.8 1.2 slice_bitcast_fusion.1
  166.1 1.5 slice_bitcast_fusion
  167.6 3.4 %shard_map.272 = (bf16[4,128,768]{2,1,0:T(8,128)(2,1)}, f32[4,128,768]{2,1,0:T(8,128)}, f32[24,2304]{1,0:T(8,128)}, f32[24,768]{1,0:T(8,128)}, f32[24,3072]{1,0:T(8,128)}, /*index=5*/f32[96,768]{1,0:T(8,128)}) custom-call(bf16[4,128,768]{2,1,0:T(8,128)(2,1)} %get-tuple-element.28.out, bf16[4,128,768]{2,1,0:T(8,128)(2,1)} %get-tuple-element.29.d_x, ...), custom_call_target="tpu_custom_call" | custom-call | tf_op jit(solution)/shard_map/pallas_call | solution.py:1343
  (1 shorter events, 0.0 us)
